TPU v7x, 32 devices: a whole 2x2x4 slice. The times are simulated.
32 devices in a mesh: sub: 8 (over z, y), sec: 4 (over x, core).
Axes of the slice: x: 2, y: 2, z: 4, core: 2. Of those that a mesh axis runs over, the one named last changes fastest.
Arguments:
- start_vectors: bfloat16 [32, 3, 256, 512], P(None, None, 'sub', 'sec'), may hold values from -6 to 6
- stiffness: bfloat16 [3, 256, 512], P(None, 'sub', 'sec'), may hold values from 1.5 to 15
- coupling: bfloat16 [256, 512], P('sub', 'sec'), may hold values from -0.5 to 0.5
- kept_ranks: int32 [8, 4], P('sub', 'sec'), may hold values from 16 to 32, as said below
- level_start: float32 [256, 16], P('sub'), may hold values from -6 to 6
Outputs:
- prolonged: float32 [16, 3, 256, 512], P(None, None, 'sub', 'sec')
Inputs may be any that keep to these rules, and one draw needn't show every extreme that they name: `kept_ranks`: every subdomain keeps at least half of its 32 vectors; some subdomain keeps all 32 and some keeps exactly half.
All inputs are finite; a program needn't handle non-finite values.
Results may differ from a plain program's by a relative error of at most 0.0003.
Values may be sent and summed in bfloat16 or wider, within the bound.
No kernel may reach another device: no remote copies, remote signals or barrier semaphores. Data moves between devices by JAX's collectives and lax.ppermute only.
A program may use at most 64 MiB of HBM per device.

v0:
```python
import math

import jax
import jax.numpy as jnp
from jax import lax
from jax.sharding import PartitionSpec as P

CX = 32
H = 4
CY = 128
NV = 32
ITERS = 2
LEVEL_ITERS = 2
XEXT = 40
YEXT = 136


highest = lax.Precision.HIGHEST


def with_halo(x, sides, width):
    for axis, dim in sides:
        devices, length = (lax.axis_size(axis), x.shape[dim])
        up = [(i, (i + 1) % devices) for i in range(devices - 1)]
        down = [(j, i) for i, j in up]
        last = lax.slice_in_dim(x, length - width, length, axis=dim)
        leading = lax.slice_in_dim(x, 0, width, axis=dim)
        before = lax.ppermute(last, axis, up)
        after = lax.ppermute(leading, axis, down)
        x = jnp.concatenate([before, x, after], axis=dim)
    return x


def from_behind(block, axis, distance):
    devices = range(lax.axis_size(axis))
    route = [(i - distance, i) for i in devices if i - distance in devices]
    return lax.ppermute(block, axis, route)


def apply_operator(vectors, stiff_diag, shear_term, inside):
    padded = jnp.pad(vectors, ((0, 0), (0, 0), (1, 1), (1, 1)))
    beside = (
        padded[:, :, 2:, 1:-1]
        + padded[:, :, :-2, 1:-1]
        + padded[:, :, 1:-1, 2:]
        + padded[:, :, 1:-1, :-2]
    )
    others = jnp.sum(vectors, axis=1, keepdims=True) - vectors
    return ((4.0 + stiff_diag) * vectors - beside + shear_term * others) * inside


def orthonormal(work):
    shape_before = work.shape
    flat = work.reshape(shape_before[0], -1)
    gram = jnp.dot(flat, flat.T, precision=highest)
    lower = jnp.linalg.cholesky(gram)
    solved = lax.linalg.triangular_solve(lower, flat, left_side=True, lower=True)
    return solved.reshape(shape_before)


def subspace_basis(vectors, stiff_diag, shear_term, inside, rank):
    for iteration in range(ITERS):
        vectors = orthonormal(apply_operator(vectors, stiff_diag, shear_term, inside))
    live = (jnp.arange(NV, dtype=jnp.int32) < rank).astype(jnp.float32)
    basis = vectors * live[:, None, None, None]
    image = apply_operator(basis, stiff_diag, shear_term, inside)
    self_block = jnp.dot(basis.reshape(NV, -1), image.reshape(NV, -1).T, precision=highest)
    return (basis, self_block)


def on_device(start_vectors, stiffness, coupling, kept_ranks, level_start):
    span_count = lax.axis_size("sub")
    sect_count = lax.axis_size("sec")
    stacked = jnp.concatenate(
        [start_vectors.reshape(NV * 3, CX, CY), stiffness, coupling[None]], axis=0
    )
    extended = with_halo(stacked, (("sub", 1), ("sec", 2)), H)
    vectors = extended[: NV * 3].astype(jnp.float32).reshape(NV, 3, XEXT, YEXT)
    stiff_diag = extended[NV * 3 : NV * 3 + 3].astype(jnp.float32)
    shear_term = extended[NV * 3 + 3].astype(jnp.float32)
    row_global = lax.axis_index("sub") * CX - H + lax.iota(jnp.int32, XEXT)
    col_global = lax.axis_index("sec") * CY - H + lax.iota(jnp.int32, YEXT)
    row_inside = (row_global >= 0) & (row_global < span_count * CX)
    col_inside = (col_global >= 0) & (col_global < sect_count * CY)
    inside = (row_inside[:, None] & col_inside[None, :]).astype(jnp.float32)
    basis, self_block = subspace_basis(vectors, stiff_diag, shear_term, inside, kept_ranks[0, 0])
    lower_next = from_behind(basis[:, :, : 2 * H, :], "sub", -1)
    upper_rim = (4.0 + stiff_diag[:, CX:, :]) * basis[:, :, CX:, :]
    couple_block = jnp.einsum("acxy,bcxy->ab", upper_rim, lower_next, precision=highest)
    own_rows = level_start
    couple_prev = from_behind(couple_block, "sub", 1)
    for iteration in range(LEVEL_ITERS):
        rows_next = from_behind(own_rows, "sub", -1)
        image = jnp.dot(self_block, own_rows, precision=highest)
        image = image + jnp.dot(couple_block, rows_next, precision=highest)
        rows_prev = from_behind(own_rows, "sub", 1)
        image = image + jnp.dot(couple_prev.T, rows_prev, precision=highest)
        gram = lax.psum(jnp.dot(image.T, image, precision=highest), "sub")
        lower = jnp.linalg.cholesky(gram)
        own_rows = lax.linalg.triangular_solve(lower, image.T, left_side=True, lower=True).T
    factor = math.sqrt(span_count * 3 * XEXT * YEXT)
    owned = basis[:, :, H : H + CX, H : H + CY]
    return factor * jnp.einsum("ak,acxy->kcxy", own_rows, owned, precision=highest)


def solution(mesh):
    placed = (
        P(None, None, "sub", "sec"),
        P(None, "sub", "sec"),
        P("sub", "sec"),
        P("sub", "sec"),
        P("sub", None),
    )
    return jax.shard_map(
        on_device,
        mesh=mesh,
        in_specs=placed,
        out_specs=P(None, None, "sub", "sec"),
        check_vma=False,
    )
```

profile of v0, /device:TPU:0, one launch (start us, length us, event | category | flops | bytes accessed | tf_op | source)
XLA Modules:
  0.0 206.5 jit_solution(7046180540235981564)
XLA Ops:
  0.0 4.9 %collective-permute-start.7 = (f32[32,16]{0,1:T(8,128)}, f32[32,16]{0,1:T(8,128)S(1)}, u32[]{:S(2)}, u32[]{:S(2)}) collective-permute-start(f32[32,16]{0,1:T(8,128)} %param.15), channel_id=1, source_target_pairs={{0,4},{4,8},{8,12},{12,16},{16,20},{20,24},{24,28},{1,5},{5,9},{9,... | collective-permute-start | bytes 6152 | tf_op jit(solution)/shard_map/ppermute | solution.py:37
  7.4 4.6 %collective-permute-start = (bf16[100,4,128]{2,1,0:T(4,128)(2,1)S(1)}, bf16[100,4,128]{2,1,0:T(4,128)(2,1)S(1)}, u32[]{:S(2)}, u32[]{:S(2)}) collective-permute-start(bf16[100,4,128]{2,1,0:T(4,128)(2,1)S(1)} %get-tuple-element.15), channel_id=1, source_target_pairs={{0,4},{4,8},{8,12},{12,16},{16,20},{20,24},{24,28},{1,5},{5,9},{9,... | collective-permute-start | bytes 307208 | tf_op jit(solution)/shard_map/ppermute | solution.py:28
  14.2 4.7 %collective-permute-done.1 = bf16[100,4,128]{2,1,0:T(4,128)(2,1)S(1)} collective-permute-done((bf16[100,4,128]{2,1,0:T(4,128)(2,1)S(1)}, bf16[100,4,128]{2,1,0:T(4,128)(2,1)S(1)}, u32[]{:S(2)}, u32[]{:S(2)}) %collective-permute-start.1) | collective-permute-done | bytes 102432 | tf_op jit(solution)/shard_map/ppermute | solution.py:29
  28.9 4.7 %pad_maximum_fusion = bf16[100,40,136]{2,1,0:T(8,128)(2,1)S(1)} fusion(bf16[100,40,4]{2,1,0:T(8,128)(2,1)S(1)} %copy.36, bf16[100,4,128]{2,1,0:T(4,128)(2,1)S(1)} %collective-permute-done.1, bf16[1,32,128]{2,1,0:T(8,128)(2,1)S(1)} %bitcast.112, bf16[3,32,128]{2,1,0:T(8,128)(2,1)S(1)} %copy-done.2, bf16[96,32,128]{2,1,0:T(8,128)(2,1)S(1)} %bitcast.105, ...), kind=kLoop, calls=%fused_computation.24 | loop fusion | flops 7616000 | bytes 2176000 | tf_op jit(solution)/shard_map/concatenate | solution.py:30
  38.3 3.2 %convolution_bitcast_fusion.2 = f32[32,32]{1,0:T(8,128)S(1)} fusion(f32[32,3,40,136]{3,0,2,1:T(8,128)S(1)} %add_multiply_fusion.1), kind=kOutput, calls=%fused_computation.35 | convolution fusion | flops 200540160 | bytes 2093056 | tf_op jit(solution)/shard_map/dot_general | solution.py:55
  41.5 4.2 %copy.42 = f32[32,3,40,136]{3,2,1,0:T(8,128)} copy(f32[32,3,40,136]{3,0,2,1:T(8,128)S(1)} %add_multiply_fusion.1) | data formatting | bytes 4177920 | tf_op jit(solution)/shard_map/mul | solution.py:49
  45.6 3.3 %reshape.107 = f32[32,16320]{1,0:T(8,128)S(1)} reshape(f32[32,3,40,136]{3,2,1,0:T(8,128)} %copy.42) | data formatting | bytes 4177920 | tf_op jit(solution)/shard_map/reshape | solution.py:54
  55.7 3.3 %fusion.35 = f32[32,16320]{1,0:T(8,128)} fusion(f32[32,16320]{1,0:T(8,128)S(1)} %reshape.107, f32[1,32,32]{1,2,0:T(8,128)S(1)} %custom-call.12), kind=kOutput, calls=%fused_computation.62 | convolution fusion | flops 200540160 | bytes 4182016 | tf_op jit(solution)/shard_map/triangular_solve/dot.1 | solution.py:57
  59.0 5.0 %reshape.108 = f32[32,3,40,136]{3,2,1,0:T(8,128)} reshape(f32[32,16320]{1,0:T(8,128)} %fusion.35) | data formatting | bytes 4177920 | tf_op jit(solution)/shard_map/reshape | solution.py:58
  64.0 5.2 %copy.43 = f32[32,3,40,136]{3,0,2,1:T(8,128)} copy(f32[32,3,40,136]{3,2,1,0:T(8,128)} %reshape.108) | data formatting | bytes 4177920 | tf_op jit(solution)/shard_map/reshape | solution.py:58
  72.2 9.2 %add_multiply_fusion = f32[32,3,40,136]{3,0,2,1:T(8,128)S(1)} fusion(f32[32,3,40,136]{3,0,2,1:T(8,128)} %copy.43, f32[32,40,136]{2,0,1:T(8,128)S(1)} %copy.45, f32[40,136]{1,0:T(8,128)S(1)} %and_convert_fusion, f32[40,136]{1,0:T(8,128)S(1)} %fusion.29, f32[3,40,136]{2,1,0:T(8,128)S(1)} %get-tuple-element.10), kind=kLoop, calls=%fused_computation.16 | loop fusion | flops 4700160 | bytes 4983040 | tf_op jit(solution)/shard_map/mul | solution.py:49
  81.5 3.2 %convolution_bitcast_fusion.1 = f32[32,32]{1,0:T(8,128)S(1)} fusion(f32[32,3,40,136]{3,0,2,1:T(8,128)S(1)} %add_multiply_fusion), kind=kOutput, calls=%fused_computation.34 | convolution fusion | flops 200540160 | bytes 2093056 | tf_op jit(solution)/shard_map/dot_general | solution.py:55
  84.7 4.2 %copy.48 = f32[32,3,40,136]{3,2,1,0:T(8,128)} copy(f32[32,3,40,136]{3,0,2,1:T(8,128)S(1)} %add_multiply_fusion) | data formatting | bytes 4177920 | tf_op jit(solution)/shard_map/mul | solution.py:49
  88.8 3.1 %reshape.109 = f32[32,16320]{1,0:T(8,128)S(1)} reshape(f32[32,3,40,136]{3,2,1,0:T(8,128)} %copy.48) | data formatting | bytes 4177920 | tf_op jit(solution)/shard_map/reshape | solution.py:54
  98.7 3.3 %fusion.32 = f32[32,16320]{1,0:T(8,128)} fusion(f32[32,16320]{1,0:T(8,128)S(1)} %reshape.109, f32[1,32,32]{1,2,0:T(8,128)S(1)} %custom-call.13), kind=kOutput, calls=%fused_computation.58 | convolution fusion | flops 200540160 | bytes 4182016 | tf_op jit(solution)/shard_map/triangular_solve/dot.1 | solution.py:57
  102.0 5.2 %reshape.110 = f32[32,3,40,136]{3,2,1,0:T(8,128)} reshape(f32[32,16320]{1,0:T(8,128)} %fusion.32) | data formatting | bytes 4177920 | tf_op jit(solution)/shard_map/reshape | solution.py:58
  107.2 3.9 %fusion.52 = (f32[32,40,136]{2,0,1:T(8,128)S(1)}, f32[32,3,40,136]{3,0,2,1:T(8,128)S(1)}) fusion(f32[32]{0:T(128)S(1)} %compare_convert_fusion, f32[32,3,40,136]{3,2,1,0:T(8,128)} %reshape.110), kind=kLoop, calls=%fused_computation.97 | loop fusion | flops 870400 | bytes 4874368 | tf_op jit(solution)/shard_map/reduce_sum | solution.py:48
  111.2 5.0 %fusion.25 = f32[32,32]{1,0:T(8,128)S(1)} fusion(f32[32,3,40,136]{3,0,2,1:T(8,128)S(1)} %get-tuple-element.8, f32[32,40,136]{2,0,1:T(8,128)S(1)} %get-tuple-element.6, f32[40,136]{1,0:T(8,128)S(1)} %and_convert_fusion, f32[40,136]{1,0:T(8,128)S(1)} %fusion.29, f32[3,40,136]{2,1,0:T(8,128)S(1)} %get-tuple-element.10), kind=kOutput, calls=%fused_computation.33 | convolution fusion | flops 205240320 | bytes 9383936 | tf_op jit(solution)/shard_map/dot_general | solution.py:67
  117.6 21.1 %collective-permute-done.4 = f32[32,3,8,136]{3,0,2,1:T(8,128)S(1)} collective-permute-done((f32[32,3,8,136]{3,0,2,1:T(8,128)S(1)}, f32[32,3,8,136]{3,0,2,1:T(8,128)S(1)}, u32[]{:S(2)}, u32[]{:S(2)}) %collective-permute-start.4) | collective-permute-done | bytes 417824 | tf_op jit(solution)/shard_map/ppermute | solution.py:37
  139.5 5.1 %collective-permute-start.6 = (f32[32,32]{1,0:T(8,128)S(1)}, f32[32,32]{1,0:T(8,128)S(1)}, u32[]{:S(2)}, u32[]{:S(2)}) collective-permute-start(f32[32,32]{1,0:T(8,128)S(1)} %convolution_bitcast_fusion), channel_id=1, source_target_pairs={{0,4},{4,8},{8,12},{12,16},{16,20},{20,24},{24,28},{1,5},{5,9},{9,... | collective-permute-start | bytes 12296 | tf_op jit(solution)/shard_map/ppermute | solution.py:37
  146.3 20.0 %psum.14 = f32[16,16]{0,1:T(8,128)S(1)} all-reduce(f32[16,16]{0,1:T(8,128)S(1)} %fusion.55), channel_id=1, replica_groups=mesh['sub'=8,'sec'=4] {'sub'}, use_global_device_ids=true, to_apply=%region_5.8 | all-reduce | flops 256 | bytes 2048 | tf_op jit(solution)/shard_map/psum | solution.py:98
  172.0 4.6 %collective-permute-start.9 = (f32[32,16]{0,1:T(8,128)S(1)}, f32[32,16]{0,1:T(8,128)S(1)}, u32[]{:S(2)}, u32[]{:S(2)}) collective-permute-start(f32[32,16]{0,1:T(8,128)S(1)} %bitcast.116), channel_id=1, source_target_pairs={{0,4},{4,8},{8,12},{12,16},{16,20},{20,24},{24,28},{1,5},{5,9},{9,... | collective-permute-start | bytes 6152 | tf_op jit(solution)/shard_map/ppermute | solution.py:37
  178.2 19.7 %psum.15 = f32[16,16]{0,1:T(8,128)S(1)} all-reduce(f32[16,16]{0,1:T(8,128)S(1)} %fusion.57), channel_id=1, replica_groups=mesh['sub'=8,'sec'=4] {'sub'}, use_global_device_ids=true, to_apply=%region_8.13 | all-reduce | flops 256 | bytes 2048 | tf_op jit(solution)/shard_map/psum | solution.py:98
  202.2 3.0 %fusion.22 = f32[16,3,32,128]{3,0,2,1:T(8,128)S(1)} fusion(f32[16,32,1,1]{1,0,3,2:T(8,128)S(1)} %convolution_bitcast_fusion.3, f32[32,3,40,136]{3,0,2,1:T(8,128)} %copy-done.1), kind=kOutput, calls=%fused_computation.31 | convolution fusion | flops 75694080 | bytes 2361344 | tf_op jit(solution)/shard_map/ak,acxy->kcxy/dot_general | solution.py:103
  (86 shorter events, 51.8 us)
Async XLA Ops:
  0.0 144.8 %collective-permute-start.7 = (f32[32,16]{0,1:T(8,128)}, f32[32,16]{0,1:T(8,128)S(1)}, u32[]{:S(2)}, u32[]{:S(2)}) collective-permute-start(f32[32,16]{0,1:T(8,128)} %param.15), channel_id=1, source_target_pairs={{0,4},{4,8},{8,12},{12,16},{16,20},{20,24},{24,28},{1,5},{5,9},{9,... | collective-permute-start | bytes 6152 | tf_op jit(solution)/shard_map/ppermute | solution.py:37
  4.9 139.7 %collective-permute-start.5 = (f32[32,16]{0,1:T(8,128)}, f32[32,16]{0,1:T(8,128)S(1)}, u32[]{:S(2)}, u32[]{:S(2)}) collective-permute-start(f32[32,16]{0,1:T(8,128)} %param.15), channel_id=1, source_target_pairs={{4,0},{8,4},{12,8},{16,12},{20,16},{24,20},{28,24},{5,1},{9,5},{13... | collective-permute-start | bytes 6152 | tf_op jit(solution)/shard_map/ppermute | solution.py:37
  7.4 6.8 %collective-permute-start = (bf16[100,4,128]{2,1,0:T(4,128)(2,1)S(1)}, bf16[100,4,128]{2,1,0:T(4,128)(2,1)S(1)}, u32[]{:S(2)}, u32[]{:S(2)}) collective-permute-start(bf16[100,4,128]{2,1,0:T(4,128)(2,1)S(1)} %get-tuple-element.15), channel_id=1, source_target_pairs={{0,4},{4,8},{8,12},{12,16},{16,20},{20,24},{24,28},{1,5},{5,9},{9,... | collective-permute-start | bytes 307208 | tf_op jit(solution)/shard_map/ppermute | solution.py:28
  11.9 7.0 %collective-permute-start.1 = (bf16[100,4,128]{2,1,0:T(4,128)(2,1)S(1)}, bf16[100,4,128]{2,1,0:T(4,128)(2,1)S(1)}, u32[]{:S(2)}, u32[]{:S(2)}) collective-permute-start(bf16[100,4,128]{2,1,0:T(4,128)(2,1)S(1)} %get-tuple-element.16), channel_id=1, source_target_pairs={{4,0},{8,4},{12,8},{16,12},{20,16},{24,20},{28,24},{5,1},{9,5},{13... | collective-permute-start | bytes 307208 | tf_op jit(solution)/shard_map/ppermute | solution.py:29
  20.6 8.2 %copy-start = (bf16[32,3,32,128]{3,2,1,0:T(8,128)(2,1)S(1)}, bf16[32,3,32,128]{3,2,1,0:T(8,128)(2,1)}, u32[]{:S(2)}) copy-start(bf16[32,3,32,128]{3,2,1,0:T(8,128)(2,1)} %param.11) | copy-start | bytes 2359300
  20.6 8.2 %copy-start.2 = (bf16[3,32,128]{2,1,0:T(8,128)(2,1)S(1)}, bf16[3,32,128]{2,1,0:T(8,128)(2,1)}, u32[]{:S(2)}) copy-start(bf16[3,32,128]{2,1,0:T(8,128)(2,1)} %param.12) | copy-start | bytes 73732
  20.6 8.2 %copy-start.3 = (bf16[32,128]{1,0:T(8,128)(2,1)S(1)}, bf16[32,128]{1,0:T(8,128)(2,1)}, u32[]{:S(2)}) copy-start(bf16[32,128]{1,0:T(8,128)(2,1)} %param.13) | copy-start | bytes 24580
  22.4 5.8 %collective-permute-start.3 = (bf16[100,40,4]{0,1,2:T(8,128)(2,1)S(1)}, bf16[100,40,4]{0,1,2:T(8,128)(2,1)S(1)}, u32[]{:S(2)}, u32[]{:S(2)}) collective-permute-start(bf16[100,40,4]{0,1,2:T(8,128)(2,1)S(1)} %copy.34), channel_id=1, source_target_pairs={{1,0},{2,1},{3,2},{5,4},{6,5},{7,6},{9,8},{10,9},{11,10},{13,12},{... | collective-permute-start | bytes 96008 | tf_op jit(solution)/shard_map/ppermute | solution.py:29
  23.7 3.9 %collective-permute-start.2 = (bf16[100,40,4]{0,1,2:T(8,128)(2,1)S(1)}, bf16[100,40,4]{0,1,2:T(8,128)(2,1)S(1)}, u32[]{:S(2)}, u32[]{:S(2)}) collective-permute-start(bf16[100,40,4]{0,1,2:T(8,128)(2,1)S(1)} %copy.33), channel_id=1, source_target_pairs={{0,1},{1,2},{2,3},{4,5},{5,6},{6,7},{8,9},{9,10},{10,11},{12,13},{... | collective-permute-start | bytes 96008 | tf_op jit(solution)/shard_map/ppermute | solution.py:28
  111.1 27.6 %copy-start.1 = (f32[32,3,40,136]{3,0,2,1:T(8,128)}, f32[32,3,40,136]{3,0,2,1:T(8,128)S(1)}, u32[]{:S(2)}) copy-start(f32[32,3,40,136]{3,0,2,1:T(8,128)S(1)} %get-tuple-element.8) | copy-start | bytes 6266884
  111.1 6.3 %copy-start.4 = (f32[32,16]{0,1:T(8,128)S(1)}, f32[32,16]{0,1:T(8,128)}, u32[]{:S(2)}) copy-start(f32[32,16]{0,1:T(8,128)} %param.15) | copy-start | bytes 6148
  116.1 22.6 %collective-permute-start.4 = (f32[32,3,8,136]{3,0,2,1:T(8,128)S(1)}, f32[32,3,8,136]{3,0,2,1:T(8,128)S(1)}, u32[]{:S(2)}, u32[]{:S(2)}) collective-permute-start(f32[32,3,8,136]{3,0,2,1:T(8,128)S(1)} %slice.109), channel_id=1, source_target_pairs={{4,0},{8,4},{12,8},{16,12},{20,16},{24,20},{28,24},{5,1},{9,5},{13... | collective-permute-start | bytes 1253384 | tf_op jit(solution)/shard_map/ppermute | solution.py:37
  139.5 6.5 %collective-permute-start.6 = (f32[32,32]{1,0:T(8,128)S(1)}, f32[32,32]{1,0:T(8,128)S(1)}, u32[]{:S(2)}, u32[]{:S(2)}) collective-permute-start(f32[32,32]{1,0:T(8,128)S(1)} %convolution_bitcast_fusion), channel_id=1, source_target_pairs={{0,4},{4,8},{8,12},{12,16},{16,20},{20,24},{24,28},{1,5},{5,9},{9,... | collective-permute-start | bytes 12296 | tf_op jit(solution)/shard_map/ppermute | solution.py:37
  170.6 6.0 %collective-permute-start.8 = (f32[32,16]{0,1:T(8,128)S(1)}, f32[32,16]{0,1:T(8,128)S(1)}, u32[]{:S(2)}, u32[]{:S(2)}) collective-permute-start(f32[32,16]{0,1:T(8,128)S(1)} %bitcast.115), channel_id=1, source_target_pairs={{4,0},{8,4},{12,8},{16,12},{20,16},{24,20},{28,24},{5,1},{9,5},{13... | collective-permute-start | bytes 6152 | tf_op jit(solution)/shard_map/ppermute | solution.py:37
  172.0 5.9 %collective-permute-start.9 = (f32[32,16]{0,1:T(8,128)S(1)}, f32[32,16]{0,1:T(8,128)S(1)}, u32[]{:S(2)}, u32[]{:S(2)}) collective-permute-start(f32[32,16]{0,1:T(8,128)S(1)} %bitcast.116), channel_id=1, source_target_pairs={{0,4},{4,8},{8,12},{12,16},{16,20},{20,24},{24,28},{1,5},{5,9},{9,... | collective-permute-start | bytes 6152 | tf_op jit(solution)/shard_map/ppermute | solution.py:37
where the time goes:
time: 211 us; the launch traced here: 207 us
  other arithmetic  48.4 us (23%)
  blocking collectives  39.6 us (19%)
  local copies, waits for them, and re-layouts  36.2 us (17%)
  waiting for transfers between devices  29.3 us (14%)
  starting transfers between devices  28.6 us (14%)
  matrix products  23.2 us (11%)
    psum x2, blocking collectives, on_device(): gram = lax.psum(jnp.dot(image.T, image, precision=highest), 'sub')  39.6 us
    ppermute x6, waiting for transfers between devices, from_behind(): return lax.ppermute(block, axis, route)  23.6 us
    ppermute x6, starting transfers between devices, from_behind(): return lax.ppermute(block, axis, route)  18.4 us
    reshape x3, local copies, waits for them, and re-layouts, orthonormal(): return solved.reshape(shape_before)  15.4 us
    mul x2, other arithmetic, apply_operator(): ((4.0 + stiff_diag) * vectors - beside + shear_term * others) * inside  12.2 us
    mul x2, local copies, waits for them, and re-layouts, apply_operator(): ((4.0 + stiff_diag) * vectors - beside + shear_term * others) * inside  8.31 us
    ppermute x2, starting transfers between devices, with_halo(): before = lax.ppermute(last, axis, up)  7.59 us
    another operation x6, other arithmetic, orthonormal(): lower = jnp.linalg.cholesky(gram)  7.19 us
  transfers between devices with their start and end apart: 10, of which 6 were waited for; matrix products, arithmetic and copies ran while one was open for 46% of the time, Pallas kernels for 0%

commit v1 on v0

v1 whole, which is shorter than its diff:
```python
import math

import jax
import jax.numpy as jnp
from jax import lax
from jax.experimental import pallas as pl
from jax.experimental.pallas import tpu as pltpu
from jax.sharding import PartitionSpec as P

H = 4
REACH = H + 2
MIB = 1 << 20
F32 = jnp.float32
BF16 = jnp.bfloat16
NN = (((1,), (0,)), ((), ()))
NT = (((1,), (1,)), ((), ()))
TN = (((0,), (0,)), ((), ()))


def iota(shape, dim):
    return lax.broadcasted_iota(jnp.int32, shape, dim)


def split(x):
    high = x.astype(BF16)
    return high, (x - high.astype(F32)).astype(BF16)


def dot(a, b, dims):
    return lax.dot_general(a, b, dims, preferred_element_type=F32)


def dot3(a, b, dims):
    (ah, al), (bh, bl) = split(a), split(b)
    return dot(ah, bh, dims) + (dot(ah, bl, dims) + dot(al, bh, dims))


def inverse_factor(gram, size):
    row, lane = iota((size, 128), 0), iota((size, 128), 1)
    work = jnp.where(lane < size, gram, jnp.where(lane == row + size, 1.0, 0.0))
    for j in range(size - 1):
        column = work[:, j : j + 1]
        pivot = work[j : j + 1, :]
        factor = jnp.where(iota((size, 1), 0) > j, column / column[j : j + 1, :], 0.0)
        work = work - factor * pivot
    diag = jnp.sum(jnp.where(lane == row, work, 0.0), axis=1, keepdims=True)
    return pltpu.roll(work / jnp.sqrt(diag), 128 - size, 1)


def pack_kernel(v_ref, k_ref, g_ref, own_ref, sec_ref, sub_ref, vf, kf):
    nv, comps, cx, cy = v_ref.shape
    sub_even = lax.rem(lax.axis_index("sub"), 2) == 0
    sec_even = lax.rem(lax.axis_index("sec"), 2) == 0
    vf[...] = v_ref[...].astype(F32).reshape(vf.shape)
    kf[...] = jnp.zeros(kf.shape, F32)
    kf[: comps * cx] = k_ref[...].astype(F32).reshape(comps * cx, cy)
    kf[comps * cx : (comps + 1) * cx] = g_ref[...].astype(F32)
    group = iota((nv, cy), 1) // H
    for c in range(comps + 1):
        left = jnp.zeros((nv, cy), F32)
        right = jnp.zeros((nv, cy), F32)
        for x in range(cx):
            if c < comps:
                tile = vf[pl.ds(c * cx + x, nv, stride=comps * cx), :]
            else:
                tile = jnp.concatenate([kf[pl.ds(x, 8, stride=cx), :], jnp.zeros((nv - 8, cy), F32)], axis=0)
            own_ref[x, c] = tile.astype(BF16)
            rolled = pltpu.roll(tile, H * x, 1) if x else tile
            left = jnp.where(group == x, rolled, left)
            right = jnp.where(group == (x + cx - 1) % cx, rolled, right)
        sec_ref[0, c] = jnp.where(sec_even, right, left).astype(BF16)
        sec_ref[1, c] = jnp.where(sec_even, left, right).astype(BF16)
    last = cx - REACH
    sub_ref[0] = own_ref[pl.ds(jnp.where(sub_even, last, 0), REACH)]
    sub_ref[1] = own_ref[pl.ds(jnp.where(sub_even, 0, last), REACH)]


def fine_kernel(sizes, rank_ref, start_ref, own_ref, sec_a, sec_b, sub_a, sub_b, pack_ref, basis_ref, v0, x1, x2, s1, coef, acc, facc):
    spans, sects = sizes
    cx, channels, nv, cy = own_ref.shape
    comps = channels - 1
    wide = 2 * cy
    s, t = lax.axis_index("sub"), lax.axis_index("sec")
    sub_even, sec_even = lax.rem(s, 2) == 0, lax.rem(t, 2) == 0
    lane = iota((nv, cy), 1)
    group = lane // H
    first, last = lane < H, lane >= cy - H

    def tail(hi, lo, x):
        rolled = jnp.where(group == x, hi, lo)
        rolled = pltpu.roll(rolled, cy - H * x, 1) if x else rolled
        return jnp.where(first | last, rolled, 0.0)

    sublane = iota((8, wide), 0)
    wide_lane = iota((1, wide), 1)
    col_in = (wide_lane < cy) | ((wide_lane < cy + H) & (t < sects - 1)) | ((wide_lane >= wide - H) & (t > 0))

    def put(x, c, main, side):
        both = jnp.concatenate([main, side], axis=1)
        if c < comps:
            v0[x + H, c] = both
        else:
            both = both[:8]
            row_in = True if 0 <= x < cx else (s > 0 if x < 0 else s < spans - 1)
            inside = jnp.where(col_in & row_in, 1.0, 0.0)
            g = both[comps : comps + 1]
            terms = jnp.where(sublane < comps, 4.0 + both - g, jnp.where(sublane == comps, both, 1.0))
            coef[x + H] = terms * inside

    def halves(ref_a, ref_b, even, index):
        a, b = ref_a[index].astype(F32), ref_b[index].astype(F32)
        return jnp.where(even, a, b), jnp.where(even, b, a)

    for c in range(channels):
        hi, lo = halves(sec_a, sec_b, sec_even, c)
        for x in range(cx):
            put(x, c, own_ref[x, c].astype(F32), tail(hi, lo, x))
        after_hi, before_hi = halves(sub_a, sub_b, sub_even, (REACH, c))
        after_lo, before_lo = halves(sub_a, sub_b, sub_even, (REACH + 1, c))
        after_hi, after_lo = jnp.where(sec_even, after_hi, after_lo), jnp.where(sec_even, after_lo, after_hi)
        before_hi, before_lo = jnp.where(sec_even, before_hi, before_lo), jnp.where(sec_even, before_lo, before_hi)
        for i in range(REACH):
            after, before = halves(sub_a, sub_b, sub_even, (i, c))
            put(cx + i, c, after, tail(after_hi, after_lo, i))
            if i >= REACH - H:
                x = i - REACH
                put(x, c, before, tail(before_hi, before_lo, cx + x))

    def operator_row(src, i, k, emit, up=True, down=True):
        diag = [jnp.broadcast_to(coef[k, c : c + 1, :], (8, wide)) for c in range(comps)]
        shear = jnp.broadcast_to(coef[k, comps : comps + 1, :], (8, wide))
        mask = jnp.broadcast_to(coef[k, comps + 1 : comps + 2, :], (8, wide))
        for o in range(nv // 8):
            rows = slice(8 * o, 8 * o + 8)
            v = [src[i, c, rows, :] for c in range(comps)]
            total = shear * (v[0] + v[1] + v[2])
            for c in range(comps):
                beside = pltpu.roll(v[c], 1, 1) + pltpu.roll(v[c], wide - 1, 1)
                if up:
                    beside = beside + src[i - 1, c, rows, :]
                if down:
                    beside = beside + src[i + 1, c, rows, :]
                emit(c, rows, diag[c] * v[c] + total - mask * beside)

    def operator(src, dst, count, coef_row, tail_down=False):
        def body(i, carry, up=True, down=True):
            def emit(c, rows, value):
                dst[i, c, rows, :] = value
            operator_row(src, i, i + coef_row, emit, up, down)
            return carry
        body(0, 0, up=False)
        lax.fori_loop(1, count if tail_down else count - 1, body, 0)
        if not tail_down:
            body(count - 1, 0, down=False)

    rows_ext = cx + 2 * H
    operator(v0, x1, rows_ext, 0)
    operator(x1, x2, rows_ext, 0)

    acc[...] = jnp.zeros(acc.shape, F32)

    def gram_row(i, carry, up=True, down=True):
        images = {}
        def emit(c, rows, value):
            images.setdefault(c, []).append(value)
        operator_row(x2, i, i, emit, up, down)
        total = carry
        for c in range(comps):
            h2, l2 = split(x2[i, c])
            h3, l3 = split(jnp.concatenate(images[c], axis=0))
            two = jnp.concatenate([h2, l2], axis=0)
            four = jnp.concatenate([two, h3, l3], axis=0)
            total = total + dot(two, four, NT)
        return total
    total = gram_row(0, jnp.zeros((2 * nv, 4 * nv), F32), up=False)
    total = lax.fori_loop(1, rows_ext - 1, gram_row, total)
    total = gram_row(rows_ext - 1, total, down=False)
    total = total[:nv] + total[nv:]
    total = total + pltpu.roll(total, 4 * nv - nv, 1)
    gram = total

    base = cx
    operator(v0.at[pl.ds(base, 2 * H + 2)], s1, 2 * H + 1, base, tail_down=True)

    def rim_row(i, carry, up=True):
        images = {}
        def emit(c, rows, value):
            images.setdefault(c, []).append(value)
        operator_row(s1, i, i + base, emit, up, True)
        total = carry
        for c in range(comps):
            stiff = jnp.broadcast_to(coef[i + base, c : c + 1, :] + coef[i + base, comps : comps + 1, :], (nv, wide))
            a = jnp.concatenate(split(x2[i + base, c] * stiff), axis=0)
            b = jnp.concatenate(split(jnp.concatenate(images[c], axis=0)), axis=0)
            total = total + dot(a, b, NT)
        return total
    rim = rim_row(0, jnp.zeros((2 * nv, 2 * nv), F32), up=False)
    rim = lax.fori_loop(1, 2 * H, rim_row, rim)
    rim = rim[:nv] + rim[nv:]
    rim = rim[:, :nv] + rim[:, nv:]
    rim = jnp.where(s < spans - 1, rim, 0.0)

    inverse = inverse_factor(gram, nv)[:, :nv]
    inverse = jnp.where(iota((nv, nv), 0) < rank_ref[0, 0], inverse, 0.0)
    start = start_ref[...]
    pad = jnp.zeros((nv, 4 * nv - 3 * nv - start.shape[1]), F32)
    pack_ref[0] = jnp.concatenate([gram[:, 2 * nv : 3 * nv], rim, inverse, start, pad], axis=1)
    basis_ref[...] = x2[H : H + cx, :, :, :cy]


def prolong(coefs, basis_ref, out_ref):
    k2, comps, cx, cy = out_ref.shape
    nv = basis_ref.shape[2]
    tiled = jnp.concatenate([coefs] * 8, axis=1)
    tiled = jnp.broadcast_to(tiled[:, None, :], (k2, 8, 8 * nv)).reshape(8 * k2, 8 * nv)
    same = lax.rem(iota(tiled.shape, 0), 8) == iota(tiled.shape, 1) // nv
    high, low = split(jnp.where(same, tiled, 0.0))
    for c in range(comps):
        for o in range(cx // 8):
            block = basis_ref[8 * o : 8 * o + 8, c].reshape(8 * nv, cy)
            bh, bl = split(block)
            out = dot(high, bh, NN) + (dot(low, bh, NN) + dot(high, bl, NN))
            out_ref[:, c, 8 * o : 8 * o + 8, :] = out.reshape(k2, 8, cy)


def level_kernel(spans, factor, p0, p1, p2, p3, basis_ref, out_ref, packs, z_ref):
    k2 = out_ref.shape[0]
    nv = basis_ref.shape[2]
    n = spans * nv
    s = lax.axis_index("sub")
    base = 0
    for part in (p0, p1, p2, p3):
        if base < spans:
            packs[base : base + part.shape[0]] = part[...]
            base += part.shape[0]
    lane = iota((nv, n), 1)
    upper, diagonal, starts = [], [], []
    for b in range(spans):
        block = packs[jnp.bitwise_xor(s, b)]
        zeros = jnp.zeros((nv, n - 4 * nv), F32)
        placed = jnp.concatenate([block, zeros], axis=1)
        pair = jnp.where(lane < nv, 0.5 * placed, jnp.where(lane < 2 * nv, placed, 0.0))
        upper.append(pltpu.roll(pair, nv * b, 1) if b else pair)
        inv = jnp.where((lane >= 2 * nv) & (lane < 3 * nv), placed, 0.0)
        diagonal.append(pltpu.roll(inv, (nv * (b - 2)) % n, 1) if b != 2 else inv)
        starts.append(block[:, 3 * nv : 3 * nv + k2])
    q = jnp.concatenate(upper, axis=0)
    inv = jnp.concatenate(diagonal, axis=0)
    y = jnp.concatenate(starts, axis=0)
    full = q + q.T
    u = dot3(y, inv, TN)
    z = dot3(dot3(u, full, NN), inv, NT)
    u = dot3(z, inv, NN)
    z = dot3(dot3(u, full, NN), inv, NT)
    gram = dot3(z, z, NT)
    gram = jnp.concatenate([gram, jnp.zeros((k2, 128 - k2), F32)], axis=1)
    solve = inverse_factor(gram, k2)[:, :k2]
    y = dot3(solve, z, NN)
    coefs = dot3(y, inv, NN)
    own = jnp.zeros((k2, nv), F32)
    for b in range(spans):
        own = jnp.where(s == b, coefs[:, nv * b : nv * b + nv], own)
    prolong(factor * own, basis_ref, out_ref)


def prolong_kernel(coefs_ref, basis_ref, out_ref):
    prolong(coefs_ref[...], basis_ref, out_ref)


def pairs(count, offset):
    return [q for i in range(offset, count - 1, 2) for q in ((i, i + 1), (i + 1, i))]


def from_behind(block, axis, distance):
    devices = range(lax.axis_size(axis))
    return lax.ppermute(block, axis, [(i - distance, i) for i in devices if i - distance in devices])


def level_coefs(pack, k2, factor):
    highest = lax.Precision.HIGHEST
    nv = pack.shape[0]
    own, rim, inv = pack[:, :nv], pack[:, nv : 2 * nv], pack[:, 2 * nv : 3 * nv]
    z = pack[:, 3 * nv : 3 * nv + k2]
    rim_prev = from_behind(rim, "sub", 1)
    for step in range(2):
        u = jnp.dot(inv.T, z, precision=highest)
        image = jnp.dot(own, u, precision=highest)
        image = image + jnp.dot(rim, from_behind(u, "sub", -1), precision=highest)
        image = image + jnp.dot(rim_prev.T, from_behind(u, "sub", 1), precision=highest)
        z = jnp.dot(inv, image, precision=highest)
    lower = jnp.linalg.cholesky(lax.psum(jnp.dot(z.T, z, precision=highest), "sub"))
    y = lax.linalg.triangular_solve(lower, z.T, left_side=True, lower=True)
    return factor * jnp.dot(y, inv, precision=highest)


def call(kernel, out_shape, scratch, name, in_specs=None):
    return pl.pallas_call(
        kernel,
        out_shape=out_shape,
        scratch_shapes=scratch,
        compiler_params=pltpu.CompilerParams(vmem_limit_bytes=48 * MIB),
        name=name,
        **({"in_specs": in_specs} if in_specs else {}),
    )


def on_device(start_vectors, stiffness, coupling, kept_ranks, level_start):
    spans, sects = lax.axis_size("sub"), lax.axis_size("sec")
    nv, comps, cx, cy = start_vectors.shape
    k2 = level_start.shape[1]
    channels = comps + 1
    xext, yext, wide = cx + 2 * H, cy + 2 * H, 2 * cy
    shape = jax.ShapeDtypeStruct
    vmem = pl.BlockSpec(memory_space=pltpu.VMEM)
    smem = pl.BlockSpec(memory_space=pltpu.SMEM)

    own, sec_out, sub_out = call(
        pack_kernel,
        (
            shape((cx, channels, nv, cy), BF16),
            shape((2, channels, nv, cy), BF16),
            shape((2, REACH, channels, nv, cy), BF16),
        ),
        [pltpu.VMEM((nv * comps * cx, cy), F32), pltpu.VMEM((8 * cx, cy), F32)],
        "pack",
    )(start_vectors, stiffness, coupling)
    sec_a = lax.ppermute(sec_out[0], "sec", pairs(sects, 0))
    sec_b = lax.ppermute(sec_out[1], "sec", pairs(sects, 1))
    edge = jnp.stack([sec_a, sec_b])
    sub_a = lax.ppermute(jnp.concatenate([sub_out[0], edge]), "sub", pairs(spans, 0))
    sub_b = lax.ppermute(jnp.concatenate([sub_out[1], edge]), "sub", pairs(spans, 1))

    def fine(*refs):
        fine_kernel((spans, sects), *refs)

    pack, basis = call(
        fine,
        (shape((1, nv, 4 * nv), F32), shape((cx, comps, nv, cy), F32)),
        [
            pltpu.VMEM((xext + 2, comps, nv, wide), F32),
            pltpu.VMEM((xext, comps, nv, wide), F32),
            pltpu.VMEM((xext, comps, nv, wide), F32),
            pltpu.VMEM((2 * H + 1, comps, nv, wide), F32),
            pltpu.VMEM((xext + 2, 8, wide), F32),
            pltpu.VMEM((2 * nv, 4 * nv), F32),
            pltpu.VMEM((2 * nv, 2 * nv), F32),
        ],
        "fine",
        [smem] + [vmem] * 6,
    )(kept_ranks, level_start, own, sec_a, sec_b, sub_a, sub_b)

    factor = math.sqrt(spans * comps * xext * yext)
    result = shape((k2, comps, cx, cy), F32)
    if spans != 8:
        return call(prolong_kernel, result, [], "prolong")(level_coefs(pack[0], k2, factor), basis)
    parts, held = [pack], pack
    for bit in (1, 2, 4):
        parts.append(lax.ppermute(held, "sub", [(i, i ^ bit) for i in range(spans)]))
        held = jnp.concatenate([held, parts[-1]])

    def level(*refs):
        level_kernel(spans, factor, *refs)

    return call(
        level, result, [pltpu.VMEM((spans, nv, 4 * nv), F32), pltpu.VMEM((k2, spans * nv), F32)], "level"
    )(*parts, basis)


def solution(mesh):
    placed = (
        P(None, None, "sub", "sec"),
        P(None, "sub", "sec"),
        P("sub", "sec"),
        P("sub", "sec"),
        P("sub", None),
    )
    return jax.shard_map(
        on_device,
        mesh=mesh,
        in_specs=placed,
        out_specs=P(None, None, "sub", "sec"),
        check_vma=False,
    )
```

time: 211 us -> 72.8 us (0.35); the launches traced: 207 us -> 72.5 us
  other arithmetic: 48.4 us -> 0.07 us
  blocking collectives: 39.6 us -> 0 us
  Pallas kernels: 0 us -> 34.1 us
  local copies, waits for them, and re-layouts: 36.2 us -> 2.68 us
  matrix products: 23.2 us -> 0 us
  waiting for transfers between devices: 29.3 us -> 17.3 us
  starting transfers between devices: 28.6 us -> 17.7 us
    psum x2 -> x0, blocking collectives: 39.6 us -> none  [on_device(): gram = lax.psum(jnp.dot(image.T, image, precision=highest), 'sub')]
    pallas_call x0 -> x3, Pallas kernels: none -> 34.1 us  [the longest x1 27.4 us: on_device(): call(fine, (shape((1, nv, 4 * nv), F32), shape((cx, comps, nv, cy), F32))...]
    reshape x6 -> x0, local copies, waits for them, and re-layouts: 22.4 us -> none  [the longest x3 15.4 us: orthonormal(): return solved.reshape(shape_before)]
    another operation x20 -> x0, other arithmetic: 21.4 us -> none  [the longest x6 7.19 us: orthonormal(): lower = jnp.linalg.cholesky(gram)]
    dot_general x13 -> x0, matrix products: 16.3 us -> none  [the longest x2 6.36 us: orthonormal(): gram = jnp.dot(flat, flat.T, precision=highest)]
    mul x2 -> x0, other arithmetic: 12.2 us -> none  [apply_operator(): ((4.0 + stiff_diag) * vectors - beside + shear_term * others) * inside]
    ppermute x10 -> x7, waiting for transfers between devices: 29.3 us -> 17.3 us  [the longest x1 10.6 us: on_device(): lax.ppermute(jnp.concatenate([sub_out[0], edge]), 'sub', pairs(spans, 0))]
    ppermute x10 -> x7, starting transfers between devices: 28.6 us -> 17.7 us  [the longest x3 7.63 us: on_device(): lax.ppermute(held, 'sub', [(i, i ^ bit) for i in range(spans)])]
  transfers between devices with their start and end apart: 10 -> 7, of which waited for: 6 -> 5; matrix products, arithmetic and copies ran while one was open for 46% -> 0% of each run, Pallas kernels for 0% -> 0%
where the time goes in v1:
time: 72.8 us; the launch traced here: 72.5 us
  Pallas kernels  34.1 us (47%)
  starting transfers between devices  17.7 us (24%)
  waiting for transfers between devices  17.3 us (24%)
  local copies, waits for them, and re-layouts  2.68 us (4%)
    pallas_call x1, Pallas kernels, on_device(): call(fine, (shape((1, nv, 4 * nv), F32), shape((cx, comps, nv, cy), F32))...  27.4 us
    ppermute x1, waiting for transfers between devices, on_device(): lax.ppermute(jnp.concatenate([sub_out[0], edge]), 'sub', pairs(spans, 0))  10.6 us
    ppermute x3, starting transfers between devices, on_device(): lax.ppermute(held, 'sub', [(i, i ^ bit) for i in range(spans)])  7.63 us
    ppermute x3, waiting for transfers between devices, on_device(): lax.ppermute(held, 'sub', [(i, i ^ bit) for i in range(spans)])  5.85 us
    pallas_call x1, Pallas kernels, on_device(): call(level, result, [pltpu.VMEM((spans, nv, 4 * nv), F32), pltpu.VMEM((k2...  5.43 us
    ppermute x1, starting transfers between devices, on_device(): sec_a = lax.ppermute(sec_out[0], 'sec', pairs(sects, 0))  4.39 us
    ppermute x1, starting transfers between devices, on_device(): lax.ppermute(jnp.concatenate([sub_out[0], edge]), 'sub', pairs(spans, 0))  4.34 us
    unnamed x9, local copies, waits for them, and re-layouts  2.64 us
  transfers between devices with their start and end apart: 7, of which 5 were waited for; matrix products, arithmetic and copies ran while one was open for 0% of the time, Pallas kernels for 0%

profile of v1, /device:TPU:0, one launch (start us, length us, event | category | flops | bytes accessed | tf_op | source)
XLA Modules:
  0.0 72.5 jit_solution(14644237975662217774)
XLA Ops:
  0.0 0.0 copy-start
  0.0 1.1 %copy-done = bf16[32,3,32,128]{3,2,1,0:T(8,128)(2,1)S(1)} copy-done((bf16[32,3,32,128]{3,2,1,0:T(8,128)(2,1)S(1)}, bf16[32,3,32,128]{3,2,1,0:T(8,128)(2,1)}, u32[]{:S(2)}) %copy-start) | copy-done | bytes 786456
  1.1 0.7 %copy-done.1 = bf16[3,32,128]{2,1,0:T(8,128)(2,1)S(1)} copy-done((bf16[3,32,128]{2,1,0:T(8,128)(2,1)S(1)}, bf16[3,32,128]{2,1,0:T(8,128)(2,1)}, u32[]{:S(2)}) %copy-start.1) | copy-done | bytes 24600
  1.9 0.7 copy-done.2
  2.6 1.2 %pack.1 = (bf16[32,4,32,128]{3,2,1,0:T(8,128)(2,1)S(1)}, bf16[2,4,32,128]{3,2,1,0:T(8,128)(2,1)S(1)}, bf16[2,6,4,32,128]{4,3,2,1,0:T(8,128)(2,1)S(1)}) custom-call(bf16[32,3,32,128]{3,2,1,0:T(8,128)(2,1)S(1)} %copy-done, bf16[3,32,128]{2,1,0:T(8,128)(2,1)S(1)} %copy-done.1, bf16[32,128]{1,0:T(8,128)(2,1)S(1)} %copy-done.2), custom_call_target="tpu_custom_call" | custom-call | tf_op jit(solution)/shard_map/pack/pallas_call | solution.py:317
  3.8 0.7 collective-permute-start.1
  4.5 4.4 %collective-permute-start = (bf16[4,32,128]{2,1,0:T(8,128)(2,1)S(1)}, bf16[4,32,128]{2,1,0:T(8,128)(2,1)S(1)}, u32[]{:S(2)}, u32[]{:S(2)}) collective-permute-start(bf16[4,32,128]{2,1,0:T(8,128)(2,1)S(1)} %get-tuple-element.20), channel_id=1, source_target_pairs={{0,1},{1,0},{2,3},{3,2},{4,5},{5,4},{6,7},{7,6},{8,9},{9,8},{10,11... | collective-permute-start | bytes 98312 | tf_op jit(solution)/shard_map/ppermute | solution.py:327
  8.9 0.0 collective-permute-done.1.refs_4_
  8.9 0.8 %collective-permute-done.refs_3_ = bf16[4,32,128]{2,1,0:T(8,128)(2,1)S(1)} collective-permute-done((bf16[4,32,128]{2,1,0:T(8,128)(2,1)S(1)}, bf16[4,32,128]{2,1,0:T(8,128)(2,1)S(1)}, u32[]{:S(2)}, u32[]{:S(2)}) %collective-permute-start) | collective-permute-done | bytes 32800 | tf_op jit(solution)/shard_map/ppermute | solution.py:327
  9.7 0.1 pad_maximum_fusion
  9.8 0.7 collective-permute-start.3
  10.5 4.3 %collective-permute-start.2 = (bf16[8,4,32,128]{3,2,1,0:T(8,128)(2,1)S(1)}, bf16[8,4,32,128]{3,2,1,0:T(8,128)(2,1)S(1)}, u32[]{:S(2)}, u32[]{:S(2)}) collective-permute-start(bf16[8,4,32,128]{3,2,1,0:T(8,128)(2,1)S(1)} %get-tuple-element.18), channel_id=1, source_target_pairs={{0,4},{4,0},{8,12},{12,8},{16,20},{20,16},{24,28},{28,24},{1,5},{5... | collective-permute-start | bytes 786440 | tf_op jit(solution)/shard_map/ppermute | solution.py:330
  15.5 0.0 copy-done.3
  15.5 0.1 copy.6.refs_1_
  15.6 0.0 collective-permute-done.3.refs_6_
  15.6 10.6 %collective-permute-done.2.refs_5_ = bf16[8,4,32,128]{3,2,1,0:T(8,128)(2,1)S(1)} collective-permute-done((bf16[8,4,32,128]{3,2,1,0:T(8,128)(2,1)S(1)}, bf16[8,4,32,128]{3,2,1,0:T(8,128)(2,1)S(1)}, u32[]{:S(2)}, u32[]{:S(2)}) %collective-permute-start.2) | collective-permute-done | bytes 262176 | tf_op jit(solution)/shard_map/ppermute | solution.py:330
  26.2 27.4 %fine.1 = (f32[1,32,128]{2,1,0:T(8,128)S(1)}, f32[32,3,32,128]{3,2,1,0:T(8,128)S(1)}) custom-call(s32[1,1]{1,0:T(1,128)S(6)} %copy.7.refs_0_, f32[32,16]{1,0:T(8,128)S(1)} %copy.6.refs_1_, bf16[32,4,32,128]{3,2,1,0:T(8,128)(2,1)S(1)} %get-tuple-element.10.refs_2_, bf16[4,32,128]{2,1,0:T(8,128)(2,1)S(1)} %collective-permute-done.refs_3_, ...), custom_call_target="tpu_custom_call" | custom-call | tf_op jit(solution)/shard_map/fine/pallas_call | solution.py:336
  53.6 2.5 %collective-permute-start.4 = (f32[1,32,128]{2,1,0:T(8,128)S(1)}, f32[1,32,128]{2,1,0:T(8,128)S(1)}, u32[]{:S(2)}, u32[]{:S(2)}) collective-permute-start(f32[1,32,128]{2,1,0:T(8,128)S(1)} %get-tuple-element.13.refs_0_), channel_id=1, source_target_pairs={{0,4},{4,0},{8,12},{12,8},{16,20},{20,16},{24,28},{28,24},{1,5},{5... | collective-permute-start | bytes 49160 | tf_op jit(solution)/shard_map/ppermute | solution.py:358
  56.1 1.7 %collective-permute-done.4.refs_1_ = f32[1,32,128]{2,1,0:T(8,128)S(1)} collective-permute-done((f32[1,32,128]{2,1,0:T(8,128)S(1)}, f32[1,32,128]{2,1,0:T(8,128)S(1)}, u32[]{:S(2)}, u32[]{:S(2)}) %collective-permute-start.4) | collective-permute-done | bytes 16416 | tf_op jit(solution)/shard_map/ppermute | solution.py:358
  57.8 2.1 %collective-permute-start.5 = (f32[2,32,128]{2,1,0:T(8,128)S(1)}, f32[2,32,128]{2,1,0:T(8,128)S(1)}, u32[]{:S(2)}, u32[]{:S(2)}) collective-permute-start(f32[2,32,128]{2,1,0:T(8,128)S(1)} %pad_maximum_fusion.5), channel_id=1, source_target_pairs={{0,8},{4,12},{8,0},{12,4},{16,24},{20,28},{24,16},{28,20},{1,9},{5... | collective-permute-start | bytes 98312 | tf_op jit(solution)/shard_map/ppermute | solution.py:358
  59.9 1.9 %collective-permute-done.5.refs_2_ = f32[2,32,128]{2,1,0:T(8,128)S(1)} collective-permute-done((f32[2,32,128]{2,1,0:T(8,128)S(1)}, f32[2,32,128]{2,1,0:T(8,128)S(1)}, u32[]{:S(2)}, u32[]{:S(2)}) %collective-permute-start.5) | collective-permute-done | bytes 32800 | tf_op jit(solution)/shard_map/ppermute | solution.py:358
  61.8 3.0 %collective-permute-start.6 = (f32[4,32,128]{2,1,0:T(8,128)S(1)}, f32[4,32,128]{2,1,0:T(8,128)S(1)}, u32[]{:S(2)}, u32[]{:S(2)}) collective-permute-start(f32[4,32,128]{2,1,0:T(8,128)S(1)} %pad_maximum_fusion.4), channel_id=1, source_target_pairs={{0,16},{4,20},{8,24},{12,28},{16,0},{20,4},{24,8},{28,12},{1,17},{... | collective-permute-start | bytes 196616 | tf_op jit(solution)/shard_map/ppermute | solution.py:358
  64.8 2.2 %collective-permute-done.6.refs_3_ = f32[4,32,128]{2,1,0:T(8,128)S(1)} collective-permute-done((f32[4,32,128]{2,1,0:T(8,128)S(1)}, f32[4,32,128]{2,1,0:T(8,128)S(1)}, u32[]{:S(2)}, u32[]{:S(2)}) %collective-permute-start.6) | collective-permute-done | bytes 65568 | tf_op jit(solution)/shard_map/ppermute | solution.py:358
  67.1 5.4 %level.1 = f32[16,3,32,128]{3,2,1,0:T(8,128)} custom-call(f32[1,32,128]{2,1,0:T(8,128)S(1)} %get-tuple-element.13.refs_0_, f32[1,32,128]{2,1,0:T(8,128)S(1)} %collective-permute-done.4.refs_1_, f32[2,32,128]{2,1,0:T(8,128)S(1)} %collective-permute-done.5.refs_2_, f32[4,32,128]{2,1,0:T(8,128)S(1)} %collective-permute-done.6.refs_3_, ...), custom_call_target="tpu_custom_call" | custom-call | tf_op jit(solution)/shard_map/level/pallas_call | solution.py:364
  (7 shorter events, 0.0 us)
Async XLA Ops:
  0.0 1.1 %copy-start = (bf16[32,3,32,128]{3,2,1,0:T(8,128)(2,1)S(1)}, bf16[32,3,32,128]{3,2,1,0:T(8,128)(2,1)}, u32[]{:S(2)}) copy-start(bf16[32,3,32,128]{3,2,1,0:T(8,128)(2,1)} %v_ref.1) | copy-start | bytes 2359300
  1.1 0.7 %copy-start.1 = (bf16[3,32,128]{2,1,0:T(8,128)(2,1)S(1)}, bf16[3,32,128]{2,1,0:T(8,128)(2,1)}, u32[]{:S(2)}) copy-start(bf16[3,32,128]{2,1,0:T(8,128)(2,1)} %k_ref.1) | copy-start | bytes 73732
  1.9 0.7 copy-start.2
  2.6 12.9 %copy-start.3 = (f32[32,16]{0,1:T(8,128)S(1)}, f32[32,16]{0,1:T(8,128)}, u32[]{:S(2)}) copy-start(f32[32,16]{0,1:T(8,128)} %param.9) | copy-start | bytes 6148
  3.8 5.1 %collective-permute-start.1 = (bf16[4,32,128]{2,1,0:T(8,128)(2,1)S(1)}, bf16[4,32,128]{2,1,0:T(8,128)(2,1)S(1)}, u32[]{:S(2)}, u32[]{:S(2)}) collective-permute-start(bf16[4,32,128]{2,1,0:T(8,128)(2,1)S(1)} %get-tuple-element.19), channel_id=1, source_target_pairs={{1,2},{2,1},{5,6},{6,5},{9,10},{10,9},{13,14},{14,13},{17,18},{18,... | collective-permute-start | bytes 98312 | tf_op jit(solution)/shard_map/ppermute | solution.py:328
  4.5 5.3 %collective-permute-start = (bf16[4,32,128]{2,1,0:T(8,128)(2,1)S(1)}, bf16[4,32,128]{2,1,0:T(8,128)(2,1)S(1)}, u32[]{:S(2)}, u32[]{:S(2)}) collective-permute-start(bf16[4,32,128]{2,1,0:T(8,128)(2,1)S(1)} %get-tuple-element.20), channel_id=1, source_target_pairs={{0,1},{1,0},{2,3},{3,2},{4,5},{5,4},{6,7},{7,6},{8,9},{9,8},{10,11... | collective-permute-start | bytes 98312 | tf_op jit(solution)/shard_map/ppermute | solution.py:327
  9.8 5.8 %collective-permute-start.3 = (bf16[8,4,32,128]{3,2,1,0:T(8,128)(2,1)S(1)}, bf16[8,4,32,128]{3,2,1,0:T(8,128)(2,1)S(1)}, u32[]{:S(2)}, u32[]{:S(2)}) collective-permute-start(bf16[8,4,32,128]{3,2,1,0:T(8,128)(2,1)S(1)} %get-tuple-element.17), channel_id=1, source_target_pairs={{4,8},{8,4},{12,16},{16,12},{20,24},{24,20},{5,9},{9,5},{13,17},{1... | collective-permute-start | bytes 786440 | tf_op jit(solution)/shard_map/ppermute | solution.py:331
  10.5 15.7 %collective-permute-start.2 = (bf16[8,4,32,128]{3,2,1,0:T(8,128)(2,1)S(1)}, bf16[8,4,32,128]{3,2,1,0:T(8,128)(2,1)S(1)}, u32[]{:S(2)}, u32[]{:S(2)}) collective-permute-start(bf16[8,4,32,128]{3,2,1,0:T(8,128)(2,1)S(1)} %get-tuple-element.18), channel_id=1, source_target_pairs={{0,4},{4,0},{8,12},{12,8},{16,20},{20,16},{24,28},{28,24},{1,5},{5... | collective-permute-start | bytes 786440 | tf_op jit(solution)/shard_map/ppermute | solution.py:330
  53.6 4.2 %collective-permute-start.4 = (f32[1,32,128]{2,1,0:T(8,128)S(1)}, f32[1,32,128]{2,1,0:T(8,128)S(1)}, u32[]{:S(2)}, u32[]{:S(2)}) collective-permute-start(f32[1,32,128]{2,1,0:T(8,128)S(1)} %get-tuple-element.13.refs_0_), channel_id=1, source_target_pairs={{0,4},{4,0},{8,12},{12,8},{16,20},{20,16},{24,28},{28,24},{1,5},{5... | collective-permute-start | bytes 49160 | tf_op jit(solution)/shard_map/ppermute | solution.py:358
  57.8 4.0 %collective-permute-start.5 = (f32[2,32,128]{2,1,0:T(8,128)S(1)}, f32[2,32,128]{2,1,0:T(8,128)S(1)}, u32[]{:S(2)}, u32[]{:S(2)}) collective-permute-start(f32[2,32,128]{2,1,0:T(8,128)S(1)} %pad_maximum_fusion.5), channel_id=1, source_target_pairs={{0,8},{4,12},{8,0},{12,4},{16,24},{20,28},{24,16},{28,20},{1,9},{5... | collective-permute-start | bytes 98312 | tf_op jit(solution)/shard_map/ppermute | solution.py:358
  61.8 5.3 %collective-permute-start.6 = (f32[4,32,128]{2,1,0:T(8,128)S(1)}, f32[4,32,128]{2,1,0:T(8,128)S(1)}, u32[]{:S(2)}, u32[]{:S(2)}) collective-permute-start(f32[4,32,128]{2,1,0:T(8,128)S(1)} %pad_maximum_fusion.4), channel_id=1, source_target_pairs={{0,16},{4,20},{8,24},{12,28},{16,0},{20,4},{24,8},{28,12},{1,17},{... | collective-permute-start | bytes 196616 | tf_op jit(solution)/shard_map/ppermute | solution.py:358

commit v2 on v0

v2 whole, which is shorter than its diff:
```python
import math

import jax
import jax.numpy as jnp
from jax import lax
from jax.experimental import pallas as pl
from jax.experimental.pallas import tpu as pltpu
from jax.sharding import PartitionSpec as P

H = 4
MIB = 1 << 20
F32 = jnp.float32
BF16 = jnp.bfloat16
NN = (((1,), (0,)), ((), ()))
NT = (((1,), (1,)), ((), ()))
TN = (((0,), (0,)), ((), ()))


def iota(shape, dim):
    return lax.broadcasted_iota(jnp.int32, shape, dim)


def split(x):
    high = x.astype(BF16)
    return high, (x - high.astype(F32)).astype(BF16)


def dot(a, b, dims):
    return lax.dot_general(a, b, dims, preferred_element_type=F32)


def dot3(a, b, dims):
    (ah, al), (bh, bl) = split(a), split(b)
    return dot(ah, bh, dims) + (dot(ah, bl, dims) + dot(al, bh, dims))


def inverse_factor(gram, size):
    row, lane = iota((size, 128), 0), iota((size, 128), 1)
    work = jnp.where(lane < size, gram, jnp.where(lane == row + size, 1.0, 0.0))
    for j in range(size - 1):
        column = work[:, j : j + 1]
        pivot = work[j : j + 1, :]
        factor = jnp.where(iota((size, 1), 0) > j, column / column[j : j + 1, :], 0.0)
        work = work - factor * pivot
    diag = jnp.sum(jnp.where(lane == row, work, 0.0), axis=1, keepdims=True)
    return pltpu.roll(work / jnp.sqrt(diag), 128 - size, 1)


def slots_of(cx):
    own = cx // H
    return own, own, own + 1, own + 2, own + 3


def halves(octet_a, octet_b):
    return jnp.where(iota(octet_a.shape, 0) < H, octet_a, octet_b)


def swap(octet):
    return pltpu.roll(octet, H, 0)


def pack_kernel(v_hbm, k_hbm, g_hbm, own_ref, kt_ref, sec_a, sec_b, v_buf, k_buf, g_buf, vf, kf, sems):
    nv, comps, cx, cy = v_buf.shape
    copies = [
        pltpu.make_async_copy(src, dst, sems.at[i])
        for i, (src, dst) in enumerate(((k_hbm, k_buf), (g_hbm, g_buf), (v_hbm, v_buf)))
    ]
    for copy in copies:
        copy.start()
    sec_even = lax.rem(lax.axis_index("sec"), 2) == 0
    for copy in copies:
        copy.wait()
    vf[...] = v_buf[...].astype(F32).reshape(vf.shape)
    kf[: comps * cx] = k_buf[...].astype(F32).reshape(comps * cx, cy)
    kf[comps * cx :] = g_buf[...].astype(F32)
    firsts, lasts = [], []
    own = cx // H
    for p in range(own + 2):
        rows = [b * own + p for b in range(H)] if p < own else [b + (p - own) * (cx - H) for b in range(H)]
        for c in range(comps):
            stack = [vf[pl.ds(c * cx + x, nv, stride=comps * cx), :] for x in rows]
            turned = jnp.concatenate(stack, axis=0).T
            own_ref[p, c] = turned.astype(BF16)
            firsts.append(turned[:8])
            lasts.append(turned[cy - 8 :])
    turned = kf[...].T
    kt_ref[...] = turned.astype(BF16)
    for octets, value in ((firsts, turned[:8]), (lasts, turned[cy - 8 :])):
        octets.append(value)
        if len(octets) % 2:
            octets.append(jnp.zeros_like(value))
    pairs_of = range(0, len(firsts), 2)
    left = [halves(firsts[q], swap(firsts[q + 1])) for q in pairs_of]
    right = [halves(swap(lasts[q]), lasts[q + 1]) for q in pairs_of]
    left, right = jnp.concatenate(left, axis=0), jnp.concatenate(right, axis=0)
    sec_a[...] = jnp.where(sec_even, right, left).astype(BF16)
    sec_b[...] = jnp.where(sec_even, left, right).astype(BF16)


def margin_octets(sec_a, sec_b, sec_even, count):
    a, b = sec_a[...].astype(F32), sec_b[...].astype(F32)
    hi, lo = jnp.where(sec_even, a, b), jnp.where(sec_even, b, a)
    out = []
    for q in range(count):
        at = slice(8 * (q // 2), 8 * (q // 2) + 8)
        out.append(halves(swap(hi[at]), lo[at]) if q % 2 else halves(hi[at], swap(lo[at])))
    return out


def edge_kernel(own_ref, kt_ref, sec_a, sec_b, sub_a, sub_b):
    slots, comps, cy, lanes = own_ref.shape
    sub_even = lax.rem(lax.axis_index("sub"), 2) == 0
    sec_even = lax.rem(lax.axis_index("sec"), 2) == 0
    octets = margin_octets(sec_a, sec_b, sec_even, slots * comps + 1)
    first, last = slots - 2, slots - 1
    head = octets[first * comps : first * comps + comps] + octets[-1:]
    tail = octets[last * comps : last * comps + comps] + octets[-1:]
    head, tail = jnp.concatenate(head, axis=0), jnp.concatenate(tail, axis=0)
    for ref, to_next in ((sub_a, sub_even), (sub_b, jnp.logical_not(sub_even))):
        slot = jnp.where(to_next, last, first)
        for c in range(comps):
            ref[c * cy : (c + 1) * cy] = own_ref[slot, c]
        ref[comps * cy : (comps + 1) * cy] = kt_ref[...]
        ref[(comps + 1) * cy :] = jnp.where(to_next, tail, head).astype(BF16)


def fine_kernel(sizes, rank_ref, start_ref, own_ref, kt_ref, sec_a, sec_b, sub_a, sub_b, pack_ref, x2, v0, x1, coef, high2, low2, high3, low3, margin3):
    spans, sects = sizes
    _, comps, cy, lanes = own_ref.shape
    nv = start_ref.shape[0]
    cx = kt_ref.shape[1] // (comps + 1)
    OWN, BEFORE, AFTER, HEAD, TAIL = slots_of(cx)
    s, t = lax.axis_index("sub"), lax.axis_index("sec")
    sub_even, sec_even = lax.rem(s, 2) == 0, lax.rem(t, 2) == 0
    kinds = comps + 1
    low, top = slice(0, 8), slice(8 + cy, 16 + cy)
    mid = slice(8, 8 + cy)

    octets = margin_octets(sec_a, sec_b, sec_even, (OWN + 2) * comps + 1)

    def put(slot, c, rows, octet):
        v0[slot, c, mid, :] = rows
        v0[slot, c, low, :] = octet
        v0[slot, c, top, :] = octet

    for p in range(OWN + 2):
        for c in range(comps):
            put(p if p < OWN else HEAD + p - OWN, c, own_ref[p, c].astype(F32), octets[p * comps + c])

    def received(first, count):
        a, b = sub_a[first : first + count].astype(F32), sub_b[first : first + count].astype(F32)
        return jnp.where(sub_even, a, b), jnp.where(sub_even, b, a)

    for c in range(comps):
        after, before = received(c * cy, cy)
        after_octet, before_octet = received(kinds * cy + 8 * c, 8)
        put(BEFORE, c, before, before_octet)
        put(AFTER, c, after, after_octet)

    octet_row = iota((8, lanes), 0)
    col_in = jnp.where(octet_row < H, jnp.where(t < sects - 1, 1.0, 0.0), jnp.where(t > 0, 1.0, 0.0))
    has_before, has_after = jnp.where(s > 0, 1.0, 0.0), jnp.where(s < spans - 1, 1.0, 0.0)
    row_in = {BEFORE: has_before, AFTER: has_after}

    def padded(rows, octet):
        return jnp.concatenate([rows, octet, jnp.zeros_like(octet)], axis=0).astype(BF16)

    after, before = received(comps * cy, cy)
    after_octet, before_octet = received(kinds * cy + 8 * comps, 8)
    table = padded(kt_ref[...].astype(F32), octets[-1])
    table_after, table_before = padded(after, after_octet), padded(before, before_octet)
    table_first = jnp.concatenate([table, table_after], axis=0)
    table_last = jnp.concatenate([table, table_before], axis=0)
    source, block = iota((lanes, lanes), 0), iota((lanes, lanes), 1) // nv

    def spread(table, wanted):
        pick = [jnp.where(source == kind * cx + wanted, 1.0, 0.0).astype(BF16) for kind in range(kinds)]
        out = dot(table, jnp.concatenate(pick, axis=1), NN)
        return [out[:, kind * lanes : (kind + 1) * lanes] for kind in range(kinds)]

    def put_coef(slot, values, first):
        inside = row_in.get(slot)
        for at, length, mask in ((0, cy, inside), (cy, 8, col_in if inside is None else col_in * inside)):
            rows = [v[first + at : first + at + length] for v in values]
            for kind in range(kinds):
                value = 4.0 + rows[kind] - rows[comps] if kind < comps else rows[kind]
                coef[slot, kind, at : at + length, :] = value if mask is None else value * mask

    for p in range(OWN):
        put_coef(p, spread(table, block * OWN + p), 0)
    values = spread(table_first, block)
    put_coef(HEAD, values, 0)
    put_coef(AFTER, values, cy + 16)
    values = spread(table_last, block + (cx - H))
    put_coef(TAIL, values, 0)
    put_coef(BEFORE, values, cy + 16)

    def operator(src, rows, first_row, length, shifted, strips, emit):
        lane = iota((length, lanes), 1)
        in_first, in_last = lane < nv, lane >= lanes - nv
        masked = shifted is not None

        def at(slot, c):
            return src[slot, c, rows(0), :]

        def up_of(slot, c):
            if 0 < slot < OWN:
                return at(slot - 1, c)
            if slot in (0, AFTER):
                return pltpu.roll(jnp.where(in_last, at(BEFORE if slot == 0 else OWN - 1, c), at(OWN - 1 if slot == 0 else AFTER, c)), nv, 1)
            if slot == HEAD:
                return pltpu.roll(jnp.where(in_last, at(BEFORE, c), at(HEAD, c)), nv, 1)
            return jnp.where(in_first, 0.0, pltpu.roll(at(slot, c), nv, 1))

        def down_of(slot, c):
            if slot < OWN - 1:
                return at(slot + 1, c)
            if slot in (OWN - 1, BEFORE):
                return pltpu.roll(jnp.where(in_first, at(AFTER if slot == OWN - 1 else 0, c), at(0 if slot == OWN - 1 else BEFORE, c)), lanes - nv, 1)
            if slot == TAIL:
                return pltpu.roll(jnp.where(in_first, at(AFTER, c), at(TAIL, c)), lanes - nv, 1)
            return jnp.where(in_last, 0.0, pltpu.roll(at(slot, c), lanes - nv, 1))

        for slot in range(TAIL + 1 if strips else AFTER + 1):
            v = [at(slot, c) for c in range(comps)]
            weight = [coef[slot, kind, first_row, :] for kind in range(kinds)]
            total = weight[comps] * (v[0] + v[1] + v[2])
            for c in range(comps):
                if masked:
                    sides = shifted(slot, c)
                else:
                    sides = src[slot, c, rows(-1), :] + src[slot, c, rows(1), :]
                beside = sides + (up_of(slot, c) + down_of(slot, c))
                inside = row_in.get(slot)
                if masked:
                    beside = beside * (col_in if inside is None else col_in * inside)
                elif inside is not None:
                    beside = beside * inside
                emit(slot, c, weight[c] * v[c] + total - beside)

    def apply(src, strips, emit_rows, emit_margin):
        def body(j, carry):
            base = 16 * j

            def rows(d):
                start = 8 + base + d
                return pl.ds(pl.multiple_of(start, 8) if d == 0 else start, 16)

            def emit(slot, c, value):
                emit_rows(slot, c, pl.multiple_of(base, 16), value)

            operator(src, rows, pl.ds(pl.multiple_of(base, 16), 16), 16, None, strips, emit)
            return carry

        lax.fori_loop(0, cy // 16, body, 0)

        def shifted(slot, c):
            left = jnp.where(octet_row == H, 0.0, src[slot, c, 7 + cy : 15 + cy, :])
            return left + jnp.where(octet_row == H - 1, 0.0, src[slot, c, 1:9, :])

        operator(src, lambda d: top, slice(cy, cy + 8), 8, shifted, strips, emit_margin)

    def store(dst, split_too=False):
        def emit_rows(slot, c, base, value):
            dst[slot, c, pl.ds(base + 8, 16), :] = value
            if split_too and slot < HEAD:
                high2[slot, c, pl.ds(base, 16), :], low2[slot, c, pl.ds(base, 16), :] = split(value)

        def emit_margin(slot, c, value):
            dst[slot, c, low, :] = value
            dst[slot, c, top, :] = value

        return emit_rows, emit_margin

    apply(v0, True, *store(x1))
    apply(x1, True, *store(x2, True))

    def split_rows(slot, c, base, value):
        high3[slot, c, pl.ds(base, 16), :], low3[slot, c, pl.ds(base, 16), :] = split(value)

    def keep_margin(slot, c, value):
        margin3[slot, c] = value

    apply(x2, False, split_rows, keep_margin)

    def fold(z):
        return sum(pltpu.roll(z[b * nv : (b + 1) * nv], (z.shape[1] - b * nv) % z.shape[1], 1) if b else z[:nv] for b in range(H))

    def gram_of(h2, l2, h3, l3):
        main = dot(h2, jnp.concatenate([h2, l2, h3, l3], axis=1), TN)
        return main, dot(l2, h3, TN)

    def flat(ref, first, count):
        return ref[first : first + count].reshape(count * comps * cy, lanes)

    octet_margins = [x2[slot, c, top, :] for slot in range(AFTER + 1) for c in range(comps)]
    h2, l2 = split(jnp.concatenate(octet_margins, axis=0))
    h3, l3 = split(margin3[...].reshape((AFTER + 1) * comps * 8, lanes))
    main, cross = gram_of(h2, l2, h3, l3)
    for first in range(0, AFTER + 1, 2):
        part = gram_of(*(flat(ref, first, 2) for ref in (high2, low2, high3, low3)))
        main, cross = main + part[0], cross + part[1]
    main, cross = fold(main), fold(cross)[:, :nv]
    mixed = main[:, lanes : lanes + nv]
    gram = main[:, :nv] + (mixed + mixed.T)
    image = main[:, 2 * lanes : 2 * lanes + nv] + main[:, 3 * lanes : 3 * lanes + nv] + cross

    def rim(strip, first, block, own_first):
        own, other = [], []
        for at, weight_at in ((mid, slice(0, cy)), (top, slice(cy, cy + 8))):
            for c in range(comps):
                held = [x2[first + i, c, at, block * nv : (block + 1) * nv] for i in range(H)]
                weight = coef[strip, c, weight_at, :] + coef[strip, comps, weight_at, :]
                own.append(jnp.concatenate(held, axis=1) * weight)
                other.append(x2[strip, c, at, :])
        own.append(jnp.zeros((8, lanes), F32))
        other.append(jnp.zeros((8, lanes), F32))
        own, other = jnp.concatenate(own, axis=0), jnp.concatenate(other, axis=0)
        a, b = (own, other) if own_first else (other, own)
        return fold(dot3(a, b, TN))[:, :nv]

    rim_next = rim(TAIL, OWN - H, H - 1, True) * has_after
    rim_prev = rim(HEAD, 0, 0, False) * has_before

    pad = jnp.zeros((nv, lanes - nv), F32)
    inverse = inverse_factor(jnp.concatenate([gram, pad], axis=1), nv)[:, :nv]
    inverse = jnp.where(iota((nv, nv), 0) < rank_ref[0, 0], inverse, 0.0)
    pack_ref[0, :nv] = jnp.concatenate([image, rim_next, rim_prev, inverse], axis=1)
    start = [start_ref[8 * i : 8 * i + 8, :] for i in range(nv // 8)]
    pad = jnp.zeros((8, lanes - start_ref.shape[1] * len(start)), F32)
    pack_ref[0, nv:] = jnp.concatenate(start + [pad], axis=1)


def prolong(coefs, basis_ref, out_ref):
    k2, comps, cx, cy = out_ref.shape
    nv = coefs.shape[1]
    own = cx // H
    tiled = jnp.concatenate([coefs] * H, axis=1)
    tiled = jnp.concatenate([tiled, jnp.zeros_like(tiled)], axis=1)[:, : H * nv]
    tiled = jnp.broadcast_to(tiled[:, None, :], (k2, 8, H * nv)).reshape(8 * k2, H * nv)
    same = lax.rem(iota(tiled.shape, 0), 8) == iota(tiled.shape, 1) // nv
    high, low = split(jnp.where(same, tiled, 0.0))
    left = jnp.concatenate([high, low, high], axis=1)
    for c in range(comps):
        for p in range(own):
            bh, bl = split(basis_ref[p, c, 8 : 8 + cy, :])
            out = dot(left, jnp.concatenate([bh, bh, bl], axis=1), NT).reshape(k2, 8, cy)
            out_ref[:, c, pl.ds(p, H, stride=own), :] = out[:, :H]


def starts_of(block, nv, k2):
    return jnp.concatenate([block[nv:, k2 * i : k2 * i + k2] for i in range(nv // 8)], axis=0)


def level_kernel(spans, nv, factor, p0, p1, p2, p3, basis_ref, out_ref, packs):
    k2 = out_ref.shape[0]
    n = spans * nv
    s = lax.axis_index("sub")
    base = 0
    for part in (p0, p1, p2, p3):
        packs[base : base + part.shape[0]] = part[...]
        base += part.shape[0]
    lane = iota((nv, n), 1)
    upper, diagonal, starts = [], [], []
    blocks = [packs[jnp.bitwise_xor(s, b)] for b in range(spans)]
    zeros = jnp.zeros((nv, n - 4 * nv), F32)
    for b in range(spans):
        placed = jnp.concatenate([blocks[b][:nv], zeros], axis=1)
        pair = jnp.where(lane < nv, 0.5 * placed, jnp.where(lane < 2 * nv, placed, 0.0))
        if b + 1 < spans:
            after = jnp.concatenate([blocks[b + 1][:nv], zeros], axis=1)
            pair = pair + pltpu.roll(jnp.where((lane >= 2 * nv) & (lane < 3 * nv), after, 0.0), n - nv, 1)
        upper.append(pltpu.roll(pair, nv * b, 1) if b else pair)
        inv = jnp.where((lane >= 3 * nv) & (lane < 4 * nv), placed, 0.0)
        diagonal.append(pltpu.roll(inv, (nv * (b - 3)) % n, 1) if b != 3 else inv)
        starts.append(starts_of(blocks[b], nv, k2))
    q = jnp.concatenate(upper, axis=0)
    inv = jnp.concatenate(diagonal, axis=0)
    y = jnp.concatenate(starts, axis=0)
    full = q + q.T
    u = dot3(y, inv, TN)
    z = dot3(dot3(u, full, NN), inv, NT)
    u = dot3(z, inv, NN)
    z = dot3(dot3(u, full, NN), inv, NT)
    gram = dot3(z, z, NT)
    gram = jnp.concatenate([gram, jnp.zeros((k2, 128 - k2), F32)], axis=1)
    solve = inverse_factor(gram, k2)[:, :k2]
    y = dot3(solve, z, NN)
    coefs = dot3(y, inv, NN)
    own = jnp.zeros((k2, nv), F32)
    for b in range(spans):
        own = jnp.where(s == b, coefs[:, nv * b : nv * b + nv], own)
    prolong(factor * own, basis_ref, out_ref)


def pairs(count, offset):
    return [q for i in range(offset, count - 1, 2) for q in ((i, i + 1), (i + 1, i))]


def from_behind(block, axis, distance):
    devices = range(lax.axis_size(axis))
    return lax.ppermute(block, axis, [(i - distance, i) for i in devices if i - distance in devices])


def level_coefs(pack, nv, k2, factor):
    highest = lax.Precision.HIGHEST
    own, rim_next, rim_prev, inv = (pack[:nv, nv * i : nv * i + nv] for i in range(4))
    z = starts_of(pack, nv, k2)
    rim = rim_next + from_behind(rim_prev, "sub", -1)
    rim_before = from_behind(rim, "sub", 1)
    for step in range(2):
        u = jnp.dot(inv.T, z, precision=highest)
        image = jnp.dot(own, u, precision=highest)
        image = image + jnp.dot(rim, from_behind(u, "sub", -1), precision=highest)
        image = image + jnp.dot(rim_before.T, from_behind(u, "sub", 1), precision=highest)
        z = jnp.dot(inv, image, precision=highest)
    lower = jnp.linalg.cholesky(lax.psum(jnp.dot(z.T, z, precision=highest), "sub"))
    y = lax.linalg.triangular_solve(lower, z.T, left_side=True, lower=True)
    return factor * jnp.dot(y, inv, precision=highest)


def call(kernel, out_shape, scratch, name, in_specs=None):
    return pl.pallas_call(
        kernel,
        out_shape=out_shape,
        scratch_shapes=scratch,
        compiler_params=pltpu.CompilerParams(vmem_limit_bytes=48 * MIB),
        name=name,
        **({"in_specs": in_specs} if in_specs else {}),
    )


def on_device(start_vectors, stiffness, coupling, kept_ranks, level_start):
    spans, sects = lax.axis_size("sub"), lax.axis_size("sec")
    nv, comps, cx, cy = start_vectors.shape
    k2 = level_start.shape[1]
    channels = comps + 1
    slots = slots_of(cx)[-1] + 1
    shape = jax.ShapeDtypeStruct
    vmem = pl.BlockSpec(memory_space=pltpu.VMEM)
    smem = pl.BlockSpec(memory_space=pltpu.SMEM)
    hbm = pl.BlockSpec(memory_space=pltpu.HBM)

    pieces = (cx // H + 2) * comps + 1
    sec_shape = shape((-(-pieces // 2) * 8, cy), BF16)
    own, kt, sec_a, sec_b = call(
        pack_kernel,
        (shape((cx // H + 2, comps, cy, H * nv), BF16), shape((cy, channels * cx), BF16), sec_shape, sec_shape),
        [
            pltpu.VMEM(start_vectors.shape, BF16),
            pltpu.VMEM(stiffness.shape, BF16),
            pltpu.VMEM(coupling.shape, BF16),
            pltpu.VMEM((nv * comps * cx, cy), F32),
            pltpu.VMEM((channels * cx, cy), F32),
            pltpu.SemaphoreType.DMA((3,)),
        ],
        "pack",
        [hbm] * 3,
    )(start_vectors, stiffness, coupling)
    sec_a = lax.ppermute(sec_a, "sec", pairs(sects, 0))
    sec_b = lax.ppermute(sec_b, "sec", pairs(sects, 1))
    sub_shape = shape((channels * (cy + 8), H * nv), BF16)
    sub_a, sub_b = call(edge_kernel, (sub_shape, sub_shape), [], "edge")(own, kt, sec_a, sec_b)
    sub_a = lax.ppermute(sub_a, "sub", pairs(spans, 0))
    sub_b = lax.ppermute(sub_b, "sub", pairs(spans, 1))

    def fine(*refs):
        fine_kernel((spans, sects), *refs)

    rows = (slots, comps, cy + 16, H * nv)
    halved = pltpu.VMEM((slots - 2, comps, cy, H * nv), BF16)
    pack, basis = call(
        fine,
        (shape((1, nv + 8, cy), F32), shape(rows, F32)),
        [
            pltpu.VMEM(rows, F32),
            pltpu.VMEM(rows, F32),
            pltpu.VMEM((slots, channels, cy + 8, H * nv), F32),
            halved,
            halved,
            halved,
            halved,
            pltpu.VMEM((slots - 2, comps, 8, H * nv), F32),
        ],
        "fine",
        [smem] + [vmem] * 7,
    )(kept_ranks, level_start, own, kt, sec_a, sec_b, sub_a, sub_b)

    factor = math.sqrt(spans * comps * (cx + 2 * H) * (cy + 2 * H))
    result = shape((k2, comps, cx, cy), F32)
    if spans != 8:

        def prolong_kernel(coefs_ref, basis_ref, out_ref):
            prolong(coefs_ref[...], basis_ref, out_ref)

        return call(prolong_kernel, result, [], "prolong")(level_coefs(pack[0], nv, k2, factor), basis)
    parts, held = [pack], pack
    for bit in (1, 2, 4):
        parts.append(lax.ppermute(held, "sub", [(i, i ^ bit) for i in range(spans)]))
        held = jnp.concatenate([held, parts[-1]])

    def level(*refs):
        level_kernel(spans, nv, factor, *refs)

    return call(level, result, [pltpu.VMEM((spans,) + pack.shape[1:], F32)], "level")(*parts, basis)


def solution(mesh):
    placed = (
        P(None, None, "sub", "sec"),
        P(None, "sub", "sec"),
        P("sub", "sec"),
        P("sub", "sec"),
        P("sub", None),
    )
    return jax.shard_map(
        on_device,
        mesh=mesh,
        in_specs=placed,
        out_specs=P(None, None, "sub", "sec"),
        check_vma=False,
    )
```

time: 211 us -> 47.4 us (0.22)
  the two profiles are of different devices: /device:TPU:0 before, /device:TPU:26 now
where the time goes in v2:
time: 47.4 us; the launch traced here: 47.1 us
  waiting for transfers between devices  19.9 us (42%)
  Pallas kernels  15.9 us (34%)
  starting transfers between devices  7.3 us (15%)
  local copies, waits for them, and re-layouts  3.34 us (7%)
  between operations  0.71 us (1%)
    ppermute x3, waiting for transfers between devices, on_device(): lax.ppermute(held, 'sub', [(i, i ^ bit) for i in range(spans)])  13.1 us
    pallas_call x1, Pallas kernels, on_device(): call(fine, (shape((1, nv + 8, cy), F32), shape(rows, F32)), [pltpu.VMEM(r...  8.51 us
    pallas_call x1, Pallas kernels, on_device(): call(level, result, [pltpu.VMEM((spans,) + pack.shape[1:], F32)], 'level')  5.84 us
    ppermute x1, waiting for transfers between devices, on_device(): sub_b = lax.ppermute(sub_b, 'sub', pairs(spans, 1))  3.63 us
    unnamed x7, local copies, waits for them, and re-layouts  3.34 us
    ppermute x1, waiting for transfers between devices, on_device(): sec_b = lax.ppermute(sec_b, 'sec', pairs(sects, 1))  2.68 us
    ppermute x1, starting transfers between devices, on_device(): sec_b = lax.ppermute(sec_b, 'sec', pairs(sects, 1))  2.53 us
    ppermute x1, starting transfers between devices, on_device(): sub_b = lax.ppermute(sub_b, 'sub', pairs(spans, 1))  2.29 us
  transfers between devices with their start and end apart: 7, of which 6 were waited for; matrix products, arithmetic and copies ran while one was open for 2% of the time, Pallas kernels for 0%

profile of v2, /device:TPU:26, one launch (start us, length us, event | category | flops | bytes accessed | tf_op | source)
XLA Modules:
  0.0 47.1 jit_solution(4057190164320915690)
XLA Ops:
  0.0 0.0 copy-start
  0.0 1.1 %copy-done = bf16[32,3,32,128]{3,2,1,0:T(8,128)(2,1)S(1)} copy-done((bf16[32,3,32,128]{3,2,1,0:T(8,128)(2,1)S(1)}, bf16[32,3,32,128]{3,2,1,0:T(8,128)(2,1)}, u32[]{:S(2)}) %copy-start) | copy-done | bytes 786456
  1.1 0.0 copy-start.1
  1.1 0.7 %copy-done.1 = bf16[3,32,128]{2,1,0:T(8,128)(2,1)S(1)} copy-done((bf16[3,32,128]{2,1,0:T(8,128)(2,1)S(1)}, bf16[3,32,128]{2,1,0:T(8,128)(2,1)}, u32[]{:S(2)}) %copy-start.1) | copy-done | bytes 24600
  1.9 0.0 copy-start.2
  1.9 0.7 %copy-done.2 = bf16[32,128]{1,0:T(8,128)(2,1)S(1)} copy-done((bf16[32,128]{1,0:T(8,128)(2,1)S(1)}, bf16[32,128]{1,0:T(8,128)(2,1)}, u32[]{:S(2)}) %copy-start.2) | copy-done | bytes 8216
  2.6 1.5 %pack.1 = (bf16[10,3,128,128]{3,2,1,0:T(8,128)(2,1)S(1)}, bf16[128,128]{1,0:T(8,128)(2,1)S(1)}, bf16[128,128]{1,0:T(8,128)(2,1)S(1)}, bf16[128,128]{1,0:T(8,128)(2,1)S(1)}) custom-call(bf16[32,3,32,128]{3,2,1,0:T(8,128)(2,1)S(1)} %copy-done, bf16[3,32,128]{2,1,0:T(8,128)(2,1)S(1)} %copy-done.1, bf16[32,128]{1,0:T(8,128)(2,1)S(1)} %copy-done.2), custom_call_target="tpu_custom_call" | custom-call | tf_op jit(solution)/shard_map/pack/pallas_call | solution.py:446
  4.1 0.1 collective-permute-start
  4.2 2.5 %collective-permute-start.1 = (bf16[128,128]{1,0:T(8,128)(2,1)S(1)}, bf16[128,128]{1,0:T(8,128)(2,1)S(1)}, u32[]{:S(2)}, u32[]{:S(2)}) collective-permute-start(bf16[128,128]{1,0:T(8,128)(2,1)S(1)} %get-tuple-element.16), channel_id=1, source_target_pairs={{1,2},{2,1},{5,6},{6,5},{9,10},{10,9},{13,14},{14,13},{17,18},{18,... | collective-permute-start | bytes 98312 | tf_op jit(solution)/shard_map/ppermute | solution.py:461
  6.7 0.0 collective-permute-done.sec_a.refs_4_
  6.7 2.7 %collective-permute-done.1.sec_b.refs_5_ = bf16[128,128]{1,0:T(8,128)(2,1)S(1)} collective-permute-done((bf16[128,128]{1,0:T(8,128)(2,1)S(1)}, bf16[128,128]{1,0:T(8,128)(2,1)S(1)}, u32[]{:S(2)}, u32[]{:S(2)}) %collective-permute-start.1) | collective-permute-done | bytes 32800 | tf_op jit(solution)/shard_map/ppermute | solution.py:461
  9.4 1.6 %collective-permute-start.2 = (bf16[544,128]{1,0:T(8,128)(2,1)S(1)}, bf16[544,128]{1,0:T(8,128)(2,1)S(1)}, u32[]{:S(2)}, u32[]{:S(2)}) collective-permute-start(bf16[544,128]{1,0:T(8,128)(2,1)S(1)} %get-tuple-element.17), channel_id=1, source_target_pairs={{0,4},{4,0},{8,12},{12,8},{16,20},{20,16},{24,28},{28,24},{1,5},{5... | collective-permute-start | bytes 417800 | tf_op jit(solution)/shard_map/ppermute | solution.py:464
  11.0 2.3 %collective-permute-start.3 = (bf16[544,128]{1,0:T(8,128)(2,1)S(1)}, bf16[544,128]{1,0:T(8,128)(2,1)S(1)}, u32[]{:S(2)}, u32[]{:S(2)}) collective-permute-start(bf16[544,128]{1,0:T(8,128)(2,1)S(1)} %get-tuple-element.18), channel_id=1, source_target_pairs={{4,8},{8,4},{12,16},{16,12},{20,24},{24,20},{5,9},{9,5},{13,17},{1... | collective-permute-start | bytes 417800 | tf_op jit(solution)/shard_map/ppermute | solution.py:465
  14.0 0.8 %copy.6.refs_1_ = f32[32,16]{1,0:T(8,128)S(1)} copy(f32[32,16]{0,1:T(8,128)} %param.9) | data formatting | bytes 4096 | tf_op args[4]
  14.7 0.5 %collective-permute-done.2.refs_6_ = bf16[544,128]{1,0:T(8,128)(2,1)S(1)} collective-permute-done((bf16[544,128]{1,0:T(8,128)(2,1)S(1)}, bf16[544,128]{1,0:T(8,128)(2,1)S(1)}, u32[]{:S(2)}, u32[]{:S(2)}) %collective-permute-start.2) | collective-permute-done | bytes 139296 | tf_op jit(solution)/shard_map/ppermute | solution.py:464
  15.2 3.6 %collective-permute-done.3.refs_7_ = bf16[544,128]{1,0:T(8,128)(2,1)S(1)} collective-permute-done((bf16[544,128]{1,0:T(8,128)(2,1)S(1)}, bf16[544,128]{1,0:T(8,128)(2,1)S(1)}, u32[]{:S(2)}, u32[]{:S(2)}) %collective-permute-start.3) | collective-permute-done | bytes 139296 | tf_op jit(solution)/shard_map/ppermute | solution.py:465
  18.8 8.5 %fine.1 = (f32[1,40,128]{2,1,0:T(8,128)S(1)}, f32[12,3,144,128]{3,2,1,0:T(8,128)S(1)}) custom-call(s32[1,1]{1,0:T(1,128)S(6)} %copy.7.refs_0_, f32[32,16]{1,0:T(8,128)S(1)} %copy.6.refs_1_, bf16[10,3,128,128]{3,2,1,0:T(8,128)(2,1)S(1)} %get-tuple-element.13.own_ref.refs_2_, bf16[128,128]{1,0:T(8,128)(2,1)S(1)} %get-tuple-element.14.kt_ref.refs_3_, ...), custom_call_target="tpu_custom_call" | custom-call | tf_op jit(solution)/shard_map/fine/pallas_call | solution.py:472
  27.4 0.0 collective-permute-start.4
  27.4 3.8 %collective-permute-done.4.refs_1_ = f32[1,40,128]{2,1,0:T(8,128)S(1)} collective-permute-done((f32[1,40,128]{2,1,0:T(8,128)S(1)}, f32[1,40,128]{2,1,0:T(8,128)S(1)}, u32[]{:S(2)}, u32[]{:S(2)}) %collective-permute-start.4) | collective-permute-done | bytes 20512 | tf_op jit(solution)/shard_map/ppermute | solution.py:499
  31.2 0.5 collective-permute-start.5
  31.6 3.6 %collective-permute-done.5.refs_2_ = f32[2,40,128]{2,1,0:T(8,128)S(1)} collective-permute-done((f32[2,40,128]{2,1,0:T(8,128)S(1)}, f32[2,40,128]{2,1,0:T(8,128)S(1)}, u32[]{:S(2)}, u32[]{:S(2)}) %collective-permute-start.5) | collective-permute-done | bytes 40992 | tf_op jit(solution)/shard_map/ppermute | solution.py:499
  35.2 0.3 collective-permute-start.6
  35.5 5.8 %collective-permute-done.6.refs_3_ = f32[4,40,128]{2,1,0:T(8,128)S(1)} collective-permute-done((f32[4,40,128]{2,1,0:T(8,128)S(1)}, f32[4,40,128]{2,1,0:T(8,128)S(1)}, u32[]{:S(2)}, u32[]{:S(2)}) %collective-permute-start.6) | collective-permute-done | bytes 81952 | tf_op jit(solution)/shard_map/ppermute | solution.py:499
  41.3 5.8 %level.1 = f32[16,3,32,128]{3,2,1,0:T(8,128)} custom-call(f32[1,40,128]{2,1,0:T(8,128)S(1)} %get-tuple-element.19.refs_0_, f32[1,40,128]{2,1,0:T(8,128)S(1)} %collective-permute-done.4.refs_1_, f32[2,40,128]{2,1,0:T(8,128)S(1)} %collective-permute-done.5.refs_2_, f32[4,40,128]{2,1,0:T(8,128)S(1)} %collective-permute-done.6.refs_3_, ...), custom_call_target="tpu_custom_call" | custom-call | tf_op jit(solution)/shard_map/level/pallas_call | solution.py:505
  (3 shorter events, 0.0 us)
Async XLA Ops:
  0.0 1.1 %copy-start = (bf16[32,3,32,128]{3,2,1,0:T(8,128)(2,1)S(1)}, bf16[32,3,32,128]{3,2,1,0:T(8,128)(2,1)}, u32[]{:S(2)}) copy-start(bf16[32,3,32,128]{3,2,1,0:T(8,128)(2,1)} %v_hbm.1) | copy-start | bytes 2359300
  1.1 0.7 %copy-start.1 = (bf16[3,32,128]{2,1,0:T(8,128)(2,1)S(1)}, bf16[3,32,128]{2,1,0:T(8,128)(2,1)}, u32[]{:S(2)}) copy-start(bf16[3,32,128]{2,1,0:T(8,128)(2,1)} %k_hbm.1) | copy-start | bytes 73732
  1.9 0.7 %copy-start.2 = (bf16[32,128]{1,0:T(8,128)(2,1)S(1)}, bf16[32,128]{1,0:T(8,128)(2,1)}, u32[]{:S(2)}) copy-start(bf16[32,128]{1,0:T(8,128)(2,1)} %g_hbm.1) | copy-start | bytes 24580
  4.1 2.6 %collective-permute-start = (bf16[128,128]{1,0:T(8,128)(2,1)S(1)}, bf16[128,128]{1,0:T(8,128)(2,1)S(1)}, u32[]{:S(2)}, u32[]{:S(2)}) collective-permute-start(bf16[128,128]{1,0:T(8,128)(2,1)S(1)} %get-tuple-element.15), channel_id=1, source_target_pairs={{0,1},{1,0},{2,3},{3,2},{4,5},{5,4},{6,7},{7,6},{8,9},{9,8},{10,11... | collective-permute-start | bytes 98312 | tf_op jit(solution)/shard_map/ppermute | solution.py:460
  4.2 5.2 %collective-permute-start.1 = (bf16[128,128]{1,0:T(8,128)(2,1)S(1)}, bf16[128,128]{1,0:T(8,128)(2,1)S(1)}, u32[]{:S(2)}, u32[]{:S(2)}) collective-permute-start(bf16[128,128]{1,0:T(8,128)(2,1)S(1)} %get-tuple-element.16), channel_id=1, source_target_pairs={{1,2},{2,1},{5,6},{6,5},{9,10},{10,9},{13,14},{14,13},{17,18},{18,... | collective-permute-start | bytes 98312 | tf_op jit(solution)/shard_map/ppermute | solution.py:461
  9.4 5.8 %collective-permute-start.2 = (bf16[544,128]{1,0:T(8,128)(2,1)S(1)}, bf16[544,128]{1,0:T(8,128)(2,1)S(1)}, u32[]{:S(2)}, u32[]{:S(2)}) collective-permute-start(bf16[544,128]{1,0:T(8,128)(2,1)S(1)} %get-tuple-element.17), channel_id=1, source_target_pairs={{0,4},{4,0},{8,12},{12,8},{16,20},{20,16},{24,28},{28,24},{1,5},{5... | collective-permute-start | bytes 417800 | tf_op jit(solution)/shard_map/ppermute | solution.py:464
  11.0 7.8 %collective-permute-start.3 = (bf16[544,128]{1,0:T(8,128)(2,1)S(1)}, bf16[544,128]{1,0:T(8,128)(2,1)S(1)}, u32[]{:S(2)}, u32[]{:S(2)}) collective-permute-start(bf16[544,128]{1,0:T(8,128)(2,1)S(1)} %get-tuple-element.18), channel_id=1, source_target_pairs={{4,8},{8,4},{12,16},{16,12},{20,24},{24,20},{5,9},{9,5},{13,17},{1... | collective-permute-start | bytes 417800 | tf_op jit(solution)/shard_map/ppermute | solution.py:465
  27.4 3.8 %collective-permute-start.4 = (f32[1,40,128]{2,1,0:T(8,128)S(1)}, f32[1,40,128]{2,1,0:T(8,128)S(1)}, u32[]{:S(2)}, u32[]{:S(2)}) collective-permute-start(f32[1,40,128]{2,1,0:T(8,128)S(1)} %get-tuple-element.19.refs_0_), channel_id=1, source_target_pairs={{0,4},{4,0},{8,12},{12,8},{16,20},{20,16},{24,28},{28,24},{1,5},{5... | collective-permute-start | bytes 61448 | tf_op jit(solution)/shard_map/ppermute | solution.py:499
  31.2 4.0 %collective-permute-start.5 = (f32[2,40,128]{2,1,0:T(8,128)S(1)}, f32[2,40,128]{2,1,0:T(8,128)S(1)}, u32[]{:S(2)}, u32[]{:S(2)}) collective-permute-start(f32[2,40,128]{2,1,0:T(8,128)S(1)} %pad_maximum_fusion.1), channel_id=1, source_target_pairs={{0,8},{4,12},{8,0},{12,4},{16,24},{20,28},{24,16},{28,20},{1,9},{5... | collective-permute-start | bytes 122888 | tf_op jit(solution)/shard_map/ppermute | solution.py:499
  35.2 6.1 %collective-permute-start.6 = (f32[4,40,128]{2,1,0:T(8,128)S(1)}, f32[4,40,128]{2,1,0:T(8,128)S(1)}, u32[]{:S(2)}, u32[]{:S(2)}) collective-permute-start(f32[4,40,128]{2,1,0:T(8,128)S(1)} %pad_maximum_fusion), channel_id=1, source_target_pairs={{0,16},{4,20},{8,24},{12,28},{16,0},{20,4},{24,8},{28,12},{1,17},{... | collective-permute-start | bytes 245768 | tf_op jit(solution)/shard_map/ppermute | solution.py:499

commit v3 on v2

v3 whole, which is shorter than its diff:
```python
import math

import jax
import jax.numpy as jnp
from jax import lax
from jax.experimental import pallas as pl
from jax.experimental.pallas import tpu as pltpu
from jax.sharding import PartitionSpec as P

H = 4
MIB = 1 << 20
VMEM_MIB = 24
F32 = jnp.float32
BF16 = jnp.bfloat16
NN = (((1,), (0,)), ((), ()))
NT = (((1,), (1,)), ((), ()))
TN = (((0,), (0,)), ((), ()))


def iota(shape, dim):
    return lax.broadcasted_iota(jnp.int32, shape, dim)


def split(x):
    high = x.astype(BF16)
    return high, (x - high.astype(F32)).astype(BF16)


def dot(a, b, dims):
    return lax.dot_general(a, b, dims, preferred_element_type=F32)


def dot3(a, b, dims):
    (ah, al), (bh, bl) = split(a), split(b)
    return dot(ah, bh, dims) + (dot(ah, bl, dims) + dot(al, bh, dims))


def inverse_factor(gram, size, step=4):
    row, lane = iota((size, 128), 0), iota((size, 128), 1)
    work = jnp.where(lane < size, gram, jnp.where(lane == row + size, 1.0, 0.0))
    for first in range(0, size, step):
        columns = [jnp.broadcast_to(work[:, j : j + 1], (size, 128)) for j in range(first, first + step)]
        update = None
        for i, j in enumerate(range(first, min(first + step, size - 1))):
            factor = jnp.where(row > j, columns[i] / columns[i][j : j + 1, :], 0.0)
            for later in range(i + 1, step):
                columns[later] = columns[later] - factor * columns[later][j : j + 1, :]
            pivot = work[j : j + 1, :]
            if update is not None:
                pivot = pivot - update[j : j + 1, :]
            update = factor * pivot if update is None else update + factor * pivot
        work = work - update
    diag = jnp.sum(jnp.where(lane == row, work, 0.0), axis=1, keepdims=True)
    return pltpu.roll(work / jnp.sqrt(diag), 128 - size, 1)


def slots_of(cx):
    own = cx // H
    return own, own, own + 1, own + 2, own + 3


def halves(octet_a, octet_b):
    return jnp.where(iota(octet_a.shape, 0) < H, octet_a, octet_b)


def swap(octet):
    return pltpu.roll(octet, H, 0)


def pack_kernel(
    v_hbm, k_hbm, g_hbm, start_hbm, own_ref, kt_ref, sec_a, sec_b, start_ref, v_buf, k_buf, g_buf, vf, kf, sems
):
    comps, nv, cx, cy = v_buf.shape
    copies = [pltpu.make_async_copy(v_hbm.at[:, c], v_buf.at[c], sems.at[c]) for c in range(comps)]
    copies.append(pltpu.make_async_copy(k_hbm, k_buf, sems.at[comps]))
    copies.append(pltpu.make_async_copy(g_hbm, g_buf, sems.at[comps + 1]))
    copies.append(pltpu.make_async_copy(start_hbm, start_ref, sems.at[comps + 2]))
    for copy in copies:
        copy.start()
    sec_even = lax.rem(lax.axis_index("sec"), 2) == 0
    own = cx // H
    pieces = (own + 2) * comps + 1
    firsts, lasts = [None] * pieces, [None] * pieces
    for c in range(comps):
        copies[c].wait()
        vf[c] = v_buf[c].astype(F32).reshape(nv * cx, cy)
        for p in range(own + 2):
            rows = [b * own + p for b in range(H)] if p < own else [b + (p - own) * (cx - H) for b in range(H)]
            stack = [vf[c, pl.ds(x, nv, stride=cx), :] for x in rows]
            turned = jnp.concatenate(stack, axis=0).T
            own_ref[p, c] = turned.astype(BF16)
            firsts[p * comps + c], lasts[p * comps + c] = turned[:8], turned[cy - 8 :]
    for copy in copies[comps:]:
        copy.wait()
    kf[: comps * cx] = k_buf[...].astype(F32).reshape(comps * cx, cy)
    kf[comps * cx :] = g_buf[...].astype(F32)
    turned = kf[...].T
    kt_ref[...] = turned.astype(BF16)
    firsts[-1], lasts[-1] = turned[:8], turned[cy - 8 :]
    for octets in (firsts, lasts):
        if len(octets) % 2:
            octets.append(jnp.zeros((8, cy), F32))
    pairs_of = range(0, len(firsts), 2)
    left = [halves(firsts[q], swap(firsts[q + 1])) for q in pairs_of]
    right = [halves(swap(lasts[q]), lasts[q + 1]) for q in pairs_of]
    left, right = jnp.concatenate(left, axis=0), jnp.concatenate(right, axis=0)
    sec_a[...] = jnp.where(sec_even, right, left).astype(BF16)
    sec_b[...] = jnp.where(sec_even, left, right).astype(BF16)


def margin_octets(sec_a, sec_b, sec_even, count):
    a, b = sec_a[...].astype(F32), sec_b[...].astype(F32)
    hi, lo = jnp.where(sec_even, a, b), jnp.where(sec_even, b, a)
    out = []
    for q in range(count):
        at = slice(8 * (q // 2), 8 * (q // 2) + 8)
        out.append(halves(swap(hi[at]), lo[at]) if q % 2 else halves(hi[at], swap(lo[at])))
    return out


def edge_kernel(own_ref, kt_ref, sec_a, sec_b, sub_a, sub_b):
    slots, comps, cy, lanes = own_ref.shape
    sub_even = lax.rem(lax.axis_index("sub"), 2) == 0
    sec_even = lax.rem(lax.axis_index("sec"), 2) == 0
    octets = margin_octets(sec_a, sec_b, sec_even, slots * comps + 1)
    first, last = slots - 2, slots - 1
    head = octets[first * comps : first * comps + comps] + octets[-1:]
    tail = octets[last * comps : last * comps + comps] + octets[-1:]
    head, tail = jnp.concatenate(head, axis=0), jnp.concatenate(tail, axis=0)
    for ref, to_next in ((sub_a, sub_even), (sub_b, jnp.logical_not(sub_even))):
        slot = jnp.where(to_next, last, first)
        for c in range(comps):
            ref[c * cy : (c + 1) * cy] = own_ref[slot, c]
        ref[comps * cy : (comps + 1) * cy] = kt_ref[...]
        ref[(comps + 1) * cy :] = jnp.where(to_next, tail, head).astype(BF16)


def spread(table, wanted, kinds, cx):
    lanes = table.shape[1]
    source = iota((lanes, lanes), 0)
    pick = [jnp.where(source == kind * cx + wanted, 1.0, 0.0).astype(BF16) for kind in range(kinds)]
    out = dot(table, jnp.concatenate(pick, axis=1), NN)
    return [out[:, kind * lanes : (kind + 1) * lanes] for kind in range(kinds)]


def terms_of(rows):
    return [4.0 + k - rows[-1] for k in rows[:-1]] + [rows[-1]]


def row_of_slot(p, own, cx, block):
    return block * own + p if p < own else block + (p - own) * (cx - H)


def prep_kernel(own_ref, kt_ref, v0, coef):
    slots, comps, cy, lanes = own_ref.shape
    own, kinds = slots - 2, comps + 1
    cx = kt_ref.shape[1] // kinds
    head = slots_of(cx)[3]
    block = iota((lanes, lanes), 1) // (lanes // H)
    for p in range(slots):
        slot = p if p < own else head + p - own
        for c in range(comps):
            v0[slot, c, 8 : 8 + cy, :] = own_ref[p, c].astype(F32)
        values = spread(kt_ref[...], row_of_slot(p, own, cx, block), kinds, cx)
        for kind, value in enumerate(terms_of(values)):
            coef[slot, kind, :cy, :] = value


def fine_kernel(sizes, rank_ref, start_ref, v0_in, coef_in, kt_ref, sec_a, sec_b, sub_a, sub_b, pack_ref, high2, low2, v0, coef, x1, x2, high3, low3, margin3):
    spans, sects = sizes
    _, comps, cy, lanes = high2.shape
    nv = start_ref.shape[1]
    cx = kt_ref.shape[1] // (comps + 1)
    OWN, BEFORE, AFTER, HEAD, TAIL = slots_of(cx)
    s, t = lax.axis_index("sub"), lax.axis_index("sec")
    sub_even, sec_even = lax.rem(s, 2) == 0, lax.rem(t, 2) == 0
    kinds = comps + 1
    low, top = slice(0, 8), slice(8 + cy, 16 + cy)
    mid = slice(8, 8 + cy)
    octets = margin_octets(sec_a, sec_b, sec_even, (OWN + 2) * comps + 1)

    def put_octet(slot, c, octet):
        v0[slot, c, low, :] = octet
        v0[slot, c, top, :] = octet

    def received(first, count):
        a, b = sub_a[first : first + count].astype(F32), sub_b[first : first + count].astype(F32)
        return jnp.where(sub_even, a, b), jnp.where(sub_even, b, a)

    for c in range(comps):
        for p in range(OWN + 2):
            put_octet(p if p < OWN else HEAD + p - OWN, c, octets[p * comps + c])
        v0[AFTER, c, mid, :], v0[BEFORE, c, mid, :] = received(c * cy, cy)
        after_octet, before_octet = received(kinds * cy + 8 * c, 8)
        put_octet(BEFORE, c, before_octet)
        put_octet(AFTER, c, after_octet)

    octet_row = iota((8, lanes), 0)
    col_in = jnp.where(octet_row < H, jnp.where(t < sects - 1, 1.0, 0.0), jnp.where(t > 0, 1.0, 0.0))
    has_before, has_after = jnp.where(s > 0, 1.0, 0.0), jnp.where(s < spans - 1, 1.0, 0.0)
    row_in = {BEFORE: has_before, AFTER: has_after}
    octet_block = iota((8, lanes), 1) // nv
    for p in range(OWN + 2):
        slot = p if p < OWN else HEAD + p - OWN
        wanted = row_of_slot(p, OWN, cx, octet_block)
        rows = [jnp.take_along_axis(octets[-1], wanted + kind * cx, axis=1) for kind in range(kinds)]
        for kind, value in enumerate(terms_of(rows)):
            coef[slot, kind, cy : cy + 8, :] = value * col_in
    after, before = received(comps * cy, cy)
    after_octet, before_octet = received(kinds * cy + 8 * comps, 8)
    block = iota((lanes, lanes), 1) // nv
    for slot, rows, octet, p in ((AFTER, after, after_octet, OWN), (BEFORE, before, before_octet, OWN + 1)):
        table = jnp.concatenate([rows, octet, jnp.zeros_like(octet)], axis=0).astype(BF16)
        values = spread(table, row_of_slot(p, OWN, cx, block), kinds, cx)
        for kind, value in enumerate(terms_of(values)):
            coef[slot, kind, :cy, :] = value[:cy] * row_in[slot]
            coef[slot, kind, cy : cy + 8, :] = value[cy : cy + 8] * (col_in * row_in[slot])

    def operator(src, rows, first_row, length, shifted, strips, emit):
        lane = iota((length, lanes), 1)
        in_first, in_last = lane < nv, lane >= lanes - nv
        masked = shifted is not None

        def at(slot, c):
            return src[slot, c, rows(0), :]

        def up_of(slot, c):
            if 0 < slot < OWN:
                return at(slot - 1, c)
            if slot in (0, AFTER):
                return pltpu.roll(jnp.where(in_last, at(BEFORE if slot == 0 else OWN - 1, c), at(OWN - 1 if slot == 0 else AFTER, c)), nv, 1)
            if slot == HEAD:
                return pltpu.roll(jnp.where(in_last, at(BEFORE, c), at(HEAD, c)), nv, 1)
            return jnp.where(in_first, 0.0, pltpu.roll(at(slot, c), nv, 1))

        def down_of(slot, c):
            if slot < OWN - 1:
                return at(slot + 1, c)
            if slot in (OWN - 1, BEFORE):
                return pltpu.roll(jnp.where(in_first, at(AFTER if slot == OWN - 1 else 0, c), at(0 if slot == OWN - 1 else BEFORE, c)), lanes - nv, 1)
            if slot == TAIL:
                return pltpu.roll(jnp.where(in_first, at(AFTER, c), at(TAIL, c)), lanes - nv, 1)
            return jnp.where(in_last, 0.0, pltpu.roll(at(slot, c), lanes - nv, 1))

        for slot in range(TAIL + 1 if strips else AFTER + 1):
            v = [at(slot, c) for c in range(comps)]
            weight = [coef[slot, kind, first_row, :] for kind in range(kinds)]
            total = weight[comps] * (v[0] + v[1] + v[2])
            for c in range(comps):
                if masked:
                    sides = shifted(slot, c)
                else:
                    sides = src[slot, c, rows(-1), :] + src[slot, c, rows(1), :]
                beside = sides + (up_of(slot, c) + down_of(slot, c))
                inside = row_in.get(slot)
                if masked:
                    beside = beside * (col_in if inside is None else col_in * inside)
                elif inside is not None:
                    beside = beside * inside
                emit(slot, c, weight[c] * v[c] + total - beside)

    def apply(src, strips, emit_rows, emit_margin):
        def body(j, carry):
            base = 16 * j

            def rows(d):
                start = 8 + base + d
                return pl.ds(pl.multiple_of(start, 8) if d == 0 else start, 16)

            def emit(slot, c, value):
                emit_rows(slot, c, pl.multiple_of(base, 16), value)

            operator(src, rows, pl.ds(pl.multiple_of(base, 16), 16), 16, None, strips, emit)
            return carry

        lax.fori_loop(0, cy // 16, body, 0)

        def shifted(slot, c):
            left = jnp.where(octet_row == H, 0.0, src[slot, c, 7 + cy : 15 + cy, :])
            return left + jnp.where(octet_row == H - 1, 0.0, src[slot, c, 1:9, :])

        operator(src, lambda d: top, slice(cy, cy + 8), 8, shifted, strips, emit_margin)

    def store(dst, split_too=False):
        def emit_rows(slot, c, base, value):
            dst[slot, c, pl.ds(base + 8, 16), :] = value
            if split_too and slot < HEAD:
                high2[slot, c, pl.ds(base, 16), :], low2[slot, c, pl.ds(base, 16), :] = split(value)

        def emit_margin(slot, c, value):
            dst[slot, c, low, :] = value
            dst[slot, c, top, :] = value

        return emit_rows, emit_margin

    apply(v0, True, *store(x1))
    apply(x1, True, *store(x2, True))

    def split_rows(slot, c, base, value):
        high3[slot, c, pl.ds(base, 16), :], low3[slot, c, pl.ds(base, 16), :] = split(value)

    def keep_margin(slot, c, value):
        margin3[slot, c] = value

    def fold(z):
        return sum(pltpu.roll(z[b * nv : (b + 1) * nv], (z.shape[1] - b * nv) % z.shape[1], 1) if b else z[:nv] for b in range(H))

    def flat(ref, first, count):
        return ref[first : first + count].reshape(count * comps * cy, lanes)

    chunks = range(0, AFTER + 1, 2)
    octet_margins = [x2[slot, c, top, :] for slot in range(AFTER + 1) for c in range(comps)]
    margin_h2, margin_l2 = split(jnp.concatenate(octet_margins, axis=0))

    def gram_m():
        def part(h2, l2):
            return dot(h2, jnp.concatenate([h2, l2], axis=1), TN)
        main = part(margin_h2, margin_l2)
        for first in chunks:
            main = main + part(flat(high2, first, 2), flat(low2, first, 2))
        main = fold(main)
        mixed = main[:, lanes : lanes + nv]
        return main[:, :nv] + (mixed + mixed.T)

    def gram_n():
        def part(h2, l2, h3, l3):
            return dot(h2, jnp.concatenate([h3, l3], axis=1), TN), dot(l2, h3, TN)
        h3, l3 = split(margin3[...].reshape((AFTER + 1) * comps * 8, lanes))
        main, cross = part(margin_h2, margin_l2, h3, l3)
        for first in chunks:
            more = part(*(flat(ref, first, 2) for ref in (high2, low2, high3, low3)))
            main, cross = main + more[0], cross + more[1]
        main = fold(main)
        return main[:, :nv] + main[:, lanes : lanes + nv] + fold(cross)[:, :nv]

    gram = gram_m()
    apply(x2, False, split_rows, keep_margin)
    pad = jnp.zeros((nv, lanes - nv), F32)
    inverse = inverse_factor(jnp.concatenate([gram, pad], axis=1), nv)[:, :nv]
    inverse = jnp.where(iota((nv, nv), 0) < rank_ref[0, 0], inverse, 0.0)
    image = gram_n()

    def rim(strip, first, block, own_first):
        own, other = [], []
        for at, weight_at in ((mid, slice(0, cy)), (top, slice(cy, cy + 8))):
            for c in range(comps):
                held = [x2[first + i, c, at, block * nv : (block + 1) * nv] for i in range(H)]
                weight = coef[strip, c, weight_at, :] + coef[strip, comps, weight_at, :]
                own.append(jnp.concatenate(held, axis=1) * weight)
                other.append(x2[strip, c, at, :])
        own.append(jnp.zeros((8, lanes), F32))
        other.append(jnp.zeros((8, lanes), F32))
        own, other = jnp.concatenate(own, axis=0), jnp.concatenate(other, axis=0)
        a, b = (own, other) if own_first else (other, own)
        return fold(dot3(a, b, TN))[:, :nv]

    rim_next = rim(TAIL, OWN - H, H - 1, True) * has_after
    rim_prev = rim(HEAD, 0, 0, True) * has_before

    start = start_ref[...]
    k2 = start.shape[0]
    products = dot3(jnp.concatenate([inverse.T, start], axis=0), inverse, NN)
    pack_ref[0, :nv] = jnp.concatenate([rim_prev, 0.5 * image, rim_next, products[:nv]], axis=1)
    starts = [products[nv + i : nv + i + 8] for i in range(0, k2, 8)]
    pad = jnp.zeros((8, lanes - nv * len(starts)), F32)
    pack_ref[0, nv:] = jnp.concatenate(starts + [pad], axis=1)


def prolong(coefs, high_ref, low_ref, out_ref, buf, sems):
    k2, nv = coefs.shape
    comps, cx = buf.shape[0], buf.shape[2]
    cy = buf.shape[3]
    own = cx // H
    tiled = jnp.concatenate([coefs] * H, axis=1)
    tiled = jnp.broadcast_to(tiled[:, None, :], (k2, 8, H * nv)).reshape(8 * k2, H * nv)
    same = lax.rem(iota(tiled.shape, 0), 8) == iota(tiled.shape, 1) // nv
    high, low = split(jnp.where(same, tiled, 0.0))
    left = jnp.concatenate([high, low, high], axis=1)
    copies = []
    for c in range(comps):
        for p in range(own):
            bh, bl = high_ref[p, c], low_ref[p, c]
            out = dot(left, jnp.concatenate([bh, bh, bl], axis=1), NT).reshape(k2, 8, cy)
            buf[c, :, pl.ds(p, H, stride=own), :] = out[:, :H]
        copies.append(pltpu.make_async_copy(buf.at[c], out_ref.at[:, c], sems.at[c]))
        copies[-1].start()
    for copy in copies:
        copy.wait()


def level_kernel(spans, order, factor, *refs):
    parts, (high_ref, low_ref, out_ref, packs, buf, sems) = refs[:-6], refs[-6:]
    k2 = buf.shape[1]
    nv = packs.shape[1] - 8
    n = spans * nv
    s = lax.axis_index("sub")
    index = 0
    for part in parts:
        for i in range(part.shape[0]):
            packs[order[index]] = part[i]
            index += 1
    lane = iota((nv, 128), 1)

    def placed(block, offset, first, last):
        rolled = pltpu.roll(block, offset % 128, 1) if offset % 128 else block
        at = iota(block.shape, 1) - offset
        tiles = [jnp.where((at + m >= first) & (at + m < last), rolled, 0.0) for m in range(0, n, 128)]
        return jnp.concatenate(tiles, axis=1)

    rows, products = [], []
    u = jnp.zeros((k2, n), F32)
    for b in range(spans):
        pack = packs[jnp.bitwise_xor(s, b)]
        rows.append(placed(pack[:nv], nv * (b - 1), 0, 3 * nv))
        products.append(placed(pack[:nv], nv * (b - 3), 3 * nv, 4 * nv))
        starts = [placed(pack[nv:], nv * (b - i), nv * i, nv * i + nv) for i in range(k2 // 8)]
        u = u + jnp.concatenate(starts, axis=0)
    rows = jnp.concatenate(rows, axis=0)
    full = split(rows + rows.T)
    products = split(jnp.concatenate(products, axis=0))

    def times(x, halves):
        xh, xl = split(x)
        out = dot(jnp.concatenate([xh, xl], axis=0), halves[0], NN)
        return out[:k2] + (out[k2:] + dot(xh, halves[1], NN))

    z = times(times(times(u, full), products), full)
    w = times(z, products)
    gram = dot3(w, z, NT)
    gram = jnp.concatenate([gram, jnp.zeros((k2, 128 - k2), F32)], axis=1)
    own = pltpu.roll(w, lax.rem(n - nv * s, n), 1)[:, :nv]
    coefs = dot3(inverse_factor(gram, k2)[:, :k2], factor * own, NN)
    prolong(coefs, high_ref, low_ref, out_ref, buf, sems)


def pairs(count, offset):
    return [q for i in range(offset, count - 1, 2) for q in ((i, i + 1), (i + 1, i))]


def from_behind(block, axis, distance):
    devices = range(lax.axis_size(axis))
    return lax.ppermute(block, axis, [(i - distance, i) for i in devices if i - distance in devices])


def level_coefs(pack, nv, k2, factor):
    highest = lax.Precision.HIGHEST
    rim_prev, half, rim_next, product = (pack[:nv, nv * i : nv * i + nv] for i in range(4))
    u = jnp.concatenate([pack[nv:, nv * i : nv * i + nv] for i in range(k2 // 8)], axis=0).T
    own = half + half.T
    rim = rim_next + from_behind(rim_prev, "sub", -1).T
    rim_before = from_behind(rim, "sub", 1)
    for step in range(2):
        z = jnp.dot(own, u, precision=highest)
        z = z + jnp.dot(rim, from_behind(u, "sub", -1), precision=highest)
        z = z + jnp.dot(rim_before.T, from_behind(u, "sub", 1), precision=highest)
        u = jnp.dot(product, z, precision=highest)
    lower = jnp.linalg.cholesky(lax.psum(jnp.dot(z.T, u, precision=highest), "sub"))
    return factor * lax.linalg.triangular_solve(lower, u.T, left_side=True, lower=True)


def in_vmem(x):
    return pltpu.with_memory_space_constraint(x, pltpu.VMEM)


def call(kernel, out_shape, scratch, name, in_specs=None, **more):
    return pl.pallas_call(
        kernel,
        out_shape=out_shape,
        scratch_shapes=scratch,
        compiler_params=pltpu.CompilerParams(vmem_limit_bytes=VMEM_MIB * MIB),
        name=name,
        **({"in_specs": in_specs} if in_specs else {}),
        **more,
    )


def on_device(start_vectors, stiffness, coupling, kept_ranks, level_start):
    spans, sects = lax.axis_size("sub"), lax.axis_size("sec")
    nv, comps, cx, cy = start_vectors.shape
    k2 = level_start.shape[1]
    channels = comps + 1
    slots = slots_of(cx)[-1] + 1
    shape = jax.ShapeDtypeStruct
    vmem = pl.BlockSpec(memory_space=pltpu.VMEM)
    hbm = pl.BlockSpec(memory_space=pltpu.HBM)

    pieces = (cx // H + 2) * comps + 1
    inputs = (start_vectors, stiffness, coupling, level_start.T)
    sec_shape = shape((-(-pieces // 2) * 8, cy), BF16)
    own, kt, sec_a, sec_b, start = call(
        pack_kernel,
        (shape((cx // H + 2, comps, cy, H * nv), BF16), shape((cy, channels * cx), BF16), sec_shape, sec_shape)
        + (shape((k2, nv), F32),),
        [
            pltpu.VMEM((comps, nv, cx, cy), BF16),
            pltpu.VMEM(stiffness.shape, BF16),
            pltpu.VMEM(coupling.shape, BF16),
            pltpu.VMEM((comps, nv * cx, cy), F32),
            pltpu.VMEM((channels * cx, cy), F32),
            pltpu.SemaphoreType.DMA((comps + 3,)),
        ],
        "pack",
        [hbm] * 4,
    )(*(pltpu.with_memory_space_constraint(x, pltpu.HBM) for x in inputs))
    sec_a = lax.ppermute(sec_a, "sec", pairs(sects, 0))
    sec_b = lax.ppermute(sec_b, "sec", pairs(sects, 1))
    sub_shape = shape((channels * (cy + 8), H * nv), BF16)
    sub_a, sub_b = call(edge_kernel, (sub_shape, sub_shape), [], "edge")(own, kt, sec_a, sec_b)
    sub_a = lax.ppermute(sub_a, "sub", pairs(spans, 0))
    sub_b = lax.ppermute(sub_b, "sub", pairs(spans, 1))

    def fine(*refs):
        fine_kernel((spans, sects), *refs)

    rows = shape((slots, comps, cy + 16, H * nv), F32)
    weights = shape((slots, channels, cy + 8, H * nv), F32)
    half = shape((slots - 2, comps, cy, H * nv), BF16)
    v0, coef = (in_vmem(x) for x in call(prep_kernel, (rows, weights), [], "prep")(own, kt))
    pack, high, low, _, _ = call(
        fine,
        (shape((1, nv + 8, cy), F32), half, half, rows, weights),
        [
            pltpu.VMEM(rows.shape, F32),
            pltpu.VMEM(rows.shape, F32),
            pltpu.VMEM(half.shape, BF16),
            pltpu.VMEM(half.shape, BF16),
            pltpu.VMEM((slots - 2, comps, 8, H * nv), F32),
        ],
        "fine",
        [pl.BlockSpec(memory_space=pltpu.SMEM)] + [vmem] * 8,
        input_output_aliases={2: 3, 3: 4},
    )(kept_ranks, start, v0, coef, kt, sec_a, sec_b, sub_a, sub_b)

    factor = math.sqrt(spans * comps * (cx + 2 * H) * (cy + 2 * H))
    result = shape((k2, comps, cx, cy), F32)
    tiles = [pltpu.VMEM((comps, k2, cx, cy), F32), pltpu.SemaphoreType.DMA((comps,))]
    if spans != 8:

        def prolong_kernel(coefs_ref, *refs):
            prolong(coefs_ref[...], *refs)

        coefs = level_coefs(pack[0], nv, k2, factor)
        return call(prolong_kernel, result, tiles, "prolong", [vmem] * 3, out_specs=hbm)(coefs, high, low)

    def swapped(block, bit):
        return lax.ppermute(block, "sub", [(i, i ^ bit) for i in range(spans)])

    far = swapped(pack, 4)
    both = jnp.concatenate([pack, far])
    parts = [both] + [swapped(both, bit) for bit in (2, 1, 3)]
    order = [high_bit ^ bit for bit in (0, 2, 1, 3) for high_bit in (0, 4)]

    def level(*refs):
        level_kernel(spans, order, factor, *refs)

    packs = pltpu.VMEM((spans,) + pack.shape[1:], F32)
    return call(level, result, [packs] + tiles, "level", [vmem] * 6, out_specs=hbm)(*parts, high, low)


def solution(mesh):
    placed = (
        P(None, None, "sub", "sec"),
        P(None, "sub", "sec"),
        P("sub", "sec"),
        P("sub", "sec"),
        P("sub", None),
    )
    return jax.shard_map(
        on_device,
        mesh=mesh,
        in_specs=placed,
        out_specs=P(None, None, "sub", "sec"),
        check_vma=False,
    )
```

time: 47.4 us -> 40.4 us (0.85)
  the two profiles are of different devices: /device:TPU:26 before, /device:TPU:2 now
where the time goes in v3:
time: 40.4 us; the launch traced here: 40.2 us
  starting transfers between devices  14.7 us (36%)
  Pallas kernels  14.1 us (35%)
  waiting for transfers between devices  10.6 us (26%)
  between operations  0.71 us (2%)
    ppermute x4, starting transfers between devices, swapped(): return lax.ppermute(block, 'sub', [(i, i ^ bit) for i in range(spans)])  10.5 us
    pallas_call x1, Pallas kernels, on_device(): call(fine, (shape((1, nv + 8, cy), F32), half, half, rows, weights), [plt...  7.24 us
    ppermute x4, waiting for transfers between devices, swapped(): return lax.ppermute(block, 'sub', [(i, i ^ bit) for i in range(spans)])  5.76 us
    pallas_call x1, Pallas kernels, on_device(): call(level, result, [packs] + tiles, 'level', [vmem] * 6, out_specs=hbm)  3.73 us
    ppermute x1, waiting for transfers between devices, on_device(): sec_b = lax.ppermute(sec_b, 'sec', pairs(sects, 1))  3.29 us
    pallas_call x1, Pallas kernels, on_device(): call(pack_kernel, (shape((cx // H + 2, comps, cy, H * nv), BF16), shape((...  2.52 us
    ppermute x1, starting transfers between devices, on_device(): sec_b = lax.ppermute(sec_b, 'sec', pairs(sects, 1))  1.92 us
    ppermute x1, waiting for transfers between devices, on_device(): sub_a = lax.ppermute(sub_a, 'sub', pairs(spans, 0))  1.59 us
  transfers between devices with their start and end apart: 8, of which 6 were waited for; matrix products, arithmetic and copies ran while one was open for 0% of the time, Pallas kernels for 2%

profile of v3, /device:TPU:2, one launch (start us, length us, event | category | flops | bytes accessed | tf_op | source)
XLA Modules:
  0.0 40.2 jit_solution(16886170073237677667)
XLA Ops:
  0.0 2.5 %pack.1 = (bf16[10,3,128,128]{3,2,1,0:T(8,128)(2,1)S(1)}, bf16[128,128]{1,0:T(8,128)(2,1)S(1)}, bf16[128,128]{1,0:T(8,128)(2,1)S(1)}, bf16[128,128]{1,0:T(8,128)(2,1)S(1)}, f32[16,32]{1,0:T(8,128)S(1)}) custom-call(bf16[32,3,32,128]{3,2,1,0:T(8,128)(2,1)} %v_hbm.1, bf16[3,32,128]{2,1,0:T(8,128)(2,1)} %k_hbm.1, bf16[32,128]{1,0:T(8,128)(2,1)} %g_hbm.1, ...), custom_call_target="tpu_custom_call" | custom-call | tf_op jit(solution)/shard_map/pack/pallas_call | solution.py:490
  2.5 0.1 collective-permute-start
  2.6 1.9 %collective-permute-start.1 = (bf16[128,128]{1,0:T(8,128)(2,1)S(1)}, bf16[128,128]{1,0:T(8,128)(2,1)S(1)}, u32[]{:S(2)}, u32[]{:S(2)}) collective-permute-start(bf16[128,128]{1,0:T(8,128)(2,1)S(1)} %get-tuple-element.23), channel_id=1, source_target_pairs={{1,2},{2,1},{5,6},{6,5},{9,10},{10,9},{13,14},{14,13},{17,18},{18,... | collective-permute-start | bytes 98312 | tf_op jit(solution)/shard_map/ppermute | solution.py:506
  4.5 0.0 collective-permute-done.sec_a.refs_5_
  4.5 3.3 %collective-permute-done.1.sec_b.refs_6_ = bf16[128,128]{1,0:T(8,128)(2,1)S(1)} collective-permute-done((bf16[128,128]{1,0:T(8,128)(2,1)S(1)}, bf16[128,128]{1,0:T(8,128)(2,1)S(1)}, u32[]{:S(2)}, u32[]{:S(2)}) %collective-permute-start.1) | collective-permute-done | bytes 32800 | tf_op jit(solution)/shard_map/ppermute | solution.py:506
  7.9 1.6 %collective-permute-start.2 = (bf16[544,128]{1,0:T(8,128)(2,1)S(1)}, bf16[544,128]{1,0:T(8,128)(2,1)S(1)}, u32[]{:S(2)}, u32[]{:S(2)}) collective-permute-start(bf16[544,128]{1,0:T(8,128)(2,1)S(1)} %get-tuple-element.24), channel_id=1, source_target_pairs={{0,4},{4,0},{8,12},{12,8},{16,20},{20,16},{24,28},{28,24},{1,5},{5... | collective-permute-start | bytes 417800 | tf_op jit(solution)/shard_map/ppermute | solution.py:509
  9.5 0.7 %collective-permute-start.3 = (bf16[544,128]{1,0:T(8,128)(2,1)S(1)}, bf16[544,128]{1,0:T(8,128)(2,1)S(1)}, u32[]{:S(2)}, u32[]{:S(2)}) collective-permute-start(bf16[544,128]{1,0:T(8,128)(2,1)S(1)} %get-tuple-element.25), channel_id=1, source_target_pairs={{4,8},{8,4},{12,16},{16,12},{20,24},{24,20},{5,9},{9,5},{13,17},{1... | collective-permute-start | bytes 417800 | tf_op jit(solution)/shard_map/ppermute | solution.py:510
  10.1 0.6 %prep.1 = (f32[12,3,144,128]{3,2,1,0:T(8,128)S(1)}, f32[12,4,136,128]{3,2,1,0:T(8,128)S(1)}) custom-call(bf16[10,3,128,128]{3,2,1,0:T(8,128)(2,1)S(1)} %get-tuple-element.18.own_ref, bf16[128,128]{1,0:T(8,128)(2,1)S(1)} %get-tuple-element.19.kt_ref.refs_4_), custom_call_target="tpu_custom_call" | custom-call | tf_op jit(solution)/shard_map/prep/pallas_call | solution.py:518
  11.4 1.6 %collective-permute-done.2.refs_7_ = bf16[544,128]{1,0:T(8,128)(2,1)S(1)} collective-permute-done((bf16[544,128]{1,0:T(8,128)(2,1)S(1)}, bf16[544,128]{1,0:T(8,128)(2,1)S(1)}, u32[]{:S(2)}, u32[]{:S(2)}) %collective-permute-start.2) | collective-permute-done | bytes 139296 | tf_op jit(solution)/shard_map/ppermute | solution.py:509
  13.0 0.0 collective-permute-done.3.refs_8_
  13.0 7.2 %fine.1 = (f32[1,40,128]{2,1,0:T(8,128)S(1)}, bf16[10,3,128,128]{3,2,1,0:T(8,128)(2,1)S(1)}, bf16[10,3,128,128]{3,2,1,0:T(8,128)(2,1)S(1)}, f32[12,3,144,128]{3,2,1,0:T(8,128)S(1)}, f32[12,4,136,128]{3,2,1,0:T(8,128)S(1)}) custom-call(s32[1,1]{1,0:T(1,128)S(6)} %copy.11.refs_0_, ...), custom_call_target="tpu_custom_call", output_to_operand_aliasing={{3}: (2, {}), {4}: (3, {})} | custom-call | tf_op jit(solution)/shard_map/fine/pallas_call | solution.py:519
  20.3 7.0 %collective-permute-start.4 = (f32[1,40,128]{2,1,0:T(8,128)S(1)}, f32[1,40,128]{2,1,0:T(8,128)S(1)}, u32[]{:S(2)}, u32[]{:S(2)}) collective-permute-start(f32[1,40,128]{2,1,0:T(8,128)S(1)} %get-tuple-element.26), channel_id=1, source_target_pairs={{0,16},{4,20},{8,24},{12,28},{16,0},{20,4},{24,8},{28,12},{1,17},{... | collective-permute-start | bytes 61448 | tf_op jit(solution)/shard_map/ppermute | solution.py:546
  27.2 1.8 %collective-permute-done.4 = f32[1,40,128]{2,1,0:T(8,128)S(1)} collective-permute-done((f32[1,40,128]{2,1,0:T(8,128)S(1)}, f32[1,40,128]{2,1,0:T(8,128)S(1)}, u32[]{:S(2)}, u32[]{:S(2)}) %collective-permute-start.4) | collective-permute-done | bytes 20512 | tf_op jit(solution)/shard_map/ppermute | solution.py:546
  29.0 2.1 %collective-permute-start.7 = (f32[2,40,128]{2,1,0:T(8,128)S(1)}, f32[2,40,128]{2,1,0:T(8,128)S(1)}, u32[]{:S(2)}, u32[]{:S(2)}) collective-permute-start(f32[2,40,128]{2,1,0:T(8,128)S(1)} %constant_dynamic-update-slice_fusion.refs_0_), channel_id=1, source_target_pairs={{0,12},{4,8},{8,4},{12,0},{16,28},{20,24},{24,20},{28,16},{1,13},{... | collective-permute-start | bytes 122888 | tf_op jit(solution)/shard_map/ppermute | solution.py:546
  31.0 1.5 %collective-permute-start.6 = (f32[2,40,128]{2,1,0:T(8,128)S(1)}, f32[2,40,128]{2,1,0:T(8,128)S(1)}, u32[]{:S(2)}, u32[]{:S(2)}) collective-permute-start(f32[2,40,128]{2,1,0:T(8,128)S(1)} %constant_dynamic-update-slice_fusion.refs_0_), channel_id=1, source_target_pairs={{0,4},{4,0},{8,12},{12,8},{16,20},{20,16},{24,28},{28,24},{1,5},{5... | collective-permute-start | bytes 122888 | tf_op jit(solution)/shard_map/ppermute | solution.py:546
  32.5 0.0 collective-permute-start.5
  32.5 1.3 %collective-permute-done.7.refs_3_ = f32[2,40,128]{2,1,0:T(8,128)S(1)} collective-permute-done((f32[2,40,128]{2,1,0:T(8,128)S(1)}, f32[2,40,128]{2,1,0:T(8,128)S(1)}, u32[]{:S(2)}, u32[]{:S(2)}) %collective-permute-start.7) | collective-permute-done | bytes 40992 | tf_op jit(solution)/shard_map/ppermute | solution.py:546
  33.9 1.2 %collective-permute-done.6.refs_2_ = f32[2,40,128]{2,1,0:T(8,128)S(1)} collective-permute-done((f32[2,40,128]{2,1,0:T(8,128)S(1)}, f32[2,40,128]{2,1,0:T(8,128)S(1)}, u32[]{:S(2)}, u32[]{:S(2)}) %collective-permute-start.6) | collective-permute-done | bytes 40992 | tf_op jit(solution)/shard_map/ppermute | solution.py:546
  35.0 1.5 %collective-permute-done.5.refs_1_ = f32[2,40,128]{2,1,0:T(8,128)S(1)} collective-permute-done((f32[2,40,128]{2,1,0:T(8,128)S(1)}, f32[2,40,128]{2,1,0:T(8,128)S(1)}, u32[]{:S(2)}, u32[]{:S(2)}) %collective-permute-start.5) | collective-permute-done | bytes 40992 | tf_op jit(solution)/shard_map/ppermute | solution.py:546
  36.5 3.7 %level.1 = f32[16,3,32,128]{3,2,1,0:T(8,128)} custom-call(f32[2,40,128]{2,1,0:T(8,128)S(1)} %constant_dynamic-update-slice_fusion.refs_0_, f32[2,40,128]{2,1,0:T(8,128)S(1)} %collective-permute-done.5.refs_1_, f32[2,40,128]{2,1,0:T(8,128)S(1)} %collective-permute-done.6.refs_2_, f32[2,40,128]{2,1,0:T(8,128)S(1)} %collective-permute-done.7.refs_3_, ...), custom_call_target="tpu_custom_call" | custom-call | tf_op jit(solution)/shard_map/level/pallas_call | solution.py:557
  (3 shorter events, 0.0 us)
Async XLA Ops:
  2.5 2.0 %collective-permute-start = (bf16[128,128]{1,0:T(8,128)(2,1)S(1)}, bf16[128,128]{1,0:T(8,128)(2,1)S(1)}, u32[]{:S(2)}, u32[]{:S(2)}) collective-permute-start(bf16[128,128]{1,0:T(8,128)(2,1)S(1)} %get-tuple-element.22), channel_id=1, source_target_pairs={{0,1},{1,0},{2,3},{3,2},{4,5},{5,4},{6,7},{7,6},{8,9},{9,8},{10,11... | collective-permute-start | bytes 98312 | tf_op jit(solution)/shard_map/ppermute | solution.py:505
  2.6 5.2 %collective-permute-start.1 = (bf16[128,128]{1,0:T(8,128)(2,1)S(1)}, bf16[128,128]{1,0:T(8,128)(2,1)S(1)}, u32[]{:S(2)}, u32[]{:S(2)}) collective-permute-start(bf16[128,128]{1,0:T(8,128)(2,1)S(1)} %get-tuple-element.23), channel_id=1, source_target_pairs={{1,2},{2,1},{5,6},{6,5},{9,10},{10,9},{13,14},{14,13},{17,18},{18,... | collective-permute-start | bytes 98312 | tf_op jit(solution)/shard_map/ppermute | solution.py:506
  7.9 5.1 %collective-permute-start.2 = (bf16[544,128]{1,0:T(8,128)(2,1)S(1)}, bf16[544,128]{1,0:T(8,128)(2,1)S(1)}, u32[]{:S(2)}, u32[]{:S(2)}) collective-permute-start(bf16[544,128]{1,0:T(8,128)(2,1)S(1)} %get-tuple-element.24), channel_id=1, source_target_pairs={{0,4},{4,0},{8,12},{12,8},{16,20},{20,16},{24,28},{28,24},{1,5},{5... | collective-permute-start | bytes 417800 | tf_op jit(solution)/shard_map/ppermute | solution.py:509
  9.5 3.5 %collective-permute-start.3 = (bf16[544,128]{1,0:T(8,128)(2,1)S(1)}, bf16[544,128]{1,0:T(8,128)(2,1)S(1)}, u32[]{:S(2)}, u32[]{:S(2)}) collective-permute-start(bf16[544,128]{1,0:T(8,128)(2,1)S(1)} %get-tuple-element.25), channel_id=1, source_target_pairs={{4,8},{8,4},{12,16},{16,12},{20,24},{24,20},{5,9},{9,5},{13,17},{1... | collective-permute-start | bytes 417800 | tf_op jit(solution)/shard_map/ppermute | solution.py:510
  20.3 8.7 %collective-permute-start.4 = (f32[1,40,128]{2,1,0:T(8,128)S(1)}, f32[1,40,128]{2,1,0:T(8,128)S(1)}, u32[]{:S(2)}, u32[]{:S(2)}) collective-permute-start(f32[1,40,128]{2,1,0:T(8,128)S(1)} %get-tuple-element.26), channel_id=1, source_target_pairs={{0,16},{4,20},{8,24},{12,28},{16,0},{20,4},{24,8},{28,12},{1,17},{... | collective-permute-start | bytes 61448 | tf_op jit(solution)/shard_map/ppermute | solution.py:546
  29.0 4.9 %collective-permute-start.7 = (f32[2,40,128]{2,1,0:T(8,128)S(1)}, f32[2,40,128]{2,1,0:T(8,128)S(1)}, u32[]{:S(2)}, u32[]{:S(2)}) collective-permute-start(f32[2,40,128]{2,1,0:T(8,128)S(1)} %constant_dynamic-update-slice_fusion.refs_0_), channel_id=1, source_target_pairs={{0,12},{4,8},{8,4},{12,0},{16,28},{20,24},{24,20},{28,16},{1,13},{... | collective-permute-start | bytes 122888 | tf_op jit(solution)/shard_map/ppermute | solution.py:546
  31.0 4.0 %collective-permute-start.6 = (f32[2,40,128]{2,1,0:T(8,128)S(1)}, f32[2,40,128]{2,1,0:T(8,128)S(1)}, u32[]{:S(2)}, u32[]{:S(2)}) collective-permute-start(f32[2,40,128]{2,1,0:T(8,128)S(1)} %constant_dynamic-update-slice_fusion.refs_0_), channel_id=1, source_target_pairs={{0,4},{4,0},{8,12},{12,8},{16,20},{20,16},{24,28},{28,24},{1,5},{5... | collective-permute-start | bytes 122888 | tf_op jit(solution)/shard_map/ppermute | solution.py:546
  32.5 4.0 %collective-permute-start.5 = (f32[2,40,128]{2,1,0:T(8,128)S(1)}, f32[2,40,128]{2,1,0:T(8,128)S(1)}, u32[]{:S(2)}, u32[]{:S(2)}) collective-permute-start(f32[2,40,128]{2,1,0:T(8,128)S(1)} %constant_dynamic-update-slice_fusion.refs_0_), channel_id=1, source_target_pairs={{0,8},{4,12},{8,0},{12,4},{16,24},{20,28},{24,16},{28,20},{1,9},{5... | collective-permute-start | bytes 122888 | tf_op jit(solution)/shard_map/ppermute | solution.py:546

commit v4 on v3

--- a/solution.py
+++ b/solution.py
@@ -35,7 +35,7 @@
     return dot(ah, bh, dims) + (dot(ah, bl, dims) + dot(al, bh, dims))
 
 
-def inverse_factor(gram, size, step=4):
+def inverse_factor(gram, size, step=16):
     row, lane = iota((size, 128), 0), iota((size, 128), 1)
     work = jnp.where(lane < size, gram, jnp.where(lane == row + size, 1.0, 0.0))
     for first in range(0, size, step):
@@ -83,13 +83,15 @@
     firsts, lasts = [None] * pieces, [None] * pieces
     for c in range(comps):
         copies[c].wait()
-        vf[c] = v_buf[c].astype(F32).reshape(nv * cx, cy)
+        for a in range(nv):
+            vf[c, (cx + 8) * a : (cx + 8) * a + cx] = v_buf[c, a].astype(F32)
         for p in range(own + 2):
             rows = [b * own + p for b in range(H)] if p < own else [b + (p - own) * (cx - H) for b in range(H)]
-            stack = [vf[c, pl.ds(x, nv, stride=cx), :] for x in rows]
-            turned = jnp.concatenate(stack, axis=0).T
-            own_ref[p, c] = turned.astype(BF16)
-            firsts[p * comps + c], lasts[p * comps + c] = turned[:8], turned[cy - 8 :]
+            stack = [vf[c, pl.ds(x, nv, stride=cx + 8), :] for x in rows]
+            turned = jnp.concatenate(stack, axis=0).astype(BF16).T
+            own_ref[p, c] = turned
+            firsts[p * comps + c] = turned[:16].astype(F32)[:8]
+            lasts[p * comps + c] = turned[cy - 16 :].astype(F32)[8:]
     for copy in copies[comps:]:
         copy.wait()
     kf[: comps * cx] = k_buf[...].astype(F32).reshape(comps * cx, cy)
@@ -273,7 +275,7 @@
             operator(src, rows, pl.ds(pl.multiple_of(base, 16), 16), 16, None, strips, emit)
             return carry
 
-        lax.fori_loop(0, cy // 16, body, 0)
+        lax.fori_loop(0, cy // 16, body, 0, unroll=True)
 
         def shifted(slot, c):
             left = jnp.where(octet_row == H, 0.0, src[slot, c, 7 + cy : 15 + cy, :])
@@ -340,22 +342,34 @@
     inverse = jnp.where(iota((nv, nv), 0) < rank_ref[0, 0], inverse, 0.0)
     image = gram_n()
 
-    def rim(strip, first, block, own_first):
-        own, other = [], []
-        for at, weight_at in ((mid, slice(0, cy)), (top, slice(cy, cy + 8))):
-            for c in range(comps):
-                held = [x2[first + i, c, at, block * nv : (block + 1) * nv] for i in range(H)]
-                weight = coef[strip, c, weight_at, :] + coef[strip, comps, weight_at, :]
-                own.append(jnp.concatenate(held, axis=1) * weight)
-                other.append(x2[strip, c, at, :])
-        own.append(jnp.zeros((8, lanes), F32))
-        other.append(jnp.zeros((8, lanes), F32))
-        own, other = jnp.concatenate(own, axis=0), jnp.concatenate(other, axis=0)
-        a, b = (own, other) if own_first else (other, own)
-        return fold(dot3(a, b, TN))[:, :nv]
-
-    rim_next = rim(TAIL, OWN - H, H - 1, True) * has_after
-    rim_prev = rim(HEAD, 0, 0, True) * has_before
+    def rim(strip, first, block):
+        def rows_of(slot, weighted):
+            out = []
+            for at, weight_at in ((mid, slice(0, cy)), (top, slice(cy, cy + 8))):
+                for c in range(comps):
+                    rows = x2[slot, c, at, :]
+                    if weighted:
+                        rows = rows * (coef[slot, c, weight_at, :] + coef[slot, comps, weight_at, :])
+                    out.append(rows)
+            return out
+
+        pad = [jnp.zeros((8, lanes), F32)]
+        turned = [half.T for half in split(jnp.concatenate(rows_of(strip, True) + pad, axis=0))]
+        total = jnp.zeros((2 * nv, 2 * lanes), F32)
+        for i in range(H):
+            margin = split(jnp.concatenate([x2[first + i, c, top, :] for c in range(comps)] + pad, axis=0))
+            own = [
+                jnp.concatenate([ref[first + i, c] for c in range(comps)] + [rest], axis=0)
+                for ref, rest in zip((high2, low2), margin)
+            ]
+            other = jnp.concatenate([half[i * nv : (i + 1) * nv] for half in turned], axis=0)
+            total = total + dot(other, jnp.concatenate(own, axis=1), NN)
+        total = total[:nv] + total[nv:]
+        total = total[:, :lanes] + total[:, lanes:]
+        return total[:, block * nv : (block + 1) * nv].T
+
+    rim_next = rim(TAIL, OWN - H, H - 1) * has_after
+    rim_prev = rim(HEAD, 0, 0) * has_before
 
     start = start_ref[...]
     k2 = start.shape[0]
@@ -495,7 +509,7 @@
             pltpu.VMEM((comps, nv, cx, cy), BF16),
             pltpu.VMEM(stiffness.shape, BF16),
             pltpu.VMEM(coupling.shape, BF16),
-            pltpu.VMEM((comps, nv * cx, cy), F32),
+            pltpu.VMEM((comps, nv * (cx + 8), cy), F32),
             pltpu.VMEM((channels * cx, cy), F32),
             pltpu.SemaphoreType.DMA((comps + 3,)),
         ],

time: 40.4 us -> 37.7 us (0.933)
  Pallas kernels: 14.1 us -> 11.4 us
    pallas_call x1, Pallas kernels: 7.24 us -> 5.67 us  [on_device(): call(fine, (shape((1, nv + 8, cy), F32), half, half, rows, weights), [plt...]
    pallas_call x1, Pallas kernels: 2.52 us -> 1.66 us  [on_device(): call(pack_kernel, (shape((cx // H + 2, comps, cy, H * nv), BF16), shape((...]
where the time goes in v4:
time: 37.7 us; the launch traced here: 37.5 us
  starting transfers between devices  14.7 us (39%)
  Pallas kernels  11.4 us (30%)
  waiting for transfers between devices  10.6 us (28%)
  between operations  0.72 us (2%)
    ppermute x4, starting transfers between devices, swapped(): return lax.ppermute(block, 'sub', [(i, i ^ bit) for i in range(spans)])  10.5 us
    ppermute x4, waiting for transfers between devices, swapped(): return lax.ppermute(block, 'sub', [(i, i ^ bit) for i in range(spans)])  5.76 us
    pallas_call x1, Pallas kernels, on_device(): call(fine, (shape((1, nv + 8, cy), F32), half, half, rows, weights), [plt...  5.67 us
    pallas_call x1, Pallas kernels, on_device(): call(level, result, [packs] + tiles, 'level', [vmem] * 6, out_specs=hbm)  3.41 us
    ppermute x1, waiting for transfers between devices, on_device(): sec_b = lax.ppermute(sec_b, 'sec', pairs(sects, 1))  3.29 us
    ppermute x1, starting transfers between devices, on_device(): sec_b = lax.ppermute(sec_b, 'sec', pairs(sects, 1))  1.92 us
    pallas_call x1, Pallas kernels, on_device(): call(pack_kernel, (shape((cx // H + 2, comps, cy, H * nv), BF16), shape((...  1.66 us
    ppermute x1, waiting for transfers between devices, on_device(): sub_a = lax.ppermute(sub_a, 'sub', pairs(spans, 0))  1.59 us
  transfers between devices with their start and end apart: 8, of which 6 were waited for; matrix products, arithmetic and copies ran while one was open for 0% of the time, Pallas kernels for 2%

profile of v4, /device:TPU:2, one launch (start us, length us, event | category | flops | bytes accessed | tf_op | source)
XLA Modules:
  0.0 37.5 jit_solution(1830796557313078398)
XLA Ops:
  0.0 1.7 %pack.1 = (bf16[10,3,128,128]{3,2,1,0:T(8,128)(2,1)S(1)}, bf16[128,128]{1,0:T(8,128)(2,1)S(1)}, bf16[128,128]{1,0:T(8,128)(2,1)S(1)}, bf16[128,128]{1,0:T(8,128)(2,1)S(1)}, f32[16,32]{1,0:T(8,128)S(1)}) custom-call(bf16[32,3,32,128]{3,2,1,0:T(8,128)(2,1)} %v_hbm.1, bf16[3,32,128]{2,1,0:T(8,128)(2,1)} %k_hbm.1, bf16[32,128]{1,0:T(8,128)(2,1)} %g_hbm.1, ...), custom_call_target="tpu_custom_call" | custom-call | tf_op jit(solution)/shard_map/pack/pallas_call | solution.py:504
  1.7 0.1 collective-permute-start
  1.7 1.9 %collective-permute-start.1 = (bf16[128,128]{1,0:T(8,128)(2,1)S(1)}, bf16[128,128]{1,0:T(8,128)(2,1)S(1)}, u32[]{:S(2)}, u32[]{:S(2)}) collective-permute-start(bf16[128,128]{1,0:T(8,128)(2,1)S(1)} %get-tuple-element.23), channel_id=1, source_target_pairs={{1,2},{2,1},{5,6},{6,5},{9,10},{10,9},{13,14},{14,13},{17,18},{18,... | collective-permute-start | bytes 98312 | tf_op jit(solution)/shard_map/ppermute | solution.py:520
  3.7 0.0 collective-permute-done.sec_a.refs_5_
  3.7 3.3 %collective-permute-done.1.sec_b.refs_6_ = bf16[128,128]{1,0:T(8,128)(2,1)S(1)} collective-permute-done((bf16[128,128]{1,0:T(8,128)(2,1)S(1)}, bf16[128,128]{1,0:T(8,128)(2,1)S(1)}, u32[]{:S(2)}, u32[]{:S(2)}) %collective-permute-start.1) | collective-permute-done | bytes 32800 | tf_op jit(solution)/shard_map/ppermute | solution.py:520
  7.0 1.6 %collective-permute-start.2 = (bf16[544,128]{1,0:T(8,128)(2,1)S(1)}, bf16[544,128]{1,0:T(8,128)(2,1)S(1)}, u32[]{:S(2)}, u32[]{:S(2)}) collective-permute-start(bf16[544,128]{1,0:T(8,128)(2,1)S(1)} %get-tuple-element.24), channel_id=1, source_target_pairs={{0,4},{4,0},{8,12},{12,8},{16,20},{20,16},{24,28},{28,24},{1,5},{5... | collective-permute-start | bytes 417800 | tf_op jit(solution)/shard_map/ppermute | solution.py:523
  8.6 0.7 %collective-permute-start.3 = (bf16[544,128]{1,0:T(8,128)(2,1)S(1)}, bf16[544,128]{1,0:T(8,128)(2,1)S(1)}, u32[]{:S(2)}, u32[]{:S(2)}) collective-permute-start(bf16[544,128]{1,0:T(8,128)(2,1)S(1)} %get-tuple-element.25), channel_id=1, source_target_pairs={{4,8},{8,4},{12,16},{16,12},{20,24},{24,20},{5,9},{9,5},{13,17},{1... | collective-permute-start | bytes 417800 | tf_op jit(solution)/shard_map/ppermute | solution.py:524
  9.3 0.6 %prep.1 = (f32[12,3,144,128]{3,2,1,0:T(8,128)S(1)}, f32[12,4,136,128]{3,2,1,0:T(8,128)S(1)}) custom-call(bf16[10,3,128,128]{3,2,1,0:T(8,128)(2,1)S(1)} %get-tuple-element.18.own_ref, bf16[128,128]{1,0:T(8,128)(2,1)S(1)} %get-tuple-element.19.kt_ref.refs_4_), custom_call_target="tpu_custom_call" | custom-call | tf_op jit(solution)/shard_map/prep/pallas_call | solution.py:532
  10.6 1.6 %collective-permute-done.2.refs_7_ = bf16[544,128]{1,0:T(8,128)(2,1)S(1)} collective-permute-done((bf16[544,128]{1,0:T(8,128)(2,1)S(1)}, bf16[544,128]{1,0:T(8,128)(2,1)S(1)}, u32[]{:S(2)}, u32[]{:S(2)}) %collective-permute-start.2) | collective-permute-done | bytes 139296 | tf_op jit(solution)/shard_map/ppermute | solution.py:523
  12.1 0.0 collective-permute-done.3.refs_8_
  12.1 5.7 %fine.1 = (f32[1,40,128]{2,1,0:T(8,128)S(1)}, bf16[10,3,128,128]{3,2,1,0:T(8,128)(2,1)S(1)}, bf16[10,3,128,128]{3,2,1,0:T(8,128)(2,1)S(1)}, f32[12,3,144,128]{3,2,1,0:T(8,128)S(1)}, f32[12,4,136,128]{3,2,1,0:T(8,128)S(1)}) custom-call(s32[1,1]{1,0:T(1,128)S(6)} %copy.11.refs_0_, ...), custom_call_target="tpu_custom_call", output_to_operand_aliasing={{3}: (2, {}), {4}: (3, {})} | custom-call | tf_op jit(solution)/shard_map/fine/pallas_call | solution.py:533
  17.8 6.9 %collective-permute-start.4 = (f32[1,40,128]{2,1,0:T(8,128)S(1)}, f32[1,40,128]{2,1,0:T(8,128)S(1)}, u32[]{:S(2)}, u32[]{:S(2)}) collective-permute-start(f32[1,40,128]{2,1,0:T(8,128)S(1)} %get-tuple-element.26), channel_id=1, source_target_pairs={{0,16},{4,20},{8,24},{12,28},{16,0},{20,4},{24,8},{28,12},{1,17},{... | collective-permute-start | bytes 61448 | tf_op jit(solution)/shard_map/ppermute | solution.py:560
  24.8 1.8 %collective-permute-done.4 = f32[1,40,128]{2,1,0:T(8,128)S(1)} collective-permute-done((f32[1,40,128]{2,1,0:T(8,128)S(1)}, f32[1,40,128]{2,1,0:T(8,128)S(1)}, u32[]{:S(2)}, u32[]{:S(2)}) %collective-permute-start.4) | collective-permute-done | bytes 20512 | tf_op jit(solution)/shard_map/ppermute | solution.py:560
  26.5 2.1 %collective-permute-start.7 = (f32[2,40,128]{2,1,0:T(8,128)S(1)}, f32[2,40,128]{2,1,0:T(8,128)S(1)}, u32[]{:S(2)}, u32[]{:S(2)}) collective-permute-start(f32[2,40,128]{2,1,0:T(8,128)S(1)} %constant_dynamic-update-slice_fusion.refs_0_), channel_id=1, source_target_pairs={{0,12},{4,8},{8,4},{12,0},{16,28},{20,24},{24,20},{28,16},{1,13},{... | collective-permute-start | bytes 122888 | tf_op jit(solution)/shard_map/ppermute | solution.py:560
  28.6 1.5 %collective-permute-start.6 = (f32[2,40,128]{2,1,0:T(8,128)S(1)}, f32[2,40,128]{2,1,0:T(8,128)S(1)}, u32[]{:S(2)}, u32[]{:S(2)}) collective-permute-start(f32[2,40,128]{2,1,0:T(8,128)S(1)} %constant_dynamic-update-slice_fusion.refs_0_), channel_id=1, source_target_pairs={{0,4},{4,0},{8,12},{12,8},{16,20},{20,16},{24,28},{28,24},{1,5},{5... | collective-permute-start | bytes 122888 | tf_op jit(solution)/shard_map/ppermute | solution.py:560
  30.1 0.0 collective-permute-start.5
  30.1 1.3 %collective-permute-done.7.refs_3_ = f32[2,40,128]{2,1,0:T(8,128)S(1)} collective-permute-done((f32[2,40,128]{2,1,0:T(8,128)S(1)}, f32[2,40,128]{2,1,0:T(8,128)S(1)}, u32[]{:S(2)}, u32[]{:S(2)}) %collective-permute-start.7) | collective-permute-done | bytes 40992 | tf_op jit(solution)/shard_map/ppermute | solution.py:560
  31.4 1.2 %collective-permute-done.6.refs_2_ = f32[2,40,128]{2,1,0:T(8,128)S(1)} collective-permute-done((f32[2,40,128]{2,1,0:T(8,128)S(1)}, f32[2,40,128]{2,1,0:T(8,128)S(1)}, u32[]{:S(2)}, u32[]{:S(2)}) %collective-permute-start.6) | collective-permute-done | bytes 40992 | tf_op jit(solution)/shard_map/ppermute | solution.py:560
  32.6 1.5 %collective-permute-done.5.refs_1_ = f32[2,40,128]{2,1,0:T(8,128)S(1)} collective-permute-done((f32[2,40,128]{2,1,0:T(8,128)S(1)}, f32[2,40,128]{2,1,0:T(8,128)S(1)}, u32[]{:S(2)}, u32[]{:S(2)}) %collective-permute-start.5) | collective-permute-done | bytes 40992 | tf_op jit(solution)/shard_map/ppermute | solution.py:560
  34.1 3.4 %level.1 = f32[16,3,32,128]{3,2,1,0:T(8,128)} custom-call(f32[2,40,128]{2,1,0:T(8,128)S(1)} %constant_dynamic-update-slice_fusion.refs_0_, f32[2,40,128]{2,1,0:T(8,128)S(1)} %collective-permute-done.5.refs_1_, f32[2,40,128]{2,1,0:T(8,128)S(1)} %collective-permute-done.6.refs_2_, f32[2,40,128]{2,1,0:T(8,128)S(1)} %collective-permute-done.7.refs_3_, ...), custom_call_target="tpu_custom_call" | custom-call | tf_op jit(solution)/shard_map/level/pallas_call | solution.py:571
  (3 shorter events, 0.0 us)
Async XLA Ops:
  1.7 2.0 %collective-permute-start = (bf16[128,128]{1,0:T(8,128)(2,1)S(1)}, bf16[128,128]{1,0:T(8,128)(2,1)S(1)}, u32[]{:S(2)}, u32[]{:S(2)}) collective-permute-start(bf16[128,128]{1,0:T(8,128)(2,1)S(1)} %get-tuple-element.22), channel_id=1, source_target_pairs={{0,1},{1,0},{2,3},{3,2},{4,5},{5,4},{6,7},{7,6},{8,9},{9,8},{10,11... | collective-permute-start | bytes 98312 | tf_op jit(solution)/shard_map/ppermute | solution.py:519
  1.7 5.2 %collective-permute-start.1 = (bf16[128,128]{1,0:T(8,128)(2,1)S(1)}, bf16[128,128]{1,0:T(8,128)(2,1)S(1)}, u32[]{:S(2)}, u32[]{:S(2)}) collective-permute-start(bf16[128,128]{1,0:T(8,128)(2,1)S(1)} %get-tuple-element.23), channel_id=1, source_target_pairs={{1,2},{2,1},{5,6},{6,5},{9,10},{10,9},{13,14},{14,13},{17,18},{18,... | collective-permute-start | bytes 98312 | tf_op jit(solution)/shard_map/ppermute | solution.py:520
  7.0 5.1 %collective-permute-start.2 = (bf16[544,128]{1,0:T(8,128)(2,1)S(1)}, bf16[544,128]{1,0:T(8,128)(2,1)S(1)}, u32[]{:S(2)}, u32[]{:S(2)}) collective-permute-start(bf16[544,128]{1,0:T(8,128)(2,1)S(1)} %get-tuple-element.24), channel_id=1, source_target_pairs={{0,4},{4,0},{8,12},{12,8},{16,20},{20,16},{24,28},{28,24},{1,5},{5... | collective-permute-start | bytes 417800 | tf_op jit(solution)/shard_map/ppermute | solution.py:523
  8.6 3.5 %collective-permute-start.3 = (bf16[544,128]{1,0:T(8,128)(2,1)S(1)}, bf16[544,128]{1,0:T(8,128)(2,1)S(1)}, u32[]{:S(2)}, u32[]{:S(2)}) collective-permute-start(bf16[544,128]{1,0:T(8,128)(2,1)S(1)} %get-tuple-element.25), channel_id=1, source_target_pairs={{4,8},{8,4},{12,16},{16,12},{20,24},{24,20},{5,9},{9,5},{13,17},{1... | collective-permute-start | bytes 417800 | tf_op jit(solution)/shard_map/ppermute | solution.py:524
  17.8 8.7 %collective-permute-start.4 = (f32[1,40,128]{2,1,0:T(8,128)S(1)}, f32[1,40,128]{2,1,0:T(8,128)S(1)}, u32[]{:S(2)}, u32[]{:S(2)}) collective-permute-start(f32[1,40,128]{2,1,0:T(8,128)S(1)} %get-tuple-element.26), channel_id=1, source_target_pairs={{0,16},{4,20},{8,24},{12,28},{16,0},{20,4},{24,8},{28,12},{1,17},{... | collective-permute-start | bytes 61448 | tf_op jit(solution)/shard_map/ppermute | solution.py:560
  26.5 4.9 %collective-permute-start.7 = (f32[2,40,128]{2,1,0:T(8,128)S(1)}, f32[2,40,128]{2,1,0:T(8,128)S(1)}, u32[]{:S(2)}, u32[]{:S(2)}) collective-permute-start(f32[2,40,128]{2,1,0:T(8,128)S(1)} %constant_dynamic-update-slice_fusion.refs_0_), channel_id=1, source_target_pairs={{0,12},{4,8},{8,4},{12,0},{16,28},{20,24},{24,20},{28,16},{1,13},{... | collective-permute-start | bytes 122888 | tf_op jit(solution)/shard_map/ppermute | solution.py:560
  28.6 4.0 %collective-permute-start.6 = (f32[2,40,128]{2,1,0:T(8,128)S(1)}, f32[2,40,128]{2,1,0:T(8,128)S(1)}, u32[]{:S(2)}, u32[]{:S(2)}) collective-permute-start(f32[2,40,128]{2,1,0:T(8,128)S(1)} %constant_dynamic-update-slice_fusion.refs_0_), channel_id=1, source_target_pairs={{0,4},{4,0},{8,12},{12,8},{16,20},{20,16},{24,28},{28,24},{1,5},{5... | collective-permute-start | bytes 122888 | tf_op jit(solution)/shard_map/ppermute | solution.py:560
  30.1 4.0 %collective-permute-start.5 = (f32[2,40,128]{2,1,0:T(8,128)S(1)}, f32[2,40,128]{2,1,0:T(8,128)S(1)}, u32[]{:S(2)}, u32[]{:S(2)}) collective-permute-start(f32[2,40,128]{2,1,0:T(8,128)S(1)} %constant_dynamic-update-slice_fusion.refs_0_), channel_id=1, source_target_pairs={{0,8},{4,12},{8,0},{12,4},{16,24},{20,28},{24,16},{28,20},{1,9},{5... | collective-permute-start | bytes 122888 | tf_op jit(solution)/shard_map/ppermute | solution.py:560

commit v5 on v4

--- a/solution.py
+++ b/solution.py
@@ -67,8 +67,23 @@
     return pltpu.roll(octet, H, 0)
 
 
+def narrowed(table, kinds, cx):
+    wide = 2 * H * kinds
+    parts = table.shape[1] // wide if table.shape[0] > 8 else 1
+    count = table.shape[0] // parts
+    lane = iota((count, table.shape[1]), 1)
+    inner = lax.rem(lane, wide)
+    side, kind, i = inner // (H * kinds), lax.rem(inner // H, kinds), lax.rem(inner, H)
+    source = kind * cx + i + side * (cx - H)
+    out = jnp.zeros((count, table.shape[1]), F32)
+    for part in range(parts):
+        picked = jnp.take_along_axis(table[part * count : (part + 1) * count], source, axis=1)
+        out = picked if parts == 1 else jnp.where(lane // wide == part, picked, out)
+    return out
+
+
 def pack_kernel(
-    v_hbm, k_hbm, g_hbm, start_hbm, own_ref, kt_ref, sec_a, sec_b, start_ref, v_buf, k_buf, g_buf, vf, kf, sems
+    v_hbm, k_hbm, g_hbm, start_hbm, own_ref, kt_ref, sec_a, sec_b, start_ref, narrow_ref, v_buf, k_buf, g_buf, vf, kf, sems
 ):
     comps, nv, cx, cy = v_buf.shape
     copies = [pltpu.make_async_copy(v_hbm.at[:, c], v_buf.at[c], sems.at[c]) for c in range(comps)]
@@ -98,6 +113,7 @@
     kf[comps * cx :] = g_buf[...].astype(F32)
     turned = kf[...].T
     kt_ref[...] = turned.astype(BF16)
+    narrow_ref[...] = narrowed(turned, comps + 1, cx).astype(BF16)
     firsts[-1], lasts[-1] = turned[:8], turned[cy - 8 :]
     for octets in (firsts, lasts):
         if len(octets) % 2:
@@ -120,21 +136,23 @@
     return out
 
 
-def edge_kernel(own_ref, kt_ref, sec_a, sec_b, sub_a, sub_b):
+def edge_kernel(cx, own_ref, narrow_ref, sec_a, sec_b, sub_a, sub_b):
     slots, comps, cy, lanes = own_ref.shape
     sub_even = lax.rem(lax.axis_index("sub"), 2) == 0
     sec_even = lax.rem(lax.axis_index("sec"), 2) == 0
     octets = margin_octets(sec_a, sec_b, sec_even, slots * comps + 1)
     first, last = slots - 2, slots - 1
-    head = octets[first * comps : first * comps + comps] + octets[-1:]
-    tail = octets[last * comps : last * comps + comps] + octets[-1:]
+    table = [narrowed(octets[-1], comps + 1, cx)]
+    head = octets[first * comps : first * comps + comps] + table
+    tail = octets[last * comps : last * comps + comps] + table
     head, tail = jnp.concatenate(head, axis=0), jnp.concatenate(tail, axis=0)
     for ref, to_next in ((sub_a, sub_even), (sub_b, jnp.logical_not(sub_even))):
         slot = jnp.where(to_next, last, first)
         for c in range(comps):
             ref[c * cy : (c + 1) * cy] = own_ref[slot, c]
-        ref[comps * cy : (comps + 1) * cy] = kt_ref[...]
-        ref[(comps + 1) * cy :] = jnp.where(to_next, tail, head).astype(BF16)
+        narrow = comps * cy + narrow_ref.shape[0]
+        ref[comps * cy : narrow] = narrow_ref[...]
+        ref[narrow:] = jnp.where(to_next, tail, head).astype(BF16)
 
 
 def spread(table, wanted, kinds, cx):
@@ -153,7 +171,59 @@
     return block * own + p if p < own else block + (p - own) * (cx - H)
 
 
-def prep_kernel(own_ref, kt_ref, v0, coef):
+def operator(src, coef, nv, rows, weight_rows, sides_of, slots, margins, inside_of, emit):
+    count, comps, _, lanes = src.shape
+    OWN = count - 4
+    BEFORE, AFTER, HEAD, TAIL = range(OWN, count)
+
+    def at(slot, c):
+        return src[slot, c, rows, :]
+
+    lane = iota(at(0, 0).shape, 1)
+    in_first, in_last = lane < nv, lane >= lanes - nv
+
+    def up_of(slot, c):
+        if 0 < slot < OWN:
+            return at(slot - 1, c)
+        last, margin = {0: (OWN - 1, BEFORE), AFTER: (AFTER, OWN - 1), HEAD: (HEAD, BEFORE)}.get(slot, (slot, None))
+        if margin is None or (margin == BEFORE and not margins):
+            return jnp.where(in_first, 0.0, pltpu.roll(at(last, c), nv, 1))
+        return pltpu.roll(jnp.where(in_last, at(margin, c), at(last, c)), nv, 1)
+
+    def down_of(slot, c):
+        if slot < OWN - 1:
+            return at(slot + 1, c)
+        next_, margin = {OWN - 1: (0, AFTER), BEFORE: (BEFORE, 0), TAIL: (TAIL, AFTER)}.get(slot, (slot, None))
+        if margin is None or (margin == AFTER and not margins):
+            return jnp.where(in_last, 0.0, pltpu.roll(at(next_, c), lanes - nv, 1))
+        return pltpu.roll(jnp.where(in_first, at(margin, c), at(next_, c)), lanes - nv, 1)
+
+    for slot in slots:
+        v = [at(slot, c) for c in range(comps)]
+        weight = [coef[slot, kind, weight_rows, :] for kind in range(comps + 1)]
+        total = weight[comps] * (v[0] + v[1] + v[2])
+        for c in range(comps):
+            beside = sides_of(slot, c) + (up_of(slot, c) + down_of(slot, c))
+            inside = inside_of(slot)
+            if inside is not None:
+                beside = beside * inside
+            emit(slot, c, weight[c] * v[c] + total - beside)
+
+
+def operator_rows(src, coef, nv, slots, margins, inside_of, emit):
+    for base in range(0, src.shape[2] - 16, 16):
+
+        def sides_of(slot, c):
+            return src[slot, c, 7 + base : 23 + base, :] + src[slot, c, 9 + base : 25 + base, :]
+
+        def emit_rows(slot, c, value):
+            emit(slot, c, base, value)
+
+        rows, weight_rows = slice(8 + base, 24 + base), slice(base, base + 16)
+        operator(src, coef, nv, rows, weight_rows, sides_of, slots, margins, inside_of, emit_rows)
+
+
+def prep_kernel(own_ref, kt_ref, v0, coef, x1):
     slots, comps, cy, lanes = own_ref.shape
     own, kinds = slots - 2, comps + 1
     cx = kt_ref.shape[1] // kinds
@@ -167,8 +237,18 @@
         for kind, value in enumerate(terms_of(values)):
             coef[slot, kind, :cy, :] = value
 
-
-def fine_kernel(sizes, rank_ref, start_ref, v0_in, coef_in, kt_ref, sec_a, sec_b, sub_a, sub_b, pack_ref, high2, low2, v0, coef, x1, x2, high3, low3, margin3):
+    mine = [p if p < own else head + p - own for p in range(slots)]
+    for slot in mine:
+        v0[slot, :, :8, :] = jnp.zeros((comps, 8, lanes), F32)
+        v0[slot, :, 8 + cy :, :] = jnp.zeros((comps, 8, lanes), F32)
+
+    def emit(slot, c, base, value):
+        x1[slot, c, 8 + base : 24 + base, :] = value
+
+    operator_rows(v0, coef, lanes // H, mine, False, lambda slot: None, emit)
+
+
+def fine_kernel(sizes, rank_ref, start_ref, v0_in, coef_in, x1_in, kt_ref, sec_a, sec_b, sub_a, sub_b, pack_ref, high2, low2, v0, coef, x1, x2, high3, low3, margin3):
     spans, sects = sizes
     _, comps, cy, lanes = high2.shape
     nv = start_ref.shape[1]
@@ -189,11 +269,13 @@
         a, b = sub_a[first : first + count].astype(F32), sub_b[first : first + count].astype(F32)
         return jnp.where(sub_even, a, b), jnp.where(sub_even, b, a)
 
+    narrow, parts = comps * cy, lanes // (2 * H * kinds)
+    count = cy // parts
     for c in range(comps):
         for p in range(OWN + 2):
             put_octet(p if p < OWN else HEAD + p - OWN, c, octets[p * comps + c])
         v0[AFTER, c, mid, :], v0[BEFORE, c, mid, :] = received(c * cy, cy)
-        after_octet, before_octet = received(kinds * cy + 8 * c, 8)
+        after_octet, before_octet = received(narrow + count + 8 * c, 8)
         put_octet(BEFORE, c, before_octet)
         put_octet(AFTER, c, after_octet)
 
@@ -208,86 +290,36 @@
         rows = [jnp.take_along_axis(octets[-1], wanted + kind * cx, axis=1) for kind in range(kinds)]
         for kind, value in enumerate(terms_of(rows)):
             coef[slot, kind, cy : cy + 8, :] = value * col_in
-    after, before = received(comps * cy, cy)
-    after_octet, before_octet = received(kinds * cy + 8 * comps, 8)
+    after, before = received(narrow, count)
+    after_octet, before_octet = received(narrow + count + 8 * comps, 8)
     block = iota((lanes, lanes), 1) // nv
-    for slot, rows, octet, p in ((AFTER, after, after_octet, OWN), (BEFORE, before, before_octet, OWN + 1)):
-        table = jnp.concatenate([rows, octet, jnp.zeros_like(octet)], axis=0).astype(BF16)
-        values = spread(table, row_of_slot(p, OWN, cx, block), kinds, cx)
+    for slot, rows, octet, side in ((AFTER, after, after_octet, 0), (BEFORE, before, before_octet, 1)):
+        wide = [pltpu.roll(rows, lanes - part * 2 * H * kinds, 1) if part else rows for part in range(parts)]
+        table = jnp.concatenate(wide + [octet, jnp.zeros_like(octet)], axis=0).astype(BF16)
+        values = spread(table, block + side * H * kinds, kinds, H)
         for kind, value in enumerate(terms_of(values)):
             coef[slot, kind, :cy, :] = value[:cy] * row_in[slot]
             coef[slot, kind, cy : cy + 8, :] = value[cy : cy + 8] * (col_in * row_in[slot])
 
-    def operator(src, rows, first_row, length, shifted, strips, emit):
-        lane = iota((length, lanes), 1)
-        in_first, in_last = lane < nv, lane >= lanes - nv
-        masked = shifted is not None
-
-        def at(slot, c):
-            return src[slot, c, rows(0), :]
-
-        def up_of(slot, c):
-            if 0 < slot < OWN:
-                return at(slot - 1, c)
-            if slot in (0, AFTER):
-                return pltpu.roll(jnp.where(in_last, at(BEFORE if slot == 0 else OWN - 1, c), at(OWN - 1 if slot == 0 else AFTER, c)), nv, 1)
-            if slot == HEAD:
-                return pltpu.roll(jnp.where(in_last, at(BEFORE, c), at(HEAD, c)), nv, 1)
-            return jnp.where(in_first, 0.0, pltpu.roll(at(slot, c), nv, 1))
-
-        def down_of(slot, c):
-            if slot < OWN - 1:
-                return at(slot + 1, c)
-            if slot in (OWN - 1, BEFORE):
-                return pltpu.roll(jnp.where(in_first, at(AFTER if slot == OWN - 1 else 0, c), at(0 if slot == OWN - 1 else BEFORE, c)), lanes - nv, 1)
-            if slot == TAIL:
-                return pltpu.roll(jnp.where(in_first, at(AFTER, c), at(TAIL, c)), lanes - nv, 1)
-            return jnp.where(in_last, 0.0, pltpu.roll(at(slot, c), lanes - nv, 1))
-
-        for slot in range(TAIL + 1 if strips else AFTER + 1):
-            v = [at(slot, c) for c in range(comps)]
-            weight = [coef[slot, kind, first_row, :] for kind in range(kinds)]
-            total = weight[comps] * (v[0] + v[1] + v[2])
-            for c in range(comps):
-                if masked:
-                    sides = shifted(slot, c)
-                else:
-                    sides = src[slot, c, rows(-1), :] + src[slot, c, rows(1), :]
-                beside = sides + (up_of(slot, c) + down_of(slot, c))
-                inside = row_in.get(slot)
-                if masked:
-                    beside = beside * (col_in if inside is None else col_in * inside)
-                elif inside is not None:
-                    beside = beside * inside
-                emit(slot, c, weight[c] * v[c] + total - beside)
-
-    def apply(src, strips, emit_rows, emit_margin):
-        def body(j, carry):
-            base = 16 * j
-
-            def rows(d):
-                start = 8 + base + d
-                return pl.ds(pl.multiple_of(start, 8) if d == 0 else start, 16)
-
-            def emit(slot, c, value):
-                emit_rows(slot, c, pl.multiple_of(base, 16), value)
-
-            operator(src, rows, pl.ds(pl.multiple_of(base, 16), 16), 16, None, strips, emit)
-            return carry
-
-        lax.fori_loop(0, cy // 16, body, 0, unroll=True)
-
-        def shifted(slot, c):
+    everything = range(TAIL + 1)
+
+    def apply(src, row_slots, margin_slots, emit_rows, emit_margin):
+        operator_rows(src, coef, nv, row_slots, True, row_in.get, emit_rows)
+
+        def sides_of(slot, c):
             left = jnp.where(octet_row == H, 0.0, src[slot, c, 7 + cy : 15 + cy, :])
             return left + jnp.where(octet_row == H - 1, 0.0, src[slot, c, 1:9, :])
 
-        operator(src, lambda d: top, slice(cy, cy + 8), 8, shifted, strips, emit_margin)
+        def inside_of(slot):
+            return col_in * row_in[slot] if slot in row_in else col_in
+
+        operator(src, coef, nv, top, slice(cy, cy + 8), sides_of, margin_slots, True, inside_of, emit_margin)
 
     def store(dst, split_too=False):
         def emit_rows(slot, c, base, value):
-            dst[slot, c, pl.ds(base + 8, 16), :] = value
+            dst[slot, c, 8 + base : 24 + base, :] = value
             if split_too and slot < HEAD:
-                high2[slot, c, pl.ds(base, 16), :], low2[slot, c, pl.ds(base, 16), :] = split(value)
+                high2[slot, c, base : base + 16, :], low2[slot, c, base : base + 16, :] = split(value)
 
         def emit_margin(slot, c, value):
             dst[slot, c, low, :] = value
@@ -295,11 +327,23 @@
 
         return emit_rows, emit_margin
 
-    apply(v0, True, *store(x1))
-    apply(x1, True, *store(x2, True))
+    lane = iota((16, lanes), 1)
+    for c in range(comps):
+        for base in range(8, 8 + cy, 16):
+            rows = slice(base, base + 16)
+            before = jnp.where(lane < nv, pltpu.roll(v0[BEFORE, c, rows, :], nv, 1), 0.0)
+            after = jnp.where(lane >= lanes - nv, pltpu.roll(v0[AFTER, c, rows, :], lanes - nv, 1), 0.0)
+            for slot, part in ((0, before), (HEAD, before), (OWN - 1, after), (TAIL, after)):
+                x1[slot, c, rows, :] = x1[slot, c, rows, :] - part
+        for slot in everything:
+            if slot not in row_in:
+                for row, beside in ((8, 7), (7 + cy, 8 + cy)):
+                    x1[slot, c, row : row + 1, :] = x1[slot, c, row : row + 1, :] - v0[slot, c, beside : beside + 1, :]
+    apply(v0, (BEFORE, AFTER), everything, *store(x1))
+    apply(x1, everything, everything, *store(x2, True))
 
     def split_rows(slot, c, base, value):
-        high3[slot, c, pl.ds(base, 16), :], low3[slot, c, pl.ds(base, 16), :] = split(value)
+        high3[slot, c, base : base + 16, :], low3[slot, c, base : base + 16, :] = split(value)
 
     def keep_margin(slot, c, value):
         margin3[slot, c] = value
@@ -336,7 +380,7 @@
         return main[:, :nv] + main[:, lanes : lanes + nv] + fold(cross)[:, :nv]
 
     gram = gram_m()
-    apply(x2, False, split_rows, keep_margin)
+    apply(x2, range(HEAD), range(HEAD), split_rows, keep_margin)
     pad = jnp.zeros((nv, lanes - nv), F32)
     inverse = inverse_factor(jnp.concatenate([gram, pad], axis=1), nv)[:, :nv]
     inverse = jnp.where(iota((nv, nv), 0) < rank_ref[0, 0], inverse, 0.0)
@@ -501,10 +545,10 @@
     pieces = (cx // H + 2) * comps + 1
     inputs = (start_vectors, stiffness, coupling, level_start.T)
     sec_shape = shape((-(-pieces // 2) * 8, cy), BF16)
-    own, kt, sec_a, sec_b, start = call(
+    own, kt, sec_a, sec_b, start, narrow = call(
         pack_kernel,
         (shape((cx // H + 2, comps, cy, H * nv), BF16), shape((cy, channels * cx), BF16), sec_shape, sec_shape)
-        + (shape((k2, nv), F32),),
+        + (shape((k2, nv), F32), shape((2 * H * channels * cy // (H * nv), cy), BF16)),
         [
             pltpu.VMEM((comps, nv, cx, cy), BF16),
             pltpu.VMEM(stiffness.shape, BF16),
@@ -518,8 +562,12 @@
     )(*(pltpu.with_memory_space_constraint(x, pltpu.HBM) for x in inputs))
     sec_a = lax.ppermute(sec_a, "sec", pairs(sects, 0))
     sec_b = lax.ppermute(sec_b, "sec", pairs(sects, 1))
-    sub_shape = shape((channels * (cy + 8), H * nv), BF16)
-    sub_a, sub_b = call(edge_kernel, (sub_shape, sub_shape), [], "edge")(own, kt, sec_a, sec_b)
+
+    def edge(*refs):
+        edge_kernel(cx, *refs)
+
+    sub_shape = shape((comps * cy + narrow.shape[0] + channels * 8, H * nv), BF16)
+    sub_a, sub_b = call(edge, (sub_shape, sub_shape), [], "edge")(own, narrow, sec_a, sec_b)
     sub_a = lax.ppermute(sub_a, "sub", pairs(spans, 0))
     sub_b = lax.ppermute(sub_b, "sub", pairs(spans, 1))
 
@@ -529,21 +577,20 @@
     rows = shape((slots, comps, cy + 16, H * nv), F32)
     weights = shape((slots, channels, cy + 8, H * nv), F32)
     half = shape((slots - 2, comps, cy, H * nv), BF16)
-    v0, coef = (in_vmem(x) for x in call(prep_kernel, (rows, weights), [], "prep")(own, kt))
-    pack, high, low, _, _ = call(
+    v0, coef, x1 = (in_vmem(x) for x in call(prep_kernel, (rows, weights, rows), [], "prep")(own, kt))
+    pack, high, low, *_ = call(
         fine,
-        (shape((1, nv + 8, cy), F32), half, half, rows, weights),
+        (shape((1, nv + 8, cy), F32), half, half, rows, weights, rows),
         [
-            pltpu.VMEM(rows.shape, F32),
             pltpu.VMEM(rows.shape, F32),
             pltpu.VMEM(half.shape, BF16),
             pltpu.VMEM(half.shape, BF16),
             pltpu.VMEM((slots - 2, comps, 8, H * nv), F32),
         ],
         "fine",
-        [pl.BlockSpec(memory_space=pltpu.SMEM)] + [vmem] * 8,
-        input_output_aliases={2: 3, 3: 4},
-    )(kept_ranks, start, v0, coef, kt, sec_a, sec_b, sub_a, sub_b)
+        [pl.BlockSpec(memory_space=pltpu.SMEM)] + [vmem] * 9,
+        input_output_aliases={2: 3, 3: 4, 4: 5},
+    )(kept_ranks, start, v0, coef, x1, kt, sec_a, sec_b, sub_a, sub_b)
 
     factor = math.sqrt(spans * comps * (cx + 2 * H) * (cy + 2 * H))
     result = shape((k2, comps, cx, cy), F32)

time: 37.7 us -> 36.8 us (0.976)
  waiting for transfers between devices: 10.6 us -> 9.79 us
    ppermute x1, waiting for transfers between devices: 1.59 us -> 0.73 us  [on_device(): sub_a = lax.ppermute(sub_a, 'sub', pairs(spans, 0))]
  transfers between devices with their start and end apart: 8 -> 8, of which waited for: 6 -> 6; matrix products, arithmetic and copies ran while one was open for 0% -> 0% of each run, Pallas kernels for 2% -> 3%
where the time goes in v5:
time: 36.8 us; the launch traced here: 36.6 us
  starting transfers between devices  14.7 us (40%)
  Pallas kernels  11.4 us (31%)
  waiting for transfers between devices  9.79 us (27%)
  between operations  0.71 us (2%)
    ppermute x4, starting transfers between devices, swapped(): return lax.ppermute(block, 'sub', [(i, i ^ bit) for i in range(spans)])  10.5 us
    ppermute x4, waiting for transfers between devices, swapped(): return lax.ppermute(block, 'sub', [(i, i ^ bit) for i in range(spans)])  5.76 us
    pallas_call x1, Pallas kernels, on_device(): call(fine, (shape((1, nv + 8, cy), F32), half, half, rows, weights, rows)...  4.97 us
    pallas_call x1, Pallas kernels, on_device(): call(level, result, [packs] + tiles, 'level', [vmem] * 6, out_specs=hbm)  3.41 us
    ppermute x1, waiting for transfers between devices, on_device(): sec_b = lax.ppermute(sec_b, 'sec', pairs(sects, 1))  3.29 us
    ppermute x1, starting transfers between devices, on_device(): sec_b = lax.ppermute(sec_b, 'sec', pairs(sects, 1))  1.92 us
    pallas_call x1, Pallas kernels, on_device(): call(pack_kernel, (shape((cx // H + 2, comps, cy, H * nv), BF16), shape((...  1.72 us
    ppermute x1, starting transfers between devices, on_device(): sub_a = lax.ppermute(sub_a, 'sub', pairs(spans, 0))  1.53 us
  transfers between devices with their start and end apart: 8, of which 6 were waited for; matrix products, arithmetic and copies ran while one was open for 0% of the time, Pallas kernels for 3%

profile of v5, /device:TPU:2, one launch (start us, length us, event | category | flops | bytes accessed | tf_op | source)
XLA Modules:
  0.0 36.6 jit_solution(18175390320598386535)
XLA Ops:
  0.0 1.7 %pack.1 = (bf16[10,3,128,128]{3,2,1,0:T(8,128)(2,1)S(1)}, bf16[128,128]{1,0:T(8,128)(2,1)S(1)}, bf16[128,128]{1,0:T(8,128)(2,1)S(1)}, bf16[128,128]{1,0:T(8,128)...) custom-call(bf16[32,3,32,128]{3,2,1,0:T(8,128)(2,1)} %v_hbm.1, bf16[3,32,128]{2,1,0:T(8,128)(2,1)} %k_hbm.1, ...), custom_call_target="tpu_custom_call" | custom-call | tf_op jit(solution)/shard_map/pack/pallas_call | solution.py:548
  1.7 0.1 collective-permute-start
  1.8 1.9 %collective-permute-start.1 = (bf16[128,128]{1,0:T(8,128)(2,1)S(1)}, bf16[128,128]{1,0:T(8,128)(2,1)S(1)}, u32[]{:S(2)}, u32[]{:S(2)}) collective-permute-start(bf16[128,128]{1,0:T(8,128)(2,1)S(1)} %get-tuple-element.26), channel_id=1, source_target_pairs={{1,2},{2,1},{5,6},{6,5},{9,10},{10,9},{13,14},{14,13},{17,18},{18,... | collective-permute-start | bytes 98312 | tf_op jit(solution)/shard_map/ppermute | solution.py:564
  3.7 0.0 collective-permute-done.refs_2_.refs_6_
  3.7 3.3 %collective-permute-done.1.refs_3_.refs_7_ = bf16[128,128]{1,0:T(8,128)(2,1)S(1)} collective-permute-done((bf16[128,128]{1,0:T(8,128)(2,1)S(1)}, bf16[128,128]{1,0:T(8,128)(2,1)S(1)}, u32[]{:S(2)}, u32[]{:S(2)}) %collective-permute-start.1) | collective-permute-done | bytes 32800 | tf_op jit(solution)/shard_map/ppermute | solution.py:564
  7.0 0.1 edge.1
  7.1 1.5 %collective-permute-start.2 = (bf16[448,128]{1,0:T(8,128)(2,1)S(1)}, bf16[448,128]{1,0:T(8,128)(2,1)S(1)}, u32[]{:S(2)}, u32[]{:S(2)}) collective-permute-start(bf16[448,128]{1,0:T(8,128)(2,1)S(1)} %get-tuple-element.28), channel_id=1, source_target_pairs={{0,4},{4,0},{8,12},{12,8},{16,20},{20,16},{24,28},{28,24},{1,5},{5... | collective-permute-start | bytes 344072 | tf_op jit(solution)/shard_map/ppermute | solution.py:571
  8.7 0.7 %collective-permute-start.3 = (bf16[448,128]{1,0:T(8,128)(2,1)S(1)}, bf16[448,128]{1,0:T(8,128)(2,1)S(1)}, u32[]{:S(2)}, u32[]{:S(2)}) collective-permute-start(bf16[448,128]{1,0:T(8,128)(2,1)S(1)} %get-tuple-element.29), channel_id=1, source_target_pairs={{4,8},{8,4},{12,16},{16,12},{20,24},{24,20},{5,9},{9,5},{13,17},{1... | collective-permute-start | bytes 344072 | tf_op jit(solution)/shard_map/ppermute | solution.py:572
  10.0 1.2 %prep.1 = (f32[12,3,144,128]{3,2,1,0:T(8,128)S(1)}, f32[12,4,136,128]{3,2,1,0:T(8,128)S(1)}, f32[12,3,144,128]{3,2,1,0:T(8,128)S(1)}) custom-call(bf16[10,3,128,128]{3,2,1,0:T(8,128)(2,1)S(1)} %get-tuple-element.20.own_ref.refs_0_, bf16[128,128]{1,0:T(8,128)(2,1)S(1)} %get-tuple-element.21.kt_ref.refs_5_), custom_call_target="tpu_custom_call" | custom-call | tf_op jit(solution)/shard_map/prep/pallas_call | solution.py:580
  11.2 0.7 %collective-permute-done.2.refs_8_ = bf16[448,128]{1,0:T(8,128)(2,1)S(1)} collective-permute-done((bf16[448,128]{1,0:T(8,128)(2,1)S(1)}, bf16[448,128]{1,0:T(8,128)(2,1)S(1)}, u32[]{:S(2)}, u32[]{:S(2)}) %collective-permute-start.2) | collective-permute-done | bytes 114720 | tf_op jit(solution)/shard_map/ppermute | solution.py:571
  11.9 0.0 collective-permute-done.3.refs_9_
  11.9 5.0 %fine.1 = (f32[1,40,128]{2,1,0:T(8,128)S(1)}, bf16[10,3,128,128]{3,2,1,0:T(8,128)(2,1)S(1)}, bf16[10,3,128,128]{3,2,1,0:T(8,128)(2,1)S(1)}, f32[12,3,144,128]{3,...) custom-call(s32[1,1]{1,0:T(1,128)S(6)} %copy.13.refs_0_, ...), custom_call_target="tpu_custom_call", output_to_operand_aliasing={{3}: (2, {}), {4}: (3, {}), {5}: (4, {})} | custom-call | tf_op jit(solution)/shard_map/fine/pallas_call | solution.py:581
  16.9 6.9 %collective-permute-start.4 = (f32[1,40,128]{2,1,0:T(8,128)S(1)}, f32[1,40,128]{2,1,0:T(8,128)S(1)}, u32[]{:S(2)}, u32[]{:S(2)}) collective-permute-start(f32[1,40,128]{2,1,0:T(8,128)S(1)} %get-tuple-element.30), channel_id=1, source_target_pairs={{0,16},{4,20},{8,24},{12,28},{16,0},{20,4},{24,8},{28,12},{1,17},{... | collective-permute-start | bytes 61448 | tf_op jit(solution)/shard_map/ppermute | solution.py:607
  23.9 1.8 %collective-permute-done.4 = f32[1,40,128]{2,1,0:T(8,128)S(1)} collective-permute-done((f32[1,40,128]{2,1,0:T(8,128)S(1)}, f32[1,40,128]{2,1,0:T(8,128)S(1)}, u32[]{:S(2)}, u32[]{:S(2)}) %collective-permute-start.4) | collective-permute-done | bytes 20512 | tf_op jit(solution)/shard_map/ppermute | solution.py:607
  25.6 2.1 %collective-permute-start.7 = (f32[2,40,128]{2,1,0:T(8,128)S(1)}, f32[2,40,128]{2,1,0:T(8,128)S(1)}, u32[]{:S(2)}, u32[]{:S(2)}) collective-permute-start(f32[2,40,128]{2,1,0:T(8,128)S(1)} %constant_dynamic-update-slice_fusion.refs_0_), channel_id=1, source_target_pairs={{0,12},{4,8},{8,4},{12,0},{16,28},{20,24},{24,20},{28,16},{1,13},{... | collective-permute-start | bytes 122888 | tf_op jit(solution)/shard_map/ppermute | solution.py:607
  27.7 1.5 %collective-permute-start.6 = (f32[2,40,128]{2,1,0:T(8,128)S(1)}, f32[2,40,128]{2,1,0:T(8,128)S(1)}, u32[]{:S(2)}, u32[]{:S(2)}) collective-permute-start(f32[2,40,128]{2,1,0:T(8,128)S(1)} %constant_dynamic-update-slice_fusion.refs_0_), channel_id=1, source_target_pairs={{0,4},{4,0},{8,12},{12,8},{16,20},{20,16},{24,28},{28,24},{1,5},{5... | collective-permute-start | bytes 122888 | tf_op jit(solution)/shard_map/ppermute | solution.py:607
  29.2 0.0 collective-permute-start.5
  29.2 1.3 %collective-permute-done.7.refs_3_ = f32[2,40,128]{2,1,0:T(8,128)S(1)} collective-permute-done((f32[2,40,128]{2,1,0:T(8,128)S(1)}, f32[2,40,128]{2,1,0:T(8,128)S(1)}, u32[]{:S(2)}, u32[]{:S(2)}) %collective-permute-start.7) | collective-permute-done | bytes 40992 | tf_op jit(solution)/shard_map/ppermute | solution.py:607
  30.5 1.2 %collective-permute-done.6.refs_2_ = f32[2,40,128]{2,1,0:T(8,128)S(1)} collective-permute-done((f32[2,40,128]{2,1,0:T(8,128)S(1)}, f32[2,40,128]{2,1,0:T(8,128)S(1)}, u32[]{:S(2)}, u32[]{:S(2)}) %collective-permute-start.6) | collective-permute-done | bytes 40992 | tf_op jit(solution)/shard_map/ppermute | solution.py:607
  31.7 1.5 %collective-permute-done.5.refs_1_ = f32[2,40,128]{2,1,0:T(8,128)S(1)} collective-permute-done((f32[2,40,128]{2,1,0:T(8,128)S(1)}, f32[2,40,128]{2,1,0:T(8,128)S(1)}, u32[]{:S(2)}, u32[]{:S(2)}) %collective-permute-start.5) | collective-permute-done | bytes 40992 | tf_op jit(solution)/shard_map/ppermute | solution.py:607
  33.2 3.4 %level.1 = f32[16,3,32,128]{3,2,1,0:T(8,128)} custom-call(f32[2,40,128]{2,1,0:T(8,128)S(1)} %constant_dynamic-update-slice_fusion.refs_0_, f32[2,40,128]{2,1,0:T(8,128)S(1)} %collective-permute-done.5.refs_1_, f32[2,40,128]{2,1,0:T(8,128)S(1)} %collective-permute-done.6.refs_2_, f32[2,40,128]{2,1,0:T(8,128)S(1)} %collective-permute-done.7.refs_3_, ...), custom_call_target="tpu_custom_call" | custom-call | tf_op jit(solution)/shard_map/level/pallas_call | solution.py:618
  (2 shorter events, 0.0 us)
Async XLA Ops:
  1.7 2.0 %collective-permute-start = (bf16[128,128]{1,0:T(8,128)(2,1)S(1)}, bf16[128,128]{1,0:T(8,128)(2,1)S(1)}, u32[]{:S(2)}, u32[]{:S(2)}) collective-permute-start(bf16[128,128]{1,0:T(8,128)(2,1)S(1)} %get-tuple-element.25), channel_id=1, source_target_pairs={{0,1},{1,0},{2,3},{3,2},{4,5},{5,4},{6,7},{7,6},{8,9},{9,8},{10,11... | collective-permute-start | bytes 98312 | tf_op jit(solution)/shard_map/ppermute | solution.py:563
  1.8 5.2 %collective-permute-start.1 = (bf16[128,128]{1,0:T(8,128)(2,1)S(1)}, bf16[128,128]{1,0:T(8,128)(2,1)S(1)}, u32[]{:S(2)}, u32[]{:S(2)}) collective-permute-start(bf16[128,128]{1,0:T(8,128)(2,1)S(1)} %get-tuple-element.26), channel_id=1, source_target_pairs={{1,2},{2,1},{5,6},{6,5},{9,10},{10,9},{13,14},{14,13},{17,18},{18,... | collective-permute-start | bytes 98312 | tf_op jit(solution)/shard_map/ppermute | solution.py:564
  7.1 4.8 %collective-permute-start.2 = (bf16[448,128]{1,0:T(8,128)(2,1)S(1)}, bf16[448,128]{1,0:T(8,128)(2,1)S(1)}, u32[]{:S(2)}, u32[]{:S(2)}) collective-permute-start(bf16[448,128]{1,0:T(8,128)(2,1)S(1)} %get-tuple-element.28), channel_id=1, source_target_pairs={{0,4},{4,0},{8,12},{12,8},{16,20},{20,16},{24,28},{28,24},{1,5},{5... | collective-permute-start | bytes 344072 | tf_op jit(solution)/shard_map/ppermute | solution.py:571
  8.7 3.3 %collective-permute-start.3 = (bf16[448,128]{1,0:T(8,128)(2,1)S(1)}, bf16[448,128]{1,0:T(8,128)(2,1)S(1)}, u32[]{:S(2)}, u32[]{:S(2)}) collective-permute-start(bf16[448,128]{1,0:T(8,128)(2,1)S(1)} %get-tuple-element.29), channel_id=1, source_target_pairs={{4,8},{8,4},{12,16},{16,12},{20,24},{24,20},{5,9},{9,5},{13,17},{1... | collective-permute-start | bytes 344072 | tf_op jit(solution)/shard_map/ppermute | solution.py:572
  16.9 8.7 %collective-permute-start.4 = (f32[1,40,128]{2,1,0:T(8,128)S(1)}, f32[1,40,128]{2,1,0:T(8,128)S(1)}, u32[]{:S(2)}, u32[]{:S(2)}) collective-permute-start(f32[1,40,128]{2,1,0:T(8,128)S(1)} %get-tuple-element.30), channel_id=1, source_target_pairs={{0,16},{4,20},{8,24},{12,28},{16,0},{20,4},{24,8},{28,12},{1,17},{... | collective-permute-start | bytes 61448 | tf_op jit(solution)/shard_map/ppermute | solution.py:607
  25.6 4.9 %collective-permute-start.7 = (f32[2,40,128]{2,1,0:T(8,128)S(1)}, f32[2,40,128]{2,1,0:T(8,128)S(1)}, u32[]{:S(2)}, u32[]{:S(2)}) collective-permute-start(f32[2,40,128]{2,1,0:T(8,128)S(1)} %constant_dynamic-update-slice_fusion.refs_0_), channel_id=1, source_target_pairs={{0,12},{4,8},{8,4},{12,0},{16,28},{20,24},{24,20},{28,16},{1,13},{... | collective-permute-start | bytes 122888 | tf_op jit(solution)/shard_map/ppermute | solution.py:607
  27.7 4.0 %collective-permute-start.6 = (f32[2,40,128]{2,1,0:T(8,128)S(1)}, f32[2,40,128]{2,1,0:T(8,128)S(1)}, u32[]{:S(2)}, u32[]{:S(2)}) collective-permute-start(f32[2,40,128]{2,1,0:T(8,128)S(1)} %constant_dynamic-update-slice_fusion.refs_0_), channel_id=1, source_target_pairs={{0,4},{4,0},{8,12},{12,8},{16,20},{20,16},{24,28},{28,24},{1,5},{5... | collective-permute-start | bytes 122888 | tf_op jit(solution)/shard_map/ppermute | solution.py:607
  29.2 4.0 %collective-permute-start.5 = (f32[2,40,128]{2,1,0:T(8,128)S(1)}, f32[2,40,128]{2,1,0:T(8,128)S(1)}, u32[]{:S(2)}, u32[]{:S(2)}) collective-permute-start(f32[2,40,128]{2,1,0:T(8,128)S(1)} %constant_dynamic-update-slice_fusion.refs_0_), channel_id=1, source_target_pairs={{0,8},{4,12},{8,0},{12,4},{16,24},{20,28},{24,16},{28,20},{1,9},{5... | collective-permute-start | bytes 122888 | tf_op jit(solution)/shard_map/ppermute | solution.py:607

commit v6 on v5

--- a/solution.py
+++ b/solution.py
@@ -248,7 +248,7 @@
     operator_rows(v0, coef, lanes // H, mine, False, lambda slot: None, emit)
 
 
-def fine_kernel(sizes, rank_ref, start_ref, v0_in, coef_in, x1_in, kt_ref, sec_a, sec_b, sub_a, sub_b, pack_ref, high2, low2, v0, coef, x1, x2, high3, low3, margin3):
+def fine_kernel(sizes, rank_ref, start_ref, v0_in, coef_in, x1_in, kt_ref, sec_a, sec_b, sub_a, sub_b, pack_ref, high2, low2, v0, coef, x1, x2, twice, turned, high3, low3, margin3):
     spans, sects = sizes
     _, comps, cy, lanes = high2.shape
     nv = start_ref.shape[1]
@@ -315,17 +315,32 @@
 
         operator(src, coef, nv, top, slice(cy, cy + 8), sides_of, margin_slots, True, inside_of, emit_margin)
 
-    def store(dst, split_too=False):
-        def emit_rows(slot, c, base, value):
-            dst[slot, c, 8 + base : 24 + base, :] = value
-            if split_too and slot < HEAD:
-                high2[slot, c, base : base + 16, :], low2[slot, c, base : base + 16, :] = split(value)
-
-        def emit_margin(slot, c, value):
-            dst[slot, c, low, :] = value
-            dst[slot, c, top, :] = value
-
-        return emit_rows, emit_margin
+    def put_margin(dst, slot, c, value):
+        dst[slot, c, low, :] = value
+        dst[slot, c, top, :] = value
+
+    def store_rows(slot, c, base, value):
+        x1[slot, c, 8 + base : 24 + base, :] = value
+
+    def store_margin(slot, c, value):
+        put_margin(x1, slot, c, value)
+
+    def residual(value):
+        return value - value.astype(BF16).astype(F32)
+
+    def split_rows(slot, c, base, value):
+        rows = slice(8 + base, 24 + base)
+        if slot < HEAD:
+            rest = residual(value)
+            high2[slot, c, base : base + 16, :], low2[slot, c, base : base + 16, :] = value.astype(BF16), rest.astype(BF16)
+            twice[slot, c, rows, :] = value + rest
+        else:
+            x2[slot, c, rows, :] = value
+
+    def split_margin(slot, c, value):
+        x2[slot, c, top, :] = value
+        if slot < HEAD:
+            put_margin(twice, slot, c, value + residual(value))
 
     lane = iota((16, lanes), 1)
     for c in range(comps):
@@ -339,10 +354,10 @@
             if slot not in row_in:
                 for row, beside in ((8, 7), (7 + cy, 8 + cy)):
                     x1[slot, c, row : row + 1, :] = x1[slot, c, row : row + 1, :] - v0[slot, c, beside : beside + 1, :]
-    apply(v0, (BEFORE, AFTER), everything, *store(x1))
-    apply(x1, everything, everything, *store(x2, True))
-
-    def split_rows(slot, c, base, value):
+    apply(v0, (BEFORE, AFTER), everything, store_rows, store_margin)
+    apply(x1, everything, everything, split_rows, split_margin)
+
+    def image_rows(slot, c, base, value):
         high3[slot, c, base : base + 16, :], low3[slot, c, base : base + 16, :] = split(value)
 
     def keep_margin(slot, c, value):
@@ -358,29 +373,28 @@
     octet_margins = [x2[slot, c, top, :] for slot in range(AFTER + 1) for c in range(comps)]
     margin_h2, margin_l2 = split(jnp.concatenate(octet_margins, axis=0))
 
+    def product(other):
+        margin, rows = other
+        main = dot(margin_h2, jnp.concatenate(margin, axis=1), TN)
+        for first in chunks:
+            both = jnp.concatenate([flat(ref, first, 2) for ref in rows], axis=1)
+            main = main + dot(turned[first // 2], both, NN)
+        main = fold(main)
+        return main[:, :nv], main[:, lanes : lanes + nv]
+
     def gram_m():
-        def part(h2, l2):
-            return dot(h2, jnp.concatenate([h2, l2], axis=1), TN)
-        main = part(margin_h2, margin_l2)
         for first in chunks:
-            main = main + part(flat(high2, first, 2), flat(low2, first, 2))
-        main = fold(main)
-        mixed = main[:, lanes : lanes + nv]
-        return main[:, :nv] + (mixed + mixed.T)
+            turned[first // 2] = flat(high2, first, 2).T
+        main, mixed = product(((margin_h2, margin_l2), (high2, low2)))
+        return main + (mixed + mixed.T)
 
     def gram_n():
-        def part(h2, l2, h3, l3):
-            return dot(h2, jnp.concatenate([h3, l3], axis=1), TN), dot(l2, h3, TN)
-        h3, l3 = split(margin3[...].reshape((AFTER + 1) * comps * 8, lanes))
-        main, cross = part(margin_h2, margin_l2, h3, l3)
-        for first in chunks:
-            more = part(*(flat(ref, first, 2) for ref in (high2, low2, high3, low3)))
-            main, cross = main + more[0], cross + more[1]
-        main = fold(main)
-        return main[:, :nv] + main[:, lanes : lanes + nv] + fold(cross)[:, :nv]
+        margin = split(margin3[...].reshape((AFTER + 1) * comps * 8, lanes))
+        out = sum(product((margin, (high3, low3))))
+        return 0.5 * (out + out.T)
 
     gram = gram_m()
-    apply(x2, range(HEAD), range(HEAD), split_rows, keep_margin)
+    apply(twice, range(HEAD), range(HEAD), image_rows, keep_margin)
     pad = jnp.zeros((nv, lanes - nv), F32)
     inverse = inverse_factor(jnp.concatenate([gram, pad], axis=1), nv)[:, :nv]
     inverse = jnp.where(iota((nv, nv), 0) < rank_ref[0, 0], inverse, 0.0)
@@ -583,6 +597,8 @@
         (shape((1, nv + 8, cy), F32), half, half, rows, weights, rows),
         [
             pltpu.VMEM(rows.shape, F32),
+            pltpu.VMEM(rows.shape, F32),
+            pltpu.VMEM(((slots - 2) // 2, H * nv, 2 * comps * cy), BF16),
             pltpu.VMEM(half.shape, BF16),
             pltpu.VMEM(half.shape, BF16),
             pltpu.VMEM((slots - 2, comps, 8, H * nv), F32),

time: 36.8 us -> 36.4 us (0.989)
  Pallas kernels: 11.4 us -> 11 us
    pallas_call x1, Pallas kernels: 4.97 us -> 4.58 us  [on_device(): call(fine, (shape((1, nv + 8, cy), F32), half, half, rows, weights, rows)...]
where the time goes in v6:
time: 36.4 us; the launch traced here: 36.2 us
  starting transfers between devices  14.7 us (40%)
  Pallas kernels  11 us (30%)
  waiting for transfers between devices  9.79 us (27%)
  between operations  0.71 us (2%)
    ppermute x4, starting transfers between devices, swapped(): return lax.ppermute(block, 'sub', [(i, i ^ bit) for i in range(spans)])  10.5 us
    ppermute x4, waiting for transfers between devices, swapped(): return lax.ppermute(block, 'sub', [(i, i ^ bit) for i in range(spans)])  5.76 us
    pallas_call x1, Pallas kernels, on_device(): call(fine, (shape((1, nv + 8, cy), F32), half, half, rows, weights, rows)...  4.58 us
    pallas_call x1, Pallas kernels, on_device(): call(level, result, [packs] + tiles, 'level', [vmem] * 6, out_specs=hbm)  3.41 us
    ppermute x1, waiting for transfers between devices, on_device(): sec_b = lax.ppermute(sec_b, 'sec', pairs(sects, 1))  3.29 us
    ppermute x1, starting transfers between devices, on_device(): sec_b = lax.ppermute(sec_b, 'sec', pairs(sects, 1))  1.92 us
    pallas_call x1, Pallas kernels, on_device(): call(pack_kernel, (shape((cx // H + 2, comps, cy, H * nv), BF16), shape((...  1.72 us
    ppermute x1, starting transfers between devices, on_device(): sub_a = lax.ppermute(sub_a, 'sub', pairs(spans, 0))  1.53 us
  transfers between devices with their start and end apart: 8, of which 6 were waited for; matrix products, arithmetic and copies ran while one was open for 0% of the time, Pallas kernels for 3%

profile of v6, /device:TPU:2, one launch (start us, length us, event | category | flops | bytes accessed | tf_op | source)
XLA Modules:
  0.0 36.2 jit_solution(3171895440586640658)
XLA Ops:
  0.0 1.7 %pack.1 = (bf16[10,3,128,128]{3,2,1,0:T(8,128)(2,1)S(1)}, bf16[128,128]{1,0:T(8,128)(2,1)S(1)}, bf16[128,128]{1,0:T(8,128)(2,1)S(1)}, bf16[128,128]{1,0:T(8,128)...) custom-call(bf16[32,3,32,128]{3,2,1,0:T(8,128)(2,1)} %v_hbm.1, bf16[3,32,128]{2,1,0:T(8,128)(2,1)} %k_hbm.1, ...), custom_call_target="tpu_custom_call" | custom-call | tf_op jit(solution)/shard_map/pack/pallas_call | solution.py:562
  1.7 0.1 collective-permute-start
  1.8 1.9 %collective-permute-start.1 = (bf16[128,128]{1,0:T(8,128)(2,1)S(1)}, bf16[128,128]{1,0:T(8,128)(2,1)S(1)}, u32[]{:S(2)}, u32[]{:S(2)}) collective-permute-start(bf16[128,128]{1,0:T(8,128)(2,1)S(1)} %get-tuple-element.26), channel_id=1, source_target_pairs={{1,2},{2,1},{5,6},{6,5},{9,10},{10,9},{13,14},{14,13},{17,18},{18,... | collective-permute-start | bytes 98312 | tf_op jit(solution)/shard_map/ppermute | solution.py:578
  3.7 0.0 collective-permute-done.refs_2_.refs_6_
  3.7 3.3 %collective-permute-done.1.refs_3_.refs_7_ = bf16[128,128]{1,0:T(8,128)(2,1)S(1)} collective-permute-done((bf16[128,128]{1,0:T(8,128)(2,1)S(1)}, bf16[128,128]{1,0:T(8,128)(2,1)S(1)}, u32[]{:S(2)}, u32[]{:S(2)}) %collective-permute-start.1) | collective-permute-done | bytes 32800 | tf_op jit(solution)/shard_map/ppermute | solution.py:578
  7.0 0.1 edge.1
  7.1 1.5 %collective-permute-start.2 = (bf16[448,128]{1,0:T(8,128)(2,1)S(1)}, bf16[448,128]{1,0:T(8,128)(2,1)S(1)}, u32[]{:S(2)}, u32[]{:S(2)}) collective-permute-start(bf16[448,128]{1,0:T(8,128)(2,1)S(1)} %get-tuple-element.28), channel_id=1, source_target_pairs={{0,4},{4,0},{8,12},{12,8},{16,20},{20,16},{24,28},{28,24},{1,5},{5... | collective-permute-start | bytes 344072 | tf_op jit(solution)/shard_map/ppermute | solution.py:585
  8.7 0.7 %collective-permute-start.3 = (bf16[448,128]{1,0:T(8,128)(2,1)S(1)}, bf16[448,128]{1,0:T(8,128)(2,1)S(1)}, u32[]{:S(2)}, u32[]{:S(2)}) collective-permute-start(bf16[448,128]{1,0:T(8,128)(2,1)S(1)} %get-tuple-element.29), channel_id=1, source_target_pairs={{4,8},{8,4},{12,16},{16,12},{20,24},{24,20},{5,9},{9,5},{13,17},{1... | collective-permute-start | bytes 344072 | tf_op jit(solution)/shard_map/ppermute | solution.py:586
  10.0 1.2 %prep.1 = (f32[12,3,144,128]{3,2,1,0:T(8,128)S(1)}, f32[12,4,136,128]{3,2,1,0:T(8,128)S(1)}, f32[12,3,144,128]{3,2,1,0:T(8,128)S(1)}) custom-call(bf16[10,3,128,128]{3,2,1,0:T(8,128)(2,1)S(1)} %get-tuple-element.20.own_ref.refs_0_, bf16[128,128]{1,0:T(8,128)(2,1)S(1)} %get-tuple-element.21.kt_ref.refs_5_), custom_call_target="tpu_custom_call" | custom-call | tf_op jit(solution)/shard_map/prep/pallas_call | solution.py:594
  11.2 0.7 %collective-permute-done.2.refs_8_ = bf16[448,128]{1,0:T(8,128)(2,1)S(1)} collective-permute-done((bf16[448,128]{1,0:T(8,128)(2,1)S(1)}, bf16[448,128]{1,0:T(8,128)(2,1)S(1)}, u32[]{:S(2)}, u32[]{:S(2)}) %collective-permute-start.2) | collective-permute-done | bytes 114720 | tf_op jit(solution)/shard_map/ppermute | solution.py:585
  11.9 0.0 collective-permute-done.3.refs_9_
  11.9 4.6 %fine.1 = (f32[1,40,128]{2,1,0:T(8,128)S(1)}, bf16[10,3,128,128]{3,2,1,0:T(8,128)(2,1)S(1)}, bf16[10,3,128,128]{3,2,1,0:T(8,128)(2,1)S(1)}, f32[12,3,144,128]{3,...) custom-call(s32[1,1]{1,0:T(1,128)S(6)} %copy.13.refs_0_, ...), custom_call_target="tpu_custom_call", output_to_operand_aliasing={{3}: (2, {}), {4}: (3, {}), {5}: (4, {})} | custom-call | tf_op jit(solution)/shard_map/fine/pallas_call | solution.py:595
  16.5 7.0 %collective-permute-start.4 = (f32[1,40,128]{2,1,0:T(8,128)S(1)}, f32[1,40,128]{2,1,0:T(8,128)S(1)}, u32[]{:S(2)}, u32[]{:S(2)}) collective-permute-start(f32[1,40,128]{2,1,0:T(8,128)S(1)} %get-tuple-element.30), channel_id=1, source_target_pairs={{0,16},{4,20},{8,24},{12,28},{16,0},{20,4},{24,8},{28,12},{1,17},{... | collective-permute-start | bytes 61448 | tf_op jit(solution)/shard_map/ppermute | solution.py:623
  23.5 1.8 %collective-permute-done.4 = f32[1,40,128]{2,1,0:T(8,128)S(1)} collective-permute-done((f32[1,40,128]{2,1,0:T(8,128)S(1)}, f32[1,40,128]{2,1,0:T(8,128)S(1)}, u32[]{:S(2)}, u32[]{:S(2)}) %collective-permute-start.4) | collective-permute-done | bytes 20512 | tf_op jit(solution)/shard_map/ppermute | solution.py:623
  25.2 2.1 %collective-permute-start.7 = (f32[2,40,128]{2,1,0:T(8,128)S(1)}, f32[2,40,128]{2,1,0:T(8,128)S(1)}, u32[]{:S(2)}, u32[]{:S(2)}) collective-permute-start(f32[2,40,128]{2,1,0:T(8,128)S(1)} %constant_dynamic-update-slice_fusion.refs_0_), channel_id=1, source_target_pairs={{0,12},{4,8},{8,4},{12,0},{16,28},{20,24},{24,20},{28,16},{1,13},{... | collective-permute-start | bytes 122888 | tf_op jit(solution)/shard_map/ppermute | solution.py:623
  27.3 1.5 %collective-permute-start.6 = (f32[2,40,128]{2,1,0:T(8,128)S(1)}, f32[2,40,128]{2,1,0:T(8,128)S(1)}, u32[]{:S(2)}, u32[]{:S(2)}) collective-permute-start(f32[2,40,128]{2,1,0:T(8,128)S(1)} %constant_dynamic-update-slice_fusion.refs_0_), channel_id=1, source_target_pairs={{0,4},{4,0},{8,12},{12,8},{16,20},{20,16},{24,28},{28,24},{1,5},{5... | collective-permute-start | bytes 122888 | tf_op jit(solution)/shard_map/ppermute | solution.py:623
  28.8 0.0 collective-permute-start.5
  28.8 1.3 %collective-permute-done.7.refs_3_ = f32[2,40,128]{2,1,0:T(8,128)S(1)} collective-permute-done((f32[2,40,128]{2,1,0:T(8,128)S(1)}, f32[2,40,128]{2,1,0:T(8,128)S(1)}, u32[]{:S(2)}, u32[]{:S(2)}) %collective-permute-start.7) | collective-permute-done | bytes 40992 | tf_op jit(solution)/shard_map/ppermute | solution.py:623
  30.1 1.2 %collective-permute-done.6.refs_2_ = f32[2,40,128]{2,1,0:T(8,128)S(1)} collective-permute-done((f32[2,40,128]{2,1,0:T(8,128)S(1)}, f32[2,40,128]{2,1,0:T(8,128)S(1)}, u32[]{:S(2)}, u32[]{:S(2)}) %collective-permute-start.6) | collective-permute-done | bytes 40992 | tf_op jit(solution)/shard_map/ppermute | solution.py:623
  31.3 1.5 %collective-permute-done.5.refs_1_ = f32[2,40,128]{2,1,0:T(8,128)S(1)} collective-permute-done((f32[2,40,128]{2,1,0:T(8,128)S(1)}, f32[2,40,128]{2,1,0:T(8,128)S(1)}, u32[]{:S(2)}, u32[]{:S(2)}) %collective-permute-start.5) | collective-permute-done | bytes 40992 | tf_op jit(solution)/shard_map/ppermute | solution.py:623
  32.8 3.4 %level.1 = f32[16,3,32,128]{3,2,1,0:T(8,128)} custom-call(f32[2,40,128]{2,1,0:T(8,128)S(1)} %constant_dynamic-update-slice_fusion.refs_0_, f32[2,40,128]{2,1,0:T(8,128)S(1)} %collective-permute-done.5.refs_1_, f32[2,40,128]{2,1,0:T(8,128)S(1)} %collective-permute-done.6.refs_2_, f32[2,40,128]{2,1,0:T(8,128)S(1)} %collective-permute-done.7.refs_3_, ...), custom_call_target="tpu_custom_call" | custom-call | tf_op jit(solution)/shard_map/level/pallas_call | solution.py:634
  (2 shorter events, 0.0 us)
Async XLA Ops:
  1.7 2.0 %collective-permute-start = (bf16[128,128]{1,0:T(8,128)(2,1)S(1)}, bf16[128,128]{1,0:T(8,128)(2,1)S(1)}, u32[]{:S(2)}, u32[]{:S(2)}) collective-permute-start(bf16[128,128]{1,0:T(8,128)(2,1)S(1)} %get-tuple-element.25), channel_id=1, source_target_pairs={{0,1},{1,0},{2,3},{3,2},{4,5},{5,4},{6,7},{7,6},{8,9},{9,8},{10,11... | collective-permute-start | bytes 98312 | tf_op jit(solution)/shard_map/ppermute | solution.py:577
  1.8 5.2 %collective-permute-start.1 = (bf16[128,128]{1,0:T(8,128)(2,1)S(1)}, bf16[128,128]{1,0:T(8,128)(2,1)S(1)}, u32[]{:S(2)}, u32[]{:S(2)}) collective-permute-start(bf16[128,128]{1,0:T(8,128)(2,1)S(1)} %get-tuple-element.26), channel_id=1, source_target_pairs={{1,2},{2,1},{5,6},{6,5},{9,10},{10,9},{13,14},{14,13},{17,18},{18,... | collective-permute-start | bytes 98312 | tf_op jit(solution)/shard_map/ppermute | solution.py:578
  7.1 4.8 %collective-permute-start.2 = (bf16[448,128]{1,0:T(8,128)(2,1)S(1)}, bf16[448,128]{1,0:T(8,128)(2,1)S(1)}, u32[]{:S(2)}, u32[]{:S(2)}) collective-permute-start(bf16[448,128]{1,0:T(8,128)(2,1)S(1)} %get-tuple-element.28), channel_id=1, source_target_pairs={{0,4},{4,0},{8,12},{12,8},{16,20},{20,16},{24,28},{28,24},{1,5},{5... | collective-permute-start | bytes 344072 | tf_op jit(solution)/shard_map/ppermute | solution.py:585
  8.7 3.3 %collective-permute-start.3 = (bf16[448,128]{1,0:T(8,128)(2,1)S(1)}, bf16[448,128]{1,0:T(8,128)(2,1)S(1)}, u32[]{:S(2)}, u32[]{:S(2)}) collective-permute-start(bf16[448,128]{1,0:T(8,128)(2,1)S(1)} %get-tuple-element.29), channel_id=1, source_target_pairs={{4,8},{8,4},{12,16},{16,12},{20,24},{24,20},{5,9},{9,5},{13,17},{1... | collective-permute-start | bytes 344072 | tf_op jit(solution)/shard_map/ppermute | solution.py:586
  16.5 8.7 %collective-permute-start.4 = (f32[1,40,128]{2,1,0:T(8,128)S(1)}, f32[1,40,128]{2,1,0:T(8,128)S(1)}, u32[]{:S(2)}, u32[]{:S(2)}) collective-permute-start(f32[1,40,128]{2,1,0:T(8,128)S(1)} %get-tuple-element.30), channel_id=1, source_target_pairs={{0,16},{4,20},{8,24},{12,28},{16,0},{20,4},{24,8},{28,12},{1,17},{... | collective-permute-start | bytes 61448 | tf_op jit(solution)/shard_map/ppermute | solution.py:623
  25.2 4.9 %collective-permute-start.7 = (f32[2,40,128]{2,1,0:T(8,128)S(1)}, f32[2,40,128]{2,1,0:T(8,128)S(1)}, u32[]{:S(2)}, u32[]{:S(2)}) collective-permute-start(f32[2,40,128]{2,1,0:T(8,128)S(1)} %constant_dynamic-update-slice_fusion.refs_0_), channel_id=1, source_target_pairs={{0,12},{4,8},{8,4},{12,0},{16,28},{20,24},{24,20},{28,16},{1,13},{... | collective-permute-start | bytes 122888 | tf_op jit(solution)/shard_map/ppermute | solution.py:623
  27.3 4.0 %collective-permute-start.6 = (f32[2,40,128]{2,1,0:T(8,128)S(1)}, f32[2,40,128]{2,1,0:T(8,128)S(1)}, u32[]{:S(2)}, u32[]{:S(2)}) collective-permute-start(f32[2,40,128]{2,1,0:T(8,128)S(1)} %constant_dynamic-update-slice_fusion.refs_0_), channel_id=1, source_target_pairs={{0,4},{4,0},{8,12},{12,8},{16,20},{20,16},{24,28},{28,24},{1,5},{5... | collective-permute-start | bytes 122888 | tf_op jit(solution)/shard_map/ppermute | solution.py:623
  28.8 4.0 %collective-permute-start.5 = (f32[2,40,128]{2,1,0:T(8,128)S(1)}, f32[2,40,128]{2,1,0:T(8,128)S(1)}, u32[]{:S(2)}, u32[]{:S(2)}) collective-permute-start(f32[2,40,128]{2,1,0:T(8,128)S(1)} %constant_dynamic-update-slice_fusion.refs_0_), channel_id=1, source_target_pairs={{0,8},{4,12},{8,0},{12,4},{16,24},{20,28},{24,16},{28,20},{1,9},{5... | collective-permute-start | bytes 122888 | tf_op jit(solution)/shard_map/ppermute | solution.py:623

commit v7 on v6

--- a/solution.py
+++ b/solution.py
@@ -35,7 +35,7 @@
     return dot(ah, bh, dims) + (dot(ah, bl, dims) + dot(al, bh, dims))
 
 
-def inverse_factor(gram, size, step=16):
+def inverse_factor(gram, size, step):
     row, lane = iota((size, 128), 0), iota((size, 128), 1)
     work = jnp.where(lane < size, gram, jnp.where(lane == row + size, 1.0, 0.0))
     for first in range(0, size, step):
@@ -394,9 +394,9 @@
         return 0.5 * (out + out.T)
 
     gram = gram_m()
+    pad = jnp.zeros((nv, lanes - nv), F32)
+    inverse = inverse_factor(jnp.concatenate([gram, pad], axis=1), nv, 8)[:, :nv]
     apply(twice, range(HEAD), range(HEAD), image_rows, keep_margin)
-    pad = jnp.zeros((nv, lanes - nv), F32)
-    inverse = inverse_factor(jnp.concatenate([gram, pad], axis=1), nv)[:, :nv]
     inverse = jnp.where(iota((nv, nv), 0) < rank_ref[0, 0], inverse, 0.0)
     image = gram_n()
 
@@ -450,10 +450,13 @@
     left = jnp.concatenate([high, low, high], axis=1)
     copies = []
     for c in range(comps):
-        for p in range(own):
-            bh, bl = high_ref[p, c], low_ref[p, c]
-            out = dot(left, jnp.concatenate([bh, bh, bl], axis=1), NT).reshape(k2, 8, cy)
-            buf[c, :, pl.ds(p, H, stride=own), :] = out[:, :H]
+        for p in range(0, own, 2):
+            bh = jnp.concatenate([high_ref[p, c], high_ref[p + 1, c]], axis=0)
+            bl = jnp.concatenate([low_ref[p, c], low_ref[p + 1, c]], axis=0)
+            both = dot(left, jnp.concatenate([bh, bh, bl], axis=1), NT)
+            for i in range(2):
+                out = both[:, i * cy : (i + 1) * cy].reshape(k2, 8, cy)
+                buf[c, :, pl.ds(p + i, H, stride=own), :] = out[:, :H]
         copies.append(pltpu.make_async_copy(buf.at[c], out_ref.at[:, c], sems.at[c]))
         copies[-1].start()
     for copy in copies:
@@ -501,7 +504,7 @@
     gram = dot3(w, z, NT)
     gram = jnp.concatenate([gram, jnp.zeros((k2, 128 - k2), F32)], axis=1)
     own = pltpu.roll(w, lax.rem(n - nv * s, n), 1)[:, :nv]
-    coefs = dot3(inverse_factor(gram, k2)[:, :k2], factor * own, NN)
+    coefs = dot3(inverse_factor(gram, k2, k2)[:, :k2], factor * own, NN)
     prolong(coefs, high_ref, low_ref, out_ref, buf, sems)
 
 

time: 36.4 us -> 36 us (0.989)
  Pallas kernels: 11 us -> 10.6 us
where the time goes in v7:
time: 36 us; the launch traced here: 35.9 us
  starting transfers between devices  14.7 us (41%)
  Pallas kernels  10.6 us (29%)
  waiting for transfers between devices  9.79 us (27%)
  between operations  0.72 us (2%)
    ppermute x4, starting transfers between devices, swapped(): return lax.ppermute(block, 'sub', [(i, i ^ bit) for i in range(spans)])  10.5 us
    ppermute x4, waiting for transfers between devices, swapped(): return lax.ppermute(block, 'sub', [(i, i ^ bit) for i in range(spans)])  5.76 us
    pallas_call x1, Pallas kernels, on_device(): call(fine, (shape((1, nv + 8, cy), F32), half, half, rows, weights, rows)...  4.43 us
    ppermute x1, waiting for transfers between devices, on_device(): sec_b = lax.ppermute(sec_b, 'sec', pairs(sects, 1))  3.29 us
    pallas_call x1, Pallas kernels, on_device(): call(level, result, [packs] + tiles, 'level', [vmem] * 6, out_specs=hbm)  3.17 us
    ppermute x1, starting transfers between devices, on_device(): sec_b = lax.ppermute(sec_b, 'sec', pairs(sects, 1))  1.92 us
    pallas_call x1, Pallas kernels, on_device(): call(pack_kernel, (shape((cx // H + 2, comps, cy, H * nv), BF16), shape((...  1.72 us
    ppermute x1, starting transfers between devices, on_device(): sub_a = lax.ppermute(sub_a, 'sub', pairs(spans, 0))  1.53 us
  transfers between devices with their start and end apart: 8, of which 6 were waited for; matrix products, arithmetic and copies ran while one was open for 0% of the time, Pallas kernels for 3%

profile of v7, /device:TPU:2, one launch (start us, length us, event | category | flops | bytes accessed | tf_op | source)
XLA Modules:
  0.0 35.9 jit_solution(10840954950251270490)
XLA Ops:
  0.0 1.7 %pack.1 = (bf16[10,3,128,128]{3,2,1,0:T(8,128)(2,1)S(1)}, bf16[128,128]{1,0:T(8,128)(2,1)S(1)}, bf16[128,128]{1,0:T(8,128)(2,1)S(1)}, bf16[128,128]{1,0:T(8,128)...) custom-call(bf16[32,3,32,128]{3,2,1,0:T(8,128)(2,1)} %v_hbm.1, bf16[3,32,128]{2,1,0:T(8,128)(2,1)} %k_hbm.1, ...), custom_call_target="tpu_custom_call" | custom-call | tf_op jit(solution)/shard_map/pack/pallas_call | solution.py:565
  1.7 0.1 collective-permute-start
  1.8 1.9 %collective-permute-start.1 = (bf16[128,128]{1,0:T(8,128)(2,1)S(1)}, bf16[128,128]{1,0:T(8,128)(2,1)S(1)}, u32[]{:S(2)}, u32[]{:S(2)}) collective-permute-start(bf16[128,128]{1,0:T(8,128)(2,1)S(1)} %get-tuple-element.26), channel_id=1, source_target_pairs={{1,2},{2,1},{5,6},{6,5},{9,10},{10,9},{13,14},{14,13},{17,18},{18,... | collective-permute-start | bytes 98312 | tf_op jit(solution)/shard_map/ppermute | solution.py:581
  3.7 0.0 collective-permute-done.refs_2_.refs_6_
  3.7 3.3 %collective-permute-done.1.refs_3_.refs_7_ = bf16[128,128]{1,0:T(8,128)(2,1)S(1)} collective-permute-done((bf16[128,128]{1,0:T(8,128)(2,1)S(1)}, bf16[128,128]{1,0:T(8,128)(2,1)S(1)}, u32[]{:S(2)}, u32[]{:S(2)}) %collective-permute-start.1) | collective-permute-done | bytes 32800 | tf_op jit(solution)/shard_map/ppermute | solution.py:581
  7.0 0.1 edge.1
  7.1 1.5 %collective-permute-start.2 = (bf16[448,128]{1,0:T(8,128)(2,1)S(1)}, bf16[448,128]{1,0:T(8,128)(2,1)S(1)}, u32[]{:S(2)}, u32[]{:S(2)}) collective-permute-start(bf16[448,128]{1,0:T(8,128)(2,1)S(1)} %get-tuple-element.28), channel_id=1, source_target_pairs={{0,4},{4,0},{8,12},{12,8},{16,20},{20,16},{24,28},{28,24},{1,5},{5... | collective-permute-start | bytes 344072 | tf_op jit(solution)/shard_map/ppermute | solution.py:588
  8.7 0.7 %collective-permute-start.3 = (bf16[448,128]{1,0:T(8,128)(2,1)S(1)}, bf16[448,128]{1,0:T(8,128)(2,1)S(1)}, u32[]{:S(2)}, u32[]{:S(2)}) collective-permute-start(bf16[448,128]{1,0:T(8,128)(2,1)S(1)} %get-tuple-element.29), channel_id=1, source_target_pairs={{4,8},{8,4},{12,16},{16,12},{20,24},{24,20},{5,9},{9,5},{13,17},{1... | collective-permute-start | bytes 344072 | tf_op jit(solution)/shard_map/ppermute | solution.py:589
  10.0 1.2 %prep.1 = (f32[12,3,144,128]{3,2,1,0:T(8,128)S(1)}, f32[12,4,136,128]{3,2,1,0:T(8,128)S(1)}, f32[12,3,144,128]{3,2,1,0:T(8,128)S(1)}) custom-call(bf16[10,3,128,128]{3,2,1,0:T(8,128)(2,1)S(1)} %get-tuple-element.20.own_ref.refs_0_, bf16[128,128]{1,0:T(8,128)(2,1)S(1)} %get-tuple-element.21.kt_ref.refs_5_), custom_call_target="tpu_custom_call" | custom-call | tf_op jit(solution)/shard_map/prep/pallas_call | solution.py:597
  11.2 0.7 %collective-permute-done.2.refs_8_ = bf16[448,128]{1,0:T(8,128)(2,1)S(1)} collective-permute-done((bf16[448,128]{1,0:T(8,128)(2,1)S(1)}, bf16[448,128]{1,0:T(8,128)(2,1)S(1)}, u32[]{:S(2)}, u32[]{:S(2)}) %collective-permute-start.2) | collective-permute-done | bytes 114720 | tf_op jit(solution)/shard_map/ppermute | solution.py:588
  11.9 0.0 collective-permute-done.3.refs_9_
  11.9 4.4 %fine.1 = (f32[1,40,128]{2,1,0:T(8,128)S(1)}, bf16[10,3,128,128]{3,2,1,0:T(8,128)(2,1)S(1)}, bf16[10,3,128,128]{3,2,1,0:T(8,128)(2,1)S(1)}, f32[12,3,144,128]{3,...) custom-call(s32[1,1]{1,0:T(1,128)S(6)} %copy.13.refs_0_, ...), custom_call_target="tpu_custom_call", output_to_operand_aliasing={{3}: (2, {}), {4}: (3, {}), {5}: (4, {})} | custom-call | tf_op jit(solution)/shard_map/fine/pallas_call | solution.py:598
  16.4 7.0 %collective-permute-start.4 = (f32[1,40,128]{2,1,0:T(8,128)S(1)}, f32[1,40,128]{2,1,0:T(8,128)S(1)}, u32[]{:S(2)}, u32[]{:S(2)}) collective-permute-start(f32[1,40,128]{2,1,0:T(8,128)S(1)} %get-tuple-element.30), channel_id=1, source_target_pairs={{0,16},{4,20},{8,24},{12,28},{16,0},{20,4},{24,8},{28,12},{1,17},{... | collective-permute-start | bytes 61448 | tf_op jit(solution)/shard_map/ppermute | solution.py:626
  23.3 1.8 %collective-permute-done.4 = f32[1,40,128]{2,1,0:T(8,128)S(1)} collective-permute-done((f32[1,40,128]{2,1,0:T(8,128)S(1)}, f32[1,40,128]{2,1,0:T(8,128)S(1)}, u32[]{:S(2)}, u32[]{:S(2)}) %collective-permute-start.4) | collective-permute-done | bytes 20512 | tf_op jit(solution)/shard_map/ppermute | solution.py:626
  25.1 2.1 %collective-permute-start.7 = (f32[2,40,128]{2,1,0:T(8,128)S(1)}, f32[2,40,128]{2,1,0:T(8,128)S(1)}, u32[]{:S(2)}, u32[]{:S(2)}) collective-permute-start(f32[2,40,128]{2,1,0:T(8,128)S(1)} %constant_dynamic-update-slice_fusion.refs_0_), channel_id=1, source_target_pairs={{0,12},{4,8},{8,4},{12,0},{16,28},{20,24},{24,20},{28,16},{1,13},{... | collective-permute-start | bytes 122888 | tf_op jit(solution)/shard_map/ppermute | solution.py:626
  27.2 1.5 %collective-permute-start.6 = (f32[2,40,128]{2,1,0:T(8,128)S(1)}, f32[2,40,128]{2,1,0:T(8,128)S(1)}, u32[]{:S(2)}, u32[]{:S(2)}) collective-permute-start(f32[2,40,128]{2,1,0:T(8,128)S(1)} %constant_dynamic-update-slice_fusion.refs_0_), channel_id=1, source_target_pairs={{0,4},{4,0},{8,12},{12,8},{16,20},{20,16},{24,28},{28,24},{1,5},{5... | collective-permute-start | bytes 122888 | tf_op jit(solution)/shard_map/ppermute | solution.py:626
  28.7 0.0 collective-permute-start.5
  28.7 1.3 %collective-permute-done.7.refs_3_ = f32[2,40,128]{2,1,0:T(8,128)S(1)} collective-permute-done((f32[2,40,128]{2,1,0:T(8,128)S(1)}, f32[2,40,128]{2,1,0:T(8,128)S(1)}, u32[]{:S(2)}, u32[]{:S(2)}) %collective-permute-start.7) | collective-permute-done | bytes 40992 | tf_op jit(solution)/shard_map/ppermute | solution.py:626
  30.0 1.2 %collective-permute-done.6.refs_2_ = f32[2,40,128]{2,1,0:T(8,128)S(1)} collective-permute-done((f32[2,40,128]{2,1,0:T(8,128)S(1)}, f32[2,40,128]{2,1,0:T(8,128)S(1)}, u32[]{:S(2)}, u32[]{:S(2)}) %collective-permute-start.6) | collective-permute-done | bytes 40992 | tf_op jit(solution)/shard_map/ppermute | solution.py:626
  31.2 1.5 %collective-permute-done.5.refs_1_ = f32[2,40,128]{2,1,0:T(8,128)S(1)} collective-permute-done((f32[2,40,128]{2,1,0:T(8,128)S(1)}, f32[2,40,128]{2,1,0:T(8,128)S(1)}, u32[]{:S(2)}, u32[]{:S(2)}) %collective-permute-start.5) | collective-permute-done | bytes 40992 | tf_op jit(solution)/shard_map/ppermute | solution.py:626
  32.7 3.2 %level.1 = f32[16,3,32,128]{3,2,1,0:T(8,128)} custom-call(f32[2,40,128]{2,1,0:T(8,128)S(1)} %constant_dynamic-update-slice_fusion.refs_0_, f32[2,40,128]{2,1,0:T(8,128)S(1)} %collective-permute-done.5.refs_1_, f32[2,40,128]{2,1,0:T(8,128)S(1)} %collective-permute-done.6.refs_2_, f32[2,40,128]{2,1,0:T(8,128)S(1)} %collective-permute-done.7.refs_3_, ...), custom_call_target="tpu_custom_call" | custom-call | tf_op jit(solution)/shard_map/level/pallas_call | solution.py:637
  (2 shorter events, 0.0 us)
Async XLA Ops:
  1.7 2.0 %collective-permute-start = (bf16[128,128]{1,0:T(8,128)(2,1)S(1)}, bf16[128,128]{1,0:T(8,128)(2,1)S(1)}, u32[]{:S(2)}, u32[]{:S(2)}) collective-permute-start(bf16[128,128]{1,0:T(8,128)(2,1)S(1)} %get-tuple-element.25), channel_id=1, source_target_pairs={{0,1},{1,0},{2,3},{3,2},{4,5},{5,4},{6,7},{7,6},{8,9},{9,8},{10,11... | collective-permute-start | bytes 98312 | tf_op jit(solution)/shard_map/ppermute | solution.py:580
  1.8 5.2 %collective-permute-start.1 = (bf16[128,128]{1,0:T(8,128)(2,1)S(1)}, bf16[128,128]{1,0:T(8,128)(2,1)S(1)}, u32[]{:S(2)}, u32[]{:S(2)}) collective-permute-start(bf16[128,128]{1,0:T(8,128)(2,1)S(1)} %get-tuple-element.26), channel_id=1, source_target_pairs={{1,2},{2,1},{5,6},{6,5},{9,10},{10,9},{13,14},{14,13},{17,18},{18,... | collective-permute-start | bytes 98312 | tf_op jit(solution)/shard_map/ppermute | solution.py:581
  7.1 4.8 %collective-permute-start.2 = (bf16[448,128]{1,0:T(8,128)(2,1)S(1)}, bf16[448,128]{1,0:T(8,128)(2,1)S(1)}, u32[]{:S(2)}, u32[]{:S(2)}) collective-permute-start(bf16[448,128]{1,0:T(8,128)(2,1)S(1)} %get-tuple-element.28), channel_id=1, source_target_pairs={{0,4},{4,0},{8,12},{12,8},{16,20},{20,16},{24,28},{28,24},{1,5},{5... | collective-permute-start | bytes 344072 | tf_op jit(solution)/shard_map/ppermute | solution.py:588
  8.7 3.3 %collective-permute-start.3 = (bf16[448,128]{1,0:T(8,128)(2,1)S(1)}, bf16[448,128]{1,0:T(8,128)(2,1)S(1)}, u32[]{:S(2)}, u32[]{:S(2)}) collective-permute-start(bf16[448,128]{1,0:T(8,128)(2,1)S(1)} %get-tuple-element.29), channel_id=1, source_target_pairs={{4,8},{8,4},{12,16},{16,12},{20,24},{24,20},{5,9},{9,5},{13,17},{1... | collective-permute-start | bytes 344072 | tf_op jit(solution)/shard_map/ppermute | solution.py:589
  16.4 8.7 %collective-permute-start.4 = (f32[1,40,128]{2,1,0:T(8,128)S(1)}, f32[1,40,128]{2,1,0:T(8,128)S(1)}, u32[]{:S(2)}, u32[]{:S(2)}) collective-permute-start(f32[1,40,128]{2,1,0:T(8,128)S(1)} %get-tuple-element.30), channel_id=1, source_target_pairs={{0,16},{4,20},{8,24},{12,28},{16,0},{20,4},{24,8},{28,12},{1,17},{... | collective-permute-start | bytes 61448 | tf_op jit(solution)/shard_map/ppermute | solution.py:626
  25.1 4.9 %collective-permute-start.7 = (f32[2,40,128]{2,1,0:T(8,128)S(1)}, f32[2,40,128]{2,1,0:T(8,128)S(1)}, u32[]{:S(2)}, u32[]{:S(2)}) collective-permute-start(f32[2,40,128]{2,1,0:T(8,128)S(1)} %constant_dynamic-update-slice_fusion.refs_0_), channel_id=1, source_target_pairs={{0,12},{4,8},{8,4},{12,0},{16,28},{20,24},{24,20},{28,16},{1,13},{... | collective-permute-start | bytes 122888 | tf_op jit(solution)/shard_map/ppermute | solution.py:626
  27.2 4.0 %collective-permute-start.6 = (f32[2,40,128]{2,1,0:T(8,128)S(1)}, f32[2,40,128]{2,1,0:T(8,128)S(1)}, u32[]{:S(2)}, u32[]{:S(2)}) collective-permute-start(f32[2,40,128]{2,1,0:T(8,128)S(1)} %constant_dynamic-update-slice_fusion.refs_0_), channel_id=1, source_target_pairs={{0,4},{4,0},{8,12},{12,8},{16,20},{20,16},{24,28},{28,24},{1,5},{5... | collective-permute-start | bytes 122888 | tf_op jit(solution)/shard_map/ppermute | solution.py:626
  28.7 4.0 %collective-permute-start.5 = (f32[2,40,128]{2,1,0:T(8,128)S(1)}, f32[2,40,128]{2,1,0:T(8,128)S(1)}, u32[]{:S(2)}, u32[]{:S(2)}) collective-permute-start(f32[2,40,128]{2,1,0:T(8,128)S(1)} %constant_dynamic-update-slice_fusion.refs_0_), channel_id=1, source_target_pairs={{0,8},{4,12},{8,0},{12,4},{16,24},{20,28},{24,16},{28,20},{1,9},{5... | collective-permute-start | bytes 122888 | tf_op jit(solution)/shard_map/ppermute | solution.py:626
